TPU v7x, 512 devices: a whole 4x4x16 slice. The times are simulated.
512 devices in a mesh: net: 16 (over z), seg: 8 (over y, core), corner: 4 (over x).
Axes of the slice: x: 4, y: 4, z: 16, core: 2. Of those that a mesh axis runs over, the one named last changes fastest.
Arguments:
- tile_values: bfloat16 [8192, 128, 1024], P(('net', 'seg', 'corner')), may hold values from -48 to 48
- tile_coords: int32 [8192, 3], P(('net', 'seg', 'corner')), may hold values from 0 to 511, as said below
- tile_count: int32 [512], P(('net', 'seg', 'corner')), may hold values from 12 to 16, as said below
- owner_map: int32 [512], P('net'), may hold values from 0 to 511, as said below
- corner_factor: bfloat16 [64, 256], P('corner')
- seg_factor: bfloat16 [65536, 256], P(('seg', 'net'))
Outputs:
- net_factor: float32 [65536, 256], P(('net', 'seg', 'corner'))
Inputs may be any that keep to these rules, and one draw needn't show every extreme that they name: `tile_coords`: row t of device d gives a corner block within the corner range stored by d's corner index, a net block that owner_map assigns to an owner slot of d's net index, and a segment block within the segment range of d's seg index. Among a device's 16 rows at most 2 name segment blocks stored by any one device of the net axis, and on every device two live rows name segment blocks stored by the same device of the net axis. The first tile_count[d] rows of device d are live; the others are ignored. `owner_map`: A permutation of the 512 net blocks.
All inputs are finite; a program needn't handle non-finite values.
Results may differ from a plain program's by a relative error of at most 0.0058.
The roundings to bfloat16 on the way count: a program that leaves them out, or rounds other values in their place, can miss the bound.
Values may be sent and summed in bfloat16 or wider, within the bound.
No kernel may reach another device: no remote copies, remote signals or barrier semaphores. Data moves between devices by JAX's collectives and lax.ppermute only.
A program may use at most 64 MiB of HBM per device.

v0:
```python
import jax
import jax.numpy as jnp
from jax import lax
from jax.sharding import PartitionSpec as P

CBLK = 8
GRP = 4


def solve_rows(gram, mttkrp):
    cholesky_low = jnp.linalg.cholesky(gram)
    forward = lax.linalg.triangular_solve(cholesky_low, mttkrp.T, left_side=True, lower=True)
    backward = lax.linalg.triangular_solve(
        cholesky_low, forward, left_side=True, lower=True, transpose_a=True
    )
    return backward.T


def contract(packed):
    values, corner_rows, seg_rows = packed
    khatri = (
        corner_rows.astype(jnp.float32)[:, :, None, :] * seg_rows.astype(jnp.float32)[:, None, :, :]
    ).astype(jnp.bfloat16)
    khatri = khatri.reshape(values.shape[0], values.shape[2], corner_rows.shape[2])
    return jnp.einsum("tnj,tjr->tnr", values, khatri, preferred_element_type=jnp.float32)


def body(tile_values, tile_coords, tile_count, owner_map, corner_factor, seg_factor):
    slot_total = tile_values.shape[0]
    net_rows = tile_values.shape[1]
    columns = corner_factor.shape[1]
    seg_width = tile_values.shape[2] // CBLK
    held_blocks = seg_factor.shape[0] // seg_width
    net_devices = lax.axis_size("net")
    corner_local = tile_coords[:, 0] - lax.axis_index("corner") * (corner_factor.shape[0] // CBLK)
    seg_local = tile_coords[:, 2] - lax.axis_index("seg") * (held_blocks * net_devices)
    corner_sel = jnp.take(corner_factor.reshape(-1, CBLK, columns), corner_local, axis=0)
    gathered = lax.all_gather(seg_factor, "net", axis=0, tiled=True)
    seg_sel = jnp.take(gathered.reshape(-1, seg_width, columns), seg_local, axis=0)
    groups = slot_total // GRP
    partial_value = lax.map(
        contract,
        (
            tile_values.reshape(groups, GRP, net_rows, -1),
            corner_sel.reshape(groups, GRP, CBLK, columns),
            seg_sel.reshape(groups, GRP, seg_width, columns),
        ),
    )
    partial_value = partial_value.reshape(slot_total, net_rows * columns)
    live_mask = jnp.arange(slot_total, dtype=jnp.int32) < tile_count[0]
    member = ((tile_coords[:, 1][:, None] == owner_map[None, :]) & live_mask[:, None]).astype(
        jnp.float32
    )
    summed = jnp.dot(
        member.T, partial_value, precision=lax.Precision.HIGHEST, preferred_element_type=jnp.float32
    )
    mttkrp = lax.psum_scatter(
        summed.reshape(net_rows * lax.axis_size(("seg", "corner")), columns),
        ("seg", "corner"),
        scatter_dimension=0,
        tiled=True,
    )
    corner_part = jnp.dot(corner_factor.T, corner_factor, preferred_element_type=jnp.float32)
    seg_part = jnp.dot(seg_factor.T, seg_factor, preferred_element_type=jnp.float32)
    seg_gram = lax.psum(seg_part, ("net", "seg"))
    corner_gram = lax.psum(corner_part, "corner")
    return solve_rows(corner_gram * seg_gram, mttkrp)


def solution(mesh):
    return jax.shard_map(
        body,
        mesh=mesh,
        in_specs=(
            P(("net", "seg", "corner"), None, None),
            P(("net", "seg", "corner"), None),
            P(("net", "seg", "corner")),
            P("net"),
            P("corner", None),
            P(("seg", "net"), None),
        ),
        out_specs=P(("net", "seg", "corner"), None),
        check_vma=False,
    )
```

profile of v0, /device:TPU:1, one launch (start us, length us, event | category | flops | bytes accessed | tf_op | source)
XLA Modules:
  0.0 479.9 jit_solution(18225845388589294858)
XLA Ops:
  8.1 2.1 fusion.23
  10.3 1.0 fusion.22
  14.3 71.9 %all-gather.2.cloned.1.call-done = bf16[8192,256]{1,0:T(8,128)(2,1)} async-done(((bf16[512,256]{1,0:T(8,128)(2,1)}), bf16[8192,256]{1,0:T(8,128)(2,1)}) %all-gather.2.cloned.1.call-update) | async-done | bytes 4194320 | tf_op jit(solution)/shard_map/all_gather | solution.py:38
  86.2 2.8 gather_fusion.1
  89.2 12.6 %while.11 = (s32[]{:T(128)}, f32[4,4,128,256]{3,2,1,0:T(8,128)}, bf16[4,4,128,1024]{3,2,1,0:T(8,128)(2,1)}, bf16[4,4,8,256]{3,2,1,0:T(8,128)(2,1)S(1)}, bf16[4,4,128,256]{3,2,1,0:T(8,128)(2,1)S(1)}, /*index=5*/s32[]{:T(128)}) while((s32[]{:T(128)}, f32[4,4,128,256]{3,2,1,0:T(8,128)}, bf16[4,4,128,1024]{3,2,1,0:T(8,128)(2,1)}, ...), condition=%wide.region_7.8_spmd, body=%wide.region_6.7_spmd.sunk | while | flops 270671872 | bytes 7160917 | solution.py:41
  89.9 2.5 fusion.43
  93.0 2.5 fusion.43
  96.2 2.5 fusion.43
  99.3 2.5 fusion.43
  101.8 2.8 copy.13
  104.6 3.5 fusion.15
  108.2 4.9 %reshape.80 = f32[4096,256]{1,0:T(8,128)} reshape(f32[32,32768]{1,0:T(8,128)} %fusion.15) | data formatting | bytes 8388608 | tf_op jit(solution)/shard_map/reshape | solution.py:58
  113.1 239.5 %all-reduce.6.cloned.1.call-done = f32[256,256]{0,1:T(8,128)} async-done(((f32[256,256]{0,1:T(8,128)}), f32[256,256]{0,1:T(8,128)}) %all-reduce.6.cloned.1.call-update) | async-done | bytes 262160 | tf_op jit(solution)/shard_map/psum | solution.py:65
  352.6 54.9 %all-reduce.4.cloned.1.call-done = f32[256,256]{0,1:T(8,128)} async-done(((f32[256,256]{0,1:T(8,128)}), f32[256,256]{0,1:T(8,128)}) %all-reduce.4.cloned.1.call-update) | async-done | bytes 262160 | tf_op jit(solution)/shard_map/psum | solution.py:66
  407.5 1.1 mul.24
  408.7 11.7 %cholesky.50 = f32[128,128]{1,0:T(8,128)S(1)} custom-call(f32[128,128]{1,0:T(8,128)S(1)} %cholesky.118), custom_call_target="Cholesky" | custom-call | tf_op jit(solution)/shard_map/jit(cholesky)/cholesky | solution.py:11
  420.5 9.8 %custom-call.16 = f32[1,128,128]{1,2,0:T(8,128)S(1)} custom-call(f32[1,128,128]{2,1,0:T(8,128)S(1)} %get-tuple-element.68), custom_call_target="InvertDiagBlocksLowerTriangular" | custom-call | tf_op jit(solution)/shard_map/jit(cholesky)/cholesky | solution.py:11
  430.8 11.7 %cholesky.105 = f32[128,128]{1,0:T(8,128)S(1)} custom-call(f32[128,128]{1,0:T(8,128)S(1)} %convolution_subtract_fusion.2), custom_call_target="Cholesky" | custom-call | tf_op jit(solution)/shard_map/jit(cholesky)/cholesky | solution.py:11
  444.6 3.9 while.12
  445.2 1.3 bitcast_dynamic-update-slice_fusion.2
  447.2 1.3 bitcast_dynamic-update-slice_fusion.2
  448.5 19.9 %custom-call.17 = f32[2,128,128]{1,2,0:T(8,128)S(1)} custom-call(f32[2,128,128]{2,1,0:T(8,128)S(1)} %get-tuple-element.40), custom_call_target="InvertDiagBlocksLowerTriangular" | custom-call | tf_op jit(solution)/shard_map/triangular_solve | solution.py:13
  468.4 1.1 fusion.5
  469.5 1.1 convolution_subtract_fusion.1
  (59 shorter events, 10.4 us)
Async XLA Ops:
  7.4 2.9 copy-start
  7.4 78.9 %all-gather.2.cloned.1.call-start = ((), (), s32[]{:S(2)}) async-start(), calls=%async_computation.3 | async-start | bytes 4456448 | tf_op jit(solution)/shard_map/all_gather | solution.py:38
  8.1 344.5 %all-reduce.6.cloned.1.call-start = ((), (), s32[]{:S(2)}) async-start(), calls=%async_computation.2 | async-start | bytes 524288 | tf_op jit(solution)/shard_map/psum | solution.py:65
  10.3 397.2 %all-reduce.4.cloned.1.call-start = ((), (), s32[]{:S(2)}) async-start(), calls=%async_computation.1 | async-start | bytes 524288 | tf_op jit(solution)/shard_map/psum | solution.py:66
  11.3 457.1 %reduce-scatter.2.cloned.1.call-start = ((), (), s32[]{:S(2)}) async-start(), calls=%async_computation.4 | async-start | bytes 4325376 | tf_op jit(solution)/shard_map/reduce_scatter | solution.py:57
  101.8 2.8 copy-start.1
Sparse Core Ops, SparseCore 0:
  10.3 75.9 all-gather.1
  113.2 108.1 reduce-scatter.1
Sparse Core Ops, SparseCore 1:
  12.4 340.2 all-reduce.5
  354.9 52.5 all-reduce.3
where the time goes:
time: 482 us; the launch traced here: 480 us
  waiting for transfers between devices  367 us (76%)
  other arithmetic  58.6 us (12%)
  matrix products  20.2 us (4%)
  between operations  17 us (4%)
  local copies, waits for them, and re-layouts  16.8 us (3%)
    psum x1, waiting for transfers between devices, body(): seg_gram = lax.psum(seg_part, ('net', 'seg'))  240 us
    all_gather x1, waiting for transfers between devices, body(): gathered = lax.all_gather(seg_factor, 'net', axis=0, tiled=True)  71.9 us
    psum x1, waiting for transfers between devices, body(): corner_gram = lax.psum(corner_part, 'corner')  54.9 us
    another operation x6, other arithmetic, solve_rows(): cholesky_low = jnp.linalg.cholesky(gram)  34 us
    another operation x3, other arithmetic, solve_rows(): lax.linalg.triangular_solve(cholesky_low, forward, left_side=True, lower=...  19.9 us
    dot_general x4, matrix products, contract(): jnp.einsum('tnj,tjr->tnr', values, khatri, preferred_element_type=jnp.flo...  9.95 us
  transfers between devices with their start and end apart: 4, of which 3 were waited for; matrix products, arithmetic and copies ran while one was open for 19% of the time, Pallas kernels for 0%

commit v1 on v0

v1 whole, which is shorter than its diff:
```python
import jax
import jax.numpy as jnp
from jax import lax
from jax.experimental import pallas as pl
from jax.experimental.pallas import tpu as pltpu
from jax.sharding import Mesh, PartitionSpec as P

CBLK = 8
ALL = ("net", "y", "core", "corner")
HIGH = lax.Precision.HIGHEST


def mm(a, b):
    return jnp.dot(a, b, precision=HIGH, preferred_element_type=jnp.float32)


def invert_block(a):
    n = a.shape[0]
    lane = lax.broadcasted_iota(jnp.int32, (1, n), 1)
    sub = lax.broadcasted_iota(jnp.int32, (n, 1), 0)
    for k in range(0, n, 2):
        r1 = a[k : k + 1, :]
        r2 = a[k + 1 : k + 2, :]
        c1 = a[:, k : k + 1]
        c2 = a[:, k + 1 : k + 2]
        p11 = r1[:, k : k + 1]
        p12 = r1[:, k + 1 : k + 2]
        p22 = r2[:, k + 1 : k + 2]
        inv = 1.0 / (p11 * p22 - p12 * p12)
        q11 = p22 * inv
        q12 = -p12 * inv
        q22 = p11 * inv
        in1 = lane == k
        in2 = lane == k + 1
        n1 = jnp.where(in1, q11, jnp.where(in2, q12, q11 * r1 + q12 * r2))
        n2 = jnp.where(in1, q12, jnp.where(in2, q22, q12 * r1 + q22 * r2))
        row1 = sub == k
        row2 = sub == k + 1
        m1 = jnp.where(row1, -1.0, jnp.where(row2, 0.0, c1))
        m2 = jnp.where(row2, -1.0, jnp.where(row1, 0.0, c2))
        kept = jnp.where(in1 | in2 | row1 | row2, 0.0, a)
        a = kept - m1 * n1 - m2 * n2
    return a


def inverse_kernel(gram_ref, corner_ref, out_ref):
    corner = corner_ref[...]
    gram = gram_ref[...] * lax.dot_general(
        corner, corner, (((0,), (0,)), ((), ())), preferred_element_type=jnp.float32
    )
    h = gram.shape[0] // 2
    a12 = gram[:h, h:]
    a21 = gram[h:, :h]
    p = invert_block(gram[:h, :h])
    w = mm(p, a12)
    v = mm(a21, p)
    q = invert_block(gram[h:, h:] - mm(a21, w))
    wq = mm(w, q)
    out_ref[:h, :h] = p + mm(wq, v)
    out_ref[:h, h:] = -wq
    out_ref[h:, :h] = -mm(q, v)
    out_ref[h:, h:] = q


def contract_kernel(
    seg_ids, corner_ids, side_ids, slot_ids, live_ids, values_ref, seg_ref, corner_ref, keep_ref, send_ref
):
    step = pl.program_id(0)

    @pl.when(step == 0)
    def _():
        keep_ref[...] = jnp.zeros_like(keep_ref)
        send_ref[...] = jnp.zeros_like(send_ref)

    seg_rows = seg_ref[0].astype(jnp.float32)
    corner_rows = corner_ref[corner_ids[step]].astype(jnp.float32)
    khatri = jnp.concatenate(
        [(corner_rows[a : a + 1, :] * seg_rows).astype(jnp.bfloat16) for a in range(CBLK)], axis=0
    )
    part = jnp.dot(values_ref[0], khatri, preferred_element_type=jnp.float32)
    slot = slot_ids[step]
    live = live_ids[step] == 1
    kept = side_ids[step] == 0

    @pl.when(live & kept)
    def _():
        keep_ref[slot] += part

    @pl.when(live & jnp.logical_not(kept))
    def _():
        send_ref[slot] += part


def whiten_kernel(keep_ref, recv_ref, inv_ref, out_ref):
    rows = keep_ref[0] + recv_ref[0]
    out_ref[0] = mm(rows, inv_ref[...]).astype(jnp.bfloat16)


def body(tile_values, tile_coords, tile_count, owner_map, corner_factor, seg_factor):
    tiles, net_rows, width = tile_values.shape
    cols = corner_factor.shape[1]
    seg_width = width // CBLK
    nz = lax.axis_size("net")
    ny = lax.axis_size("y")
    nx = lax.axis_size("corner")
    core = lax.axis_index("core")
    xi = lax.axis_index("corner")
    seg_i = lax.axis_index("y") * lax.axis_size("core") + core
    per_corner = corner_factor.shape[0] // CBLK
    held = seg_factor.shape[0] // seg_width
    owners = ny * nx

    gathered = lax.all_gather(seg_factor, "net", axis=0, tiled=True)

    seg_part = lax.dot_general(
        seg_factor, seg_factor, (((0,), (0,)), ((), ())), preferred_element_type=jnp.float32
    )
    share = cols // nx
    mine = lax.dynamic_slice_in_dim(seg_part, xi * share, share, 0)
    halves = cols // 128
    chunks = mine.reshape(share // 8, 8, halves, 128).transpose(0, 2, 1, 3).reshape(nz, -1, 128)
    chunk = jnp.sum(lax.all_to_all(chunks, "net", 0, 0), axis=0)
    spread = jnp.broadcast_to(chunk[None], (ny * lax.axis_size("core"),) + chunk.shape)
    chunk = jnp.sum(lax.all_to_all(spread, ("y", "core"), 0, 0), axis=0)
    crows = corner_factor.shape[0] // nz
    zi = lax.axis_index("net")
    own = lax.dynamic_slice_in_dim(corner_factor, zi * crows, crows, 0)
    own = own.astype(jnp.float32).reshape(crows * halves, 128)
    own = jnp.pad(own, ((0, 8 - crows * halves), (0, 0)))
    packet = jnp.concatenate([chunk, own], axis=0)
    packet = jnp.broadcast_to(packet[None], (nz * nx,) + packet.shape)
    packet = lax.all_to_all(packet, ("net", "corner"), 0, 0)
    rows8 = chunk.shape[0]
    seg_gram = packet[:, :rows8].reshape(share // 8, halves, nx, 8, 128)
    seg_gram = seg_gram.transpose(2, 0, 3, 1, 4).reshape(cols, cols)
    corner_all = packet[:, rows8 : rows8 + crows * halves].reshape(-1, cols).astype(jnp.bfloat16)
    inverse = pl.pallas_call(
        inverse_kernel,
        out_shape=jax.ShapeDtypeStruct((cols, cols), jnp.float32),
        compiler_params=pltpu.CompilerParams(vmem_limit_bytes=32 << 20),
        name="gram_inverse",
    )(seg_gram, corner_all)

    corner_ids = jnp.clip(tile_coords[:, 0] - xi * per_corner, 0, per_corner - 1)
    seg_ids = jnp.clip(tile_coords[:, 2] - seg_i * (held * nz), 0, held * nz - 1)
    match = tile_coords[:, 1][:, None] == owner_map[None, :]
    slot = jnp.sum(jnp.where(match, jnp.arange(owner_map.shape[0], dtype=jnp.int32)[None, :], 0), axis=1)
    side_ids = ((slot // nx) % 2 != core).astype(jnp.int32)
    slot_ids = (slot // (2 * nx)) * nx + slot % nx
    live_ids = (jnp.arange(tiles, dtype=jnp.int32) < tile_count[0]).astype(jnp.int32)

    keep, send = pl.pallas_call(
        contract_kernel,
        grid_spec=pltpu.PrefetchScalarGridSpec(
            num_scalar_prefetch=5,
            grid=(tiles,),
            in_specs=[
                pl.BlockSpec((1, net_rows, width), lambda t, *_: (t, 0, 0)),
                pl.BlockSpec((1, seg_width, cols), lambda t, seg_ids, *_: (seg_ids[t], 0, 0)),
                pl.BlockSpec((per_corner, CBLK, cols), lambda t, *_: (0, 0, 0)),
            ],
            out_specs=[
                pl.BlockSpec((owners, net_rows, cols), lambda t, *_: (0, 0, 0)),
                pl.BlockSpec((owners, net_rows, cols), lambda t, *_: (0, 0, 0)),
            ],
        ),
        out_shape=[jax.ShapeDtypeStruct((owners, net_rows, cols), jnp.float32)] * 2,
        compiler_params=pltpu.CompilerParams(vmem_limit_bytes=48 << 20),
        name="contract",
    )(
        seg_ids,
        corner_ids,
        side_ids,
        slot_ids,
        live_ids,
        tile_values,
        gathered.reshape(-1, seg_width, cols),
        corner_factor.reshape(per_corner, CBLK, cols),
    )
    received = lax.ppermute(send, "core", [(0, 1), (1, 0)])
    block = pl.BlockSpec((1, net_rows, cols), lambda t: (t, 0, 0))
    solved = pl.pallas_call(
        whiten_kernel,
        grid=(owners,),
        in_specs=[block, block, pl.BlockSpec((cols, cols), lambda t: (0, 0))],
        out_specs=block,
        out_shape=jax.ShapeDtypeStruct((owners, net_rows, cols), jnp.bfloat16),
        name="apply_inverse",
    )(keep, received, inverse)
    shares = lax.all_to_all(solved, ("y", "corner"), 0, 0)
    return jnp.sum(shares.astype(jnp.float32), axis=0)


def solution(mesh):
    nz, seg, nx = mesh.devices.shape
    split = Mesh(mesh.devices.reshape(nz, seg // 2, 2, nx), ALL)
    return jax.shard_map(
        body,
        mesh=split,
        in_specs=(
            P(ALL, None, None),
            P(ALL, None),
            P(ALL),
            P("net"),
            P("corner", None),
            P(("y", "core", "net"), None),
        ),
        out_specs=P(ALL, None),
        check_vma=False,
    )
```

time: 482 us -> 230 us (0.48)
  waiting for transfers between devices: 367 us -> 50.2 us
  blocking collectives: 0 us -> 65.1 us
  other arithmetic: 58.6 us -> 2.5 us
  Pallas kernels: 0 us -> 56 us
  starting transfers between devices: 0.13 us -> 33.7 us
  matrix products: 20.2 us -> 1.29 us
  local copies, waits for them, and re-layouts: 16.8 us -> 6.13 us
    psum x2 -> x0, waiting for transfers between devices: 294 us -> none  [the longest x1 240 us: body(): seg_gram = lax.psum(seg_part, ('net', 'seg'))]
    all_to_all x0 -> x2, blocking collectives: none -> 65.1 us  [the longest x1 41.6 us: body(): packet = lax.all_to_all(packet, ('net', 'corner'), 0, 0)]
    pallas_call x0 -> x3, Pallas kernels: none -> 56 us  [the longest x1 33.2 us: body(): pl.pallas_call(inverse_kernel, out_shape=jax.ShapeDtypeStruct((cols, cols...]
    another operation x9 -> x0, other arithmetic: 53.9 us -> none  [the longest x6 34 us: solve_rows(): cholesky_low = jnp.linalg.cholesky(gram)]
    all_gather x1, waiting for transfers between devices: 71.9 us -> 36.1 us  [body(): gathered = lax.all_gather(seg_factor, 'net', axis=0, tiled=True)]
    all_to_all x0 -> x2, starting transfers between devices: none -> 22.3 us  [the longest x1 15.7 us: body(): chunk = jnp.sum(lax.all_to_all(chunks, 'net', 0, 0), axis=0)]
    dot_general x7 -> x1, matrix products: 16.5 us -> 1.29 us  [body(): lax.dot_general(seg_factor, seg_factor, (((0,), (0,)), ((), ())), preferr...]
    all_to_all x0 -> x2, waiting for transfers between devices: none -> 13.4 us  [the longest x1 8.62 us: body(): chunk = jnp.sum(lax.all_to_all(chunks, 'net', 0, 0), axis=0)]
  transfers between devices with their start and end apart: 4 -> 4, of which waited for: 3 -> 3; matrix products, arithmetic and copies ran while one was open for 19% -> 2% of each run, Pallas kernels for 0% -> 14%
where the time goes in v1:
time: 230 us; the launch traced here: 229 us
  blocking collectives  65.1 us (28%)
  Pallas kernels  56 us (24%)
  waiting for transfers between devices  50.2 us (22%)
  starting transfers between devices  33.7 us (15%)
  between operations  14.2 us (6%)
  local copies, waits for them, and re-layouts  6.13 us (3%)
  other arithmetic  2.5 us (1%)
    all_to_all x1, blocking collectives, body(): packet = lax.all_to_all(packet, ('net', 'corner'), 0, 0)  41.6 us
    all_gather x1, waiting for transfers between devices, body(): gathered = lax.all_gather(seg_factor, 'net', axis=0, tiled=True)  36.1 us
    pallas_call x1, Pallas kernels, body(): pl.pallas_call(inverse_kernel, out_shape=jax.ShapeDtypeStruct((cols, cols...  33.2 us
    all_to_all x1, blocking collectives, body(): shares = lax.all_to_all(solved, ('y', 'corner'), 0, 0)  23.5 us
    all_to_all x1, starting transfers between devices, body(): chunk = jnp.sum(lax.all_to_all(chunks, 'net', 0, 0), axis=0)  15.7 us
    pallas_call x1, Pallas kernels, body(): pl.pallas_call(whiten_kernel, grid=(owners,), in_specs=[block, block, pl....  11.8 us
    ppermute x1, starting transfers between devices, body(): received = lax.ppermute(send, 'core', [(0, 1), (1, 0)])  11.4 us
    pallas_call x1, Pallas kernels, body(): pl.pallas_call(contract_kernel, grid_spec=pltpu.PrefetchScalarGridSpec(nu...  11 us
  transfers between devices with their start and end apart: 4, of which 3 were waited for; matrix products, arithmetic and copies ran while one was open for 2% of the time, Pallas kernels for 14%

profile of v1, /device:TPU:1, one launch (start us, length us, event | category | flops | bytes accessed | tf_op | source)
XLA Modules:
  0.0 229.1 jit_solution(15992682678632438161)
XLA Ops:
  6.5 0.7 all-gather.2.cloned.1.call-update
  7.3 1.3 fusion.2
  8.6 0.6 constant_dynamic-slice_fusion
  9.2 15.7 %all-to-all-start = ((f32[16,8,128]{2,1,0:T(8,128)}), f32[16,8,128]{2,1,0:T(8,128)S(1)}, u32[]{:S(2)}, u32[]{:S(2)}) async-start(f32[16,8,128]{2,1,0:T(8,128)} %bitcast.8), calls=%async_computation | async-start | bytes 131072 | tf_op jit(solution)/shard_map/all_to_all | solution.py:122
  25.0 0.8 slice_bitcast_fusion
  25.8 0.8 select_reduce_fusion
  27.3 0.7 dynamic-slice_reduce_fusion
  28.0 8.6 %all-to-all-done = f32[16,8,128]{2,1,0:T(8,128)S(1)} async-done(((f32[16,8,128]{2,1,0:T(8,128)}), f32[16,8,128]{2,1,0:T(8,128)S(1)}, u32[]{:S(2)}, u32[]{:S(2)}) %all-to-all-start) | async-done | bytes 65568 | tf_op jit(solution)/shard_map/all_to_all | solution.py:122
  36.6 0.6 broadcast_in_dim.28
  37.3 6.5 %all-to-all-start.1 = ((f32[8,8,128]{2,1,0:T(8,128)}), f32[8,8,128]{2,1,0:T(8,128)S(1)}, u32[]{:S(2)}, u32[]{:S(2)}) async-start(f32[8,8,128]{2,1,0:T(8,128)} %broadcast_in_dim.28), calls=%async_computation.1 | async-start | bytes 65536 | tf_op jit(solution)/shard_map/all_to_all | solution.py:124
  43.8 4.8 %all-to-all-done.1 = f32[8,8,128]{2,1,0:T(8,128)S(1)} async-done(((f32[8,8,128]{2,1,0:T(8,128)}), f32[8,8,128]{2,1,0:T(8,128)S(1)}, u32[]{:S(2)}, u32[]{:S(2)}) %all-to-all-start.1) | async-done | bytes 32800 | tf_op jit(solution)/shard_map/all_to_all | solution.py:124
  48.6 36.1 %all-gather.2.cloned.1.call-done = bf16[8192,256]{1,0:T(8,128)(2,1)} async-done(((bf16[512,256]{1,0:T(8,128)(2,1)}), bf16[8192,256]{1,0:T(8,128)(2,1)}) %all-gather.2.cloned.1.call-update) | async-done | bytes 4194320 | tf_op jit(solution)/shard_map/all_gather | solution.py:113
  84.7 0.7 copy-done.2
  85.4 11.0 %contract.1 = (f32[16,128,256]{2,1,0:T(8,128)S(1)}, f32[16,128,256]{2,1,0:T(8,128)S(1)}) custom-call(s32[16]{0:T(128)S(1)} %get-tuple-element.10.seg_ids, s32[16]{0:T(128)S(1)} %get-tuple-element.11.corner_ids, s32[16]{0:T(128)S(1)} %get-tuple-element.13.side_ids, s32[16]{0:T(128)S(1)} %fusion.slot_ids, s32[16]{0:T(128)S(1)} %get-tuple-element.12.live_ids, ...), custom_call_target="tpu_custom_call" | custom-call | tf_op jit(solution)/shard_map/contract/pallas_call | solution.py:152
  96.4 1.3 copy-done
  97.8 11.4 %collective-permute-start = (f32[16,128,256]{2,1,0:T(8,128)S(1)}, f32[16,128,256]{2,1,0:T(8,128)S(1)}, u32[]{:S(2)}, u32[]{:S(2)}) collective-permute-start(f32[16,128,256]{2,1,0:T(8,128)S(1)} %get-tuple-element.8), channel_id=1, source_target_pairs={{0,4},{4,0},{1,5},{5,1},{2,6},{6,2},{3,7},{7,3},{8,12},{12,8},{9,1... | collective-permute-start | bytes 6291464 | tf_op jit(solution)/shard_map/ppermute | solution.py:180
  109.3 41.6 %all_to_all.20 = f32[64,16,128]{2,1,0:T(8,128)S(1)} all-to-all(f32[64,16,128]{2,1,0:T(8,128)S(1)} %broadcast_in_dim.29), channel_id=1, replica_groups=mesh['net'=16,'y'=4,'core'=2,'corner'=4] {'net','corner'}, dimensions={0} | all-to-all | bytes 1048576 | tf_op jit(solution)/shard_map/all_to_all | solution.py:132
  151.0 33.2 %gram_inverse.1.inv_ref = f32[256,256]{1,0:T(8,128)S(1)} custom-call(f32[256,256]{1,0:T(8,128)S(1)} %bitcast.26, bf16[64,256]{1,0:T(8,128)(2,1)S(1)} %bitcast.27), custom_call_target="tpu_custom_call" | custom-call | tf_op jit(solution)/shard_map/gram_inverse/pallas_call | solution.py:137
  184.2 0.7 copy-done.1
  184.9 0.0 collective-permute-done.recv_ref
  184.9 1.3 copy-done.3
  186.2 11.8 %apply_inverse.1 = bf16[16,128,256]{2,1,0:T(8,128)(2,1)} custom-call(f32[16,128,256]{2,1,0:T(8,128)} %copy-done, f32[16,128,256]{2,1,0:T(8,128)} %copy-done.3, f32[256,256]{1,0:T(8,128)} %copy-done.1), custom_call_target="tpu_custom_call" | custom-call | tf_op jit(solution)/shard_map/apply_inverse/pallas_call | solution.py:182
  198.0 23.5 %all_to_all.21 = bf16[16,128,256]{2,1,0:T(8,128)(2,1)S(1)} all-to-all(bf16[16,128,256]{2,1,0:T(8,128)(2,1)} %apply_inverse.1), channel_id=1, replica_groups=mesh['net'=16,'y'=4,'core'=2,'corner'=4] {'y','corner'}, dimensions={0} | all-to-all | bytes 2097152 | tf_op jit(solution)/shard_map/all_to_all | solution.py:190
  221.5 0.8 convert_reduce_fusion
  (16 shorter events, 0.2 us)
Async XLA Ops:
  6.5 78.2 %all-gather.2.cloned.1.call-start = ((), (), s32[]{:S(2)}) async-start(), calls=%async_computation.4 | async-start | bytes 4456448 | tf_op jit(solution)/shard_map/all_gather | solution.py:113
  9.2 27.4 %all-to-all-start = ((f32[16,8,128]{2,1,0:T(8,128)}), f32[16,8,128]{2,1,0:T(8,128)S(1)}, u32[]{:S(2)}, u32[]{:S(2)}) async-start(f32[16,8,128]{2,1,0:T(8,128)} %bitcast.8), calls=%async_computation | async-start | bytes 131072 | tf_op jit(solution)/shard_map/all_to_all | solution.py:122
  37.3 11.3 %all-to-all-start.1 = ((f32[8,8,128]{2,1,0:T(8,128)}), f32[8,8,128]{2,1,0:T(8,128)S(1)}, u32[]{:S(2)}, u32[]{:S(2)}) async-start(f32[8,8,128]{2,1,0:T(8,128)} %broadcast_in_dim.28), calls=%async_computation.1 | async-start | bytes 65536 | tf_op jit(solution)/shard_map/all_to_all | solution.py:124
  84.7 0.7 copy-start.2
  96.4 1.3 copy-start
  97.8 87.1 %collective-permute-start = (f32[16,128,256]{2,1,0:T(8,128)S(1)}, f32[16,128,256]{2,1,0:T(8,128)S(1)}, u32[]{:S(2)}, u32[]{:S(2)}) collective-permute-start(f32[16,128,256]{2,1,0:T(8,128)S(1)} %get-tuple-element.8), channel_id=1, source_target_pairs={{0,4},{4,0},{1,5},{5,1},{2,6},{6,2},{3,7},{7,3},{8,12},{12,8},{9,1... | collective-permute-start | bytes 6291464 | tf_op jit(solution)/shard_map/ppermute | solution.py:180
  184.2 0.7 copy-start.1
  184.9 1.3 copy-start.3
Sparse Core Ops, SparseCore 0:
  9.4 75.2 all-gather.1

commit v2 on v1

v2 whole, which is shorter than its diff:
```python
import jax
import jax.numpy as jnp
from jax import lax
from jax.experimental import pallas as pl
from jax.experimental.pallas import tpu as pltpu
from jax.sharding import Mesh, PartitionSpec as P

CBLK = 8
GRP = 4
PIVOTS = 4
ALL = ("net", "y", "core", "corner")
HIGH = lax.Precision.HIGHEST


def mm(a, b):
    return jnp.dot(a, b, precision=HIGH, preferred_element_type=jnp.float32)


def invert_pivot(p):
    m = len(p)
    if m == 2:
        inv = 1.0 / (p[0][0] * p[1][1] - p[0][1] * p[0][1])
        off = -p[0][1] * inv
        return [[p[1][1] * inv, off], [off, p[0][0] * inv]]
    h = m // 2
    r = range(h)
    ai = invert_pivot([row[:h] for row in p[:h]])
    b = [row[h:] for row in p[:h]]
    w = [[sum(ai[i][l] * b[l][j] for l in r) for j in r] for i in r]
    s = [[p[h + i][h + j] - sum(b[l][min(i, j)] * w[l][max(i, j)] for l in r) for j in r] for i in r]
    q = invert_pivot(s)
    wq = [[sum(w[i][l] * q[l][j] for l in r) for j in r] for i in r]
    top = [[ai[i][j] + sum(wq[i][l] * w[j][l] for l in r) for j in r] for i in r]
    return [top[i] + [-x for x in wq[i]] for i in r] + [[-wq[j][i] for j in r] + q[i] for i in r]


def invert_block(a):
    n = a.shape[0]
    m = PIVOTS
    lane = lax.broadcasted_iota(jnp.int32, (1, n), 1)
    sub = lax.broadcasted_iota(jnp.int32, (n, 1), 0)
    for k in range(0, n, m):
        rows = [a[k + i : k + i + 1, :] for i in range(m)]
        p = [[None] * m for _ in range(m)]
        for i in range(m):
            for j in range(i, m):
                p[i][j] = p[j][i] = jnp.broadcast_to(rows[i][:, k + j : k + j + 1], (1, n))
        q = invert_pivot(p)
        in_lane = (lane >= k) & (lane < k + m)
        in_sub = (sub >= k) & (sub < k + m)
        new = jnp.where(in_lane | in_sub, 0.0, a)
        for i in range(m):
            row = sum(q[i][j] * rows[j] for j in range(m))
            for j in range(m):
                row = jnp.where(lane == k + j, q[i][j], row)
            col = jnp.where(in_sub, jnp.where(sub == k + i, -1.0, 0.0), a[:, k + i : k + i + 1])
            new = new - col * row
        a = new
    return a


def inverse_kernel(packet_ref, out_ref):
    cols = out_ref.shape[1]
    packet = packet_ref[...]
    corner = packet[:, 8:, :].reshape(-1, cols).astype(jnp.bfloat16)
    gram = packet[:, :8, :].reshape(-1, cols) * lax.dot_general(
        corner, corner, (((0,), (0,)), ((), ())), preferred_element_type=jnp.float32
    )
    h = cols // 2
    a12 = gram[:h, h:]
    a21 = gram[h:, :h]
    p = invert_block(gram[:h, :h])
    w = mm(p, a12)
    v = mm(a21, p)
    q = invert_block(gram[h:, h:] - mm(a21, w))
    wq = mm(w, q)
    out_ref[:h, :h] = p + mm(wq, v)
    out_ref[:h, h:] = -wq
    out_ref[h:, :h] = -mm(q, v)
    out_ref[h:, h:] = q


def contract_kernel(seg_ids, corner_ids, side_ids, slot_ids, live_ids, values_ref, *refs):
    seg_refs, (corner_ref, keep_ref, send_ref) = refs[:GRP], refs[GRP:]
    step = pl.program_id(0)

    @pl.when(step == 0)
    def _():
        keep_ref[...] = jnp.zeros_like(keep_ref)
        send_ref[...] = jnp.zeros_like(send_ref)

    for g in range(GRP):
        t = step * GRP + g
        seg_rows = seg_refs[g][0].astype(jnp.float32)
        corner_rows = corner_ref[corner_ids[t]].astype(jnp.float32)
        khatri = jnp.concatenate(
            [(corner_rows[a : a + 1, :] * seg_rows).astype(jnp.bfloat16) for a in range(CBLK)], axis=0
        )
        part = jnp.dot(values_ref[g], khatri, preferred_element_type=jnp.float32)
        slot = slot_ids[t]
        live = live_ids[t] == 1
        kept = side_ids[t] == 0

        @pl.when(live & kept)
        def _(part=part, slot=slot):
            keep_ref[slot] += part

        @pl.when(live & jnp.logical_not(kept))
        def _(part=part, slot=slot):
            send_ref[slot] += part


def split(x):
    high = x.astype(jnp.bfloat16)
    return high, (x - high.astype(jnp.float32)).astype(jnp.bfloat16)


def whiten_kernel(keep_ref, recv_ref, inv_ref, out_ref):
    inv_high, inv_low = split(inv_ref[...])

    def block(i, carry):
        rows_high, rows_low = split(keep_ref[i] + recv_ref[i])
        out = jnp.dot(rows_high, inv_low, preferred_element_type=jnp.float32)
        out += jnp.dot(rows_low, inv_high, preferred_element_type=jnp.float32)
        out += jnp.dot(rows_high, inv_high, preferred_element_type=jnp.float32)
        out_ref[i] = out.astype(jnp.bfloat16)
        return carry

    lax.fori_loop(0, keep_ref.shape[0], block, 0, unroll=4)


def body(tile_values, tile_coords, tile_count, owner_map, corner_factor, seg_factor):
    tiles, net_rows, width = tile_values.shape
    cols = corner_factor.shape[1]
    seg_width = width // CBLK
    nz = lax.axis_size("net")
    ny = lax.axis_size("y")
    nx = lax.axis_size("corner")
    core = lax.axis_index("core")
    xi = lax.axis_index("corner")
    seg_i = lax.axis_index("y") * lax.axis_size("core") + core
    per_corner = corner_factor.shape[0] // CBLK
    held = seg_factor.shape[0] // seg_width
    owners = ny * nx

    gathered = lax.all_gather(seg_factor, "net", axis=0, tiled=True)

    seg_part = lax.dot_general(
        seg_factor, seg_factor, (((0,), (0,)), ((), ())), preferred_element_type=jnp.float32
    )
    nseg = ny * lax.axis_size("core")
    mine = lax.dynamic_index_in_dim(seg_part.reshape(nseg, nx, -1, cols), xi, 1, keepdims=False)
    chunk = jnp.sum(lax.all_to_all(mine, ("y", "core"), 0, 0), axis=0)
    chunk = jnp.sum(lax.all_to_all(jnp.broadcast_to(chunk[None], (nz,) + chunk.shape), "net", 0, 0), axis=0)
    crows = corner_factor.shape[0] // nseg
    own = lax.dynamic_slice_in_dim(corner_factor, seg_i * crows, crows, 0).astype(jnp.float32)
    packet = jnp.concatenate([chunk, jnp.pad(own, ((0, 8 - crows), (0, 0)))], axis=0)
    packet = jnp.broadcast_to(packet[None], (nseg * nx,) + packet.shape)
    packet = lax.all_to_all(packet, ("y", "core", "corner"), 0, 0)
    inverse = pl.pallas_call(
        inverse_kernel,
        out_shape=jax.ShapeDtypeStruct((cols, cols), jnp.float32),
        compiler_params=pltpu.CompilerParams(vmem_limit_bytes=32 << 20),
        name="gram_inverse",
    )(packet)
    gathered, inverse = lax.optimization_barrier((gathered, inverse))

    corner_ids = jnp.clip(tile_coords[:, 0] - xi * per_corner, 0, per_corner - 1)
    seg_ids = jnp.clip(tile_coords[:, 2] - seg_i * (held * nz), 0, held * nz - 1)
    match = tile_coords[:, 1][:, None] == owner_map[None, :]
    slot = jnp.sum(jnp.where(match, jnp.arange(owner_map.shape[0], dtype=jnp.int32)[None, :], 0), axis=1)
    side_ids = ((slot // nx) % 2 != core).astype(jnp.int32)
    slot_ids = (slot // (2 * nx)) * nx + slot % nx
    live_ids = (jnp.arange(tiles, dtype=jnp.int32) < tile_count[0]).astype(jnp.int32)

    blocks = gathered.reshape(-1, seg_width, cols)

    def seg_spec(g):
        return pl.BlockSpec((1, seg_width, cols), lambda t, ids, *_: (ids[t * GRP + g], 0, 0))

    keep, send = pl.pallas_call(
        contract_kernel,
        grid_spec=pltpu.PrefetchScalarGridSpec(
            num_scalar_prefetch=5,
            grid=(tiles // GRP,),
            in_specs=[
                pl.BlockSpec((GRP, net_rows, width), lambda t, *_: (t, 0, 0)),
                *[seg_spec(g) for g in range(GRP)],
                pl.BlockSpec((per_corner, CBLK, cols), lambda t, *_: (0, 0, 0)),
            ],
            out_specs=[
                pl.BlockSpec((owners, net_rows, cols), lambda t, *_: (0, 0, 0)),
                pl.BlockSpec((owners, net_rows, cols), lambda t, *_: (0, 0, 0)),
            ],
        ),
        out_shape=[jax.ShapeDtypeStruct((owners, net_rows, cols), jnp.float32)] * 2,
        compiler_params=pltpu.CompilerParams(vmem_limit_bytes=48 << 20),
        name="contract",
    )(
        seg_ids,
        corner_ids,
        side_ids,
        slot_ids,
        live_ids,
        tile_values,
        *[blocks] * GRP,
        corner_factor.reshape(per_corner, CBLK, cols),
    )
    received = lax.ppermute(send, "core", [(0, 1), (1, 0)])
    solved = pl.pallas_call(
        whiten_kernel,
        out_shape=jax.ShapeDtypeStruct((owners, net_rows, cols), jnp.bfloat16),
        compiler_params=pltpu.CompilerParams(vmem_limit_bytes=32 << 20),
        name="apply_inverse",
    )(keep, received, inverse)
    shares = lax.all_to_all(solved, ("y", "corner"), 0, 0)
    return jnp.sum(shares.astype(jnp.float32), axis=0)


def solution(mesh):
    nz, seg, nx = mesh.devices.shape
    split = Mesh(mesh.devices.reshape(nz, seg // 2, 2, nx), ALL)
    return jax.shard_map(
        body,
        mesh=split,
        in_specs=(
            P(ALL, None, None),
            P(ALL, None),
            P(ALL),
            P("net"),
            P("corner", None),
            P(("y", "core", "net"), None),
        ),
        out_specs=P(ALL, None),
        check_vma=False,
    )
```

time: 230 us -> 145 us (0.63)
  Pallas kernels: 56 us -> 18.8 us
  blocking collectives: 65.1 us -> 37.2 us
  waiting for transfers between devices: 50.2 us -> 36.9 us
  local copies, waits for them, and re-layouts: 6.13 us -> 2.24 us
    all_to_all x1, blocking collectives: 41.6 us -> 14.1 us  [body(): chunk = jnp.sum(lax.all_to_all(mine, ('y', 'core'), 0, 0), axis=0)]
    all_gather x1, waiting for transfers between devices: 36.1 us -> 11.2 us  [body(): gathered = lax.all_gather(seg_factor, 'net', axis=0, tiled=True)]
    pallas_call x1, Pallas kernels: 33.2 us -> 9.94 us  [body(): pl.pallas_call(inverse_kernel, out_shape=jax.ShapeDtypeStruct((cols, cols...]
    pallas_call x1, Pallas kernels: 11.8 us -> 1.61 us  [body(): pl.pallas_call(whiten_kernel, out_shape=jax.ShapeDtypeStruct((owners, net...]
    all_to_all x2, waiting for transfers between devices: 13.4 us -> 21.2 us  [the longest x1 11.2 us: body(): packet = lax.all_to_all(packet, ('y', 'core', 'corner'), 0, 0)]
    unnamed x9 -> x4, local copies, waits for them, and re-layouts: 4.07 us -> 0.01 us
    pallas_call x1, Pallas kernels: 11 us -> 7.22 us  [body(): pl.pallas_call(contract_kernel, grid_spec=pltpu.PrefetchScalarGridSpec(nu...]
    ppermute x1, waiting for transfers between devices: 0.01 us -> 3.76 us  [body(): received = lax.ppermute(send, 'core', [(0, 1), (1, 0)])]
  transfers between devices with their start and end apart: 4 -> 4, of which waited for: 3 -> 4; matrix products, arithmetic and copies ran while one was open for 2% -> 3% of each run, Pallas kernels for 14% -> 7%
where the time goes in v2:
time: 145 us; the launch traced here: 144 us
  blocking collectives  37.2 us (26%)
  waiting for transfers between devices  36.9 us (25%)
  starting transfers between devices  31.8 us (22%)
  Pallas kernels  18.8 us (13%)
  between operations  14.2 us (10%)
  local copies, waits for them, and re-layouts  2.24 us (2%)
  other arithmetic  1.85 us (1%)
    all_to_all x1, blocking collectives, body(): shares = lax.all_to_all(solved, ('y', 'corner'), 0, 0)  23.1 us
    all_to_all x1, blocking collectives, body(): chunk = jnp.sum(lax.all_to_all(mine, ('y', 'core'), 0, 0), axis=0)  14.1 us
    all_to_all x1, starting transfers between devices, body(): lax.all_to_all(jnp.broadcast_to(chunk[None], (nz,) + chunk.shape), 'net',...  11.4 us
    all_gather x1, waiting for transfers between devices, body(): gathered = lax.all_gather(seg_factor, 'net', axis=0, tiled=True)  11.2 us
    all_to_all x1, waiting for transfers between devices, body(): packet = lax.all_to_all(packet, ('y', 'core', 'corner'), 0, 0)  11.2 us
    ppermute x1, starting transfers between devices, body(): received = lax.ppermute(send, 'core', [(0, 1), (1, 0)])  10.6 us
    all_to_all x1, waiting for transfers between devices, body(): lax.all_to_all(jnp.broadcast_to(chunk[None], (nz,) + chunk.shape), 'net',...  10 us
    pallas_call x1, Pallas kernels, body(): pl.pallas_call(inverse_kernel, out_shape=jax.ShapeDtypeStruct((cols, cols...  9.94 us
  transfers between devices with their start and end apart: 4, of which 4 were waited for; matrix products, arithmetic and copies ran while one was open for 3% of the time, Pallas kernels for 7%

profile of v2, /device:TPU:1, one launch (start us, length us, event | category | flops | bytes accessed | tf_op | source)
XLA Modules:
  0.0 144.2 jit_solution(18070660882958102709)
XLA Ops:
  6.5 0.0 all-gather.2.cloned.1.call-start
  6.5 0.7 all-gather.2.cloned.1.call-update
  7.3 0.0 copy-start
  7.3 1.3 fusion.2
  8.6 14.1 %all_to_all.20 = f32[8,8,256]{2,1,0:T(8,128)S(1)} all-to-all(f32[8,8,256]{2,1,0:T(8,128)S(1)} %dynamic-slice_bitcast_fusion), channel_id=1, replica_groups=mesh['net'=16,'y'=4,'core'=2,'corner'=4] {'y','core'}, dimensions={0} | all-to-all | bytes 131072 | tf_op jit(solution)/shard_map/all_to_all | solution.py:153
  22.8 0.7 broadcast_in_dim.28
  23.4 11.4 %all-to-all-start.1 = ((f32[16,8,256]{2,1,0:T(8,128)}), f32[16,8,256]{2,1,0:T(8,128)S(1)}, u32[]{:S(2)}, u32[]{:S(2)}) async-start(f32[16,8,256]{2,1,0:T(8,128)} %broadcast_in_dim.28), calls=%async_computation.1 | async-start | bytes 262144 | tf_op jit(solution)/shard_map/all_to_all | solution.py:154
  35.5 0.7 constant_dynamic-slice_fusion
  36.2 0.8 slice_bitcast_fusion
  37.0 10.0 %all-to-all-done.1 = f32[16,8,256]{2,1,0:T(8,128)S(1)} async-done(((f32[16,8,256]{2,1,0:T(8,128)}), f32[16,8,256]{2,1,0:T(8,128)S(1)}, u32[]{:S(2)}, u32[]{:S(2)}) %all-to-all-start.1) | async-done | bytes 131104 | tf_op jit(solution)/shard_map/all_to_all | solution.py:154
  47.1 0.9 broadcast_in_dim.29
  48.0 9.8 %all-to-all-start.2 = ((f32[32,16,256]{2,1,0:T(8,128)}), f32[32,16,256]{2,1,0:T(8,128)S(1)}, u32[]{:S(2)}, u32[]{:S(2)}) async-start(f32[32,16,256]{2,1,0:T(8,128)} %broadcast_in_dim.29), calls=%async_computation.2 | async-start | bytes 1048576 | tf_op jit(solution)/shard_map/all_to_all | solution.py:159
  57.7 0.0 copy-done.1
  57.7 0.2 select_reduce_fusion
  57.9 11.2 %all-to-all-done.2.packet_ref = f32[32,16,256]{2,1,0:T(8,128)S(1)} async-done(((f32[32,16,256]{2,1,0:T(8,128)}), f32[32,16,256]{2,1,0:T(8,128)S(1)}, u32[]{:S(2)}, u32[]{:S(2)}) %all-to-all-start.2) | async-done | bytes 524320 | tf_op jit(solution)/shard_map/all_to_all | solution.py:159
  69.1 9.9 %gram_inverse.1.inv_ref = f32[256,256]{1,0:T(8,128)S(1)} custom-call(f32[32,16,256]{2,1,0:T(8,128)S(1)} %all-to-all-done.2.packet_ref), custom_call_target="tpu_custom_call" | custom-call | tf_op jit(solution)/shard_map/gram_inverse/pallas_call | solution.py:160
  79.1 11.2 %all-gather.2.cloned.1.call-done = bf16[8192,256]{1,0:T(8,128)(2,1)} async-done(((bf16[512,256]{1,0:T(8,128)(2,1)}), bf16[8192,256]{1,0:T(8,128)(2,1)}) %all-gather.2.cloned.1.call-update) | async-done | bytes 4194320 | tf_op jit(solution)/shard_map/all_gather | solution.py:146
  90.3 0.0 copy-done
  90.3 7.2 %contract.1 = (f32[16,128,256]{2,1,0:T(8,128)S(1)}, f32[16,128,256]{2,1,0:T(8,128)S(1)}) custom-call(s32[16]{0:T(128)S(1)} %get-tuple-element.14.seg_ids, s32[16]{0:T(128)S(1)} %get-tuple-element.15.corner_ids, s32[16]{0:T(128)S(1)} %get-tuple-element.17.side_ids, s32[16]{0:T(128)S(1)} %fusion.slot_ids, s32[16]{0:T(128)S(1)} %get-tuple-element.16.live_ids, ...), custom_call_target="tpu_custom_call" | custom-call | tf_op jit(solution)/shard_map/contract/pallas_call | solution.py:181
  97.5 10.6 %collective-permute-start = (f32[16,128,256]{2,1,0:T(8,128)S(1)}, f32[16,128,256]{2,1,0:T(8,128)S(1)}, u32[]{:S(2)}, u32[]{:S(2)}) collective-permute-start(f32[16,128,256]{2,1,0:T(8,128)S(1)} %get-tuple-element.11), channel_id=1, source_target_pairs={{0,4},{4,0},{1,5},{5,1},{2,6},{6,2},{3,7},{7,3},{8,12},{12,8},{9,1... | collective-permute-start | bytes 6291464 | tf_op jit(solution)/shard_map/ppermute | solution.py:209
  108.1 3.8 %collective-permute-done.recv_ref = f32[16,128,256]{2,1,0:T(8,128)S(1)} collective-permute-done((f32[16,128,256]{2,1,0:T(8,128)S(1)}, f32[16,128,256]{2,1,0:T(8,128)S(1)}, u32[]{:S(2)}, u32[]{:S(2)}) %collective-permute-start) | collective-permute-done | bytes 2097184 | tf_op jit(solution)/shard_map/ppermute | solution.py:209
  111.9 1.6 %apply_inverse.1 = bf16[16,128,256]{2,1,0:T(8,128)(2,1)S(1)} custom-call(f32[16,128,256]{2,1,0:T(8,128)S(1)} %get-tuple-element.10.keep_ref, f32[16,128,256]{2,1,0:T(8,128)S(1)} %collective-permute-done.recv_ref, f32[256,256]{1,0:T(8,128)S(1)} %gram_inverse.1.inv_ref), custom_call_target="tpu_custom_call" | custom-call | tf_op jit(solution)/shard_map/apply_inverse/pallas_call | solution.py:210
  113.5 23.1 %all_to_all.21 = bf16[16,128,256]{2,1,0:T(8,128)(2,1)S(1)} all-to-all(bf16[16,128,256]{2,1,0:T(8,128)(2,1)S(1)} %apply_inverse.1), channel_id=1, replica_groups=mesh['net'=16,'y'=4,'core'=2,'corner'=4] {'y','corner'}, dimensions={0} | all-to-all | bytes 2097152 | tf_op jit(solution)/shard_map/all_to_all | solution.py:216
  136.6 0.8 convert_reduce_fusion
  (8 shorter events, 0.1 us)
Async XLA Ops:
  6.5 51.2 %copy-start.1 = (s32[32]{0:T(128)S(1)}, s32[32]{0:T(128)}, u32[]{:S(2)}) copy-start(s32[32]{0:T(128)} %param.9) | copy-start | bytes 388
  6.5 83.8 %all-gather.2.cloned.1.call-start = ((), (), s32[]{:S(2)}) async-start(), calls=%async_computation.4 | async-start | bytes 4456448 | tf_op jit(solution)/shard_map/all_gather | solution.py:146
  7.3 83.0 %copy-start = (bf16[16,256]{1,0:T(8,128)(2,1)S(1)}, bf16[16,256]{1,0:T(8,128)(2,1)}, u32[]{:S(2)}) copy-start(bf16[16,256]{1,0:T(8,128)(2,1)} %param.10) | copy-start | bytes 24580
  23.4 23.6 %all-to-all-start.1 = ((f32[16,8,256]{2,1,0:T(8,128)}), f32[16,8,256]{2,1,0:T(8,128)S(1)}, u32[]{:S(2)}, u32[]{:S(2)}) async-start(f32[16,8,256]{2,1,0:T(8,128)} %broadcast_in_dim.28), calls=%async_computation.1 | async-start | bytes 262144 | tf_op jit(solution)/shard_map/all_to_all | solution.py:154
  48.0 21.1 %all-to-all-start.2 = ((f32[32,16,256]{2,1,0:T(8,128)}), f32[32,16,256]{2,1,0:T(8,128)S(1)}, u32[]{:S(2)}, u32[]{:S(2)}) async-start(f32[32,16,256]{2,1,0:T(8,128)} %broadcast_in_dim.29), calls=%async_computation.2 | async-start | bytes 1048576 | tf_op jit(solution)/shard_map/all_to_all | solution.py:159
  97.5 14.4 %collective-permute-start = (f32[16,128,256]{2,1,0:T(8,128)S(1)}, f32[16,128,256]{2,1,0:T(8,128)S(1)}, u32[]{:S(2)}, u32[]{:S(2)}) collective-permute-start(f32[16,128,256]{2,1,0:T(8,128)S(1)} %get-tuple-element.11), channel_id=1, source_target_pairs={{0,4},{4,0},{1,5},{5,1},{2,6},{6,2},{3,7},{7,3},{8,12},{12,8},{9,1... | collective-permute-start | bytes 6291464 | tf_op jit(solution)/shard_map/ppermute | solution.py:209
Sparse Core Ops, SparseCore 0:
  9.4 80.8 all-gather.1

commit v3 on v2

--- a/solution.py
+++ b/solution.py
@@ -1,3 +1,5 @@
+import functools
+
 import jax
 import jax.numpy as jnp
 from jax import lax
@@ -7,8 +9,12 @@
 
 CBLK = 8
 GRP = 4
+CAP = 2
 PIVOTS = 4
-ALL = ("net", "y", "core", "corner")
+NET = ("zh", "zl")
+SEG = ("y", "core")
+ALL = NET + SEG + ("corner",)
+FREE = pl.CostEstimate(flops=0, transcendentals=0, bytes_accessed=0)
 HIGH = lax.Precision.HIGHEST
 
 
@@ -81,7 +87,8 @@
 
 
 def contract_kernel(seg_ids, corner_ids, side_ids, slot_ids, live_ids, values_ref, *refs):
-    seg_refs, (corner_ref, keep_ref, send_ref) = refs[:GRP], refs[GRP:]
+    seg_refs, (corner_ref, keep_ref, send_ref) = refs[:-3], refs[-3:]
+    per = seg_refs[0].shape[0]
     step = pl.program_id(0)
 
     @pl.when(step == 0)
@@ -91,7 +98,10 @@
 
     for g in range(GRP):
         t = step * GRP + g
-        seg_rows = seg_refs[g][0].astype(jnp.float32)
+        place = seg_ids[t]
+        seg_rows = lax.switch(
+            place // per, [lambda at, ref=ref: ref[at] for ref in seg_refs], place % per
+        ).astype(jnp.float32)
         corner_rows = corner_ref[corner_ids[t]].astype(jnp.float32)
         khatri = jnp.concatenate(
             [(corner_rows[a : a + 1, :] * seg_rows).astype(jnp.bfloat16) for a in range(CBLK)], axis=0
@@ -110,6 +120,38 @@
             send_ref[slot] += part
 
 
+def request_kernel(coords_ref, slot_ref, request_ref, *, held, holders, near):
+    seg_i = lax.axis_index("y") * lax.axis_size("core") + lax.axis_index("core")
+    request_ref[...] = jnp.zeros_like(request_ref)
+    seen = []
+    for t in range(coords_ref.shape[0]):
+        local = jnp.clip(coords_ref[t, 2] - seg_i * (held * holders), 0, held * holders - 1)
+        holder = local // held
+        rank = jnp.int32(0)
+        for other in seen:
+            rank += (other == holder).astype(jnp.int32)
+        rank = jnp.minimum(rank, CAP - 1)
+        seen.append(holder)
+        shift = lax.rem(lax.axis_index("corner") - holder // near + near, near)
+        slot_ref[t] = shift * (near * CAP) + (holder % near) * CAP + rank
+        row = jnp.full((1, request_ref.shape[2]), local % held, jnp.int32)
+        request_ref[holder // near, pl.ds((holder % near) * CAP + rank, 1), :] = row
+
+
+def select_kernel(req_ref, *refs):
+    hold = len(refs) // 2
+    parts, outs = refs[:hold], refs[hold:]
+    zl = lax.axis_index("zl")
+    xi = lax.axis_index("corner")
+    for offset in range(hold):
+        residue = lax.rem(zl + offset, hold)
+        for shift in range(hold):
+            dest = lax.rem(xi + shift, hold)
+            for rank in range(CAP):
+                slot = residue * CAP + rank
+                outs[shift][slot] = parts[offset][req_ref[dest, slot]]
+
+
 def split(x):
     high = x.astype(jnp.bfloat16)
     return high, (x - high.astype(jnp.float32)).astype(jnp.bfloat16)
@@ -133,7 +175,7 @@
     tiles, net_rows, width = tile_values.shape
     cols = corner_factor.shape[1]
     seg_width = width // CBLK
-    nz = lax.axis_size("net")
+    nz = lax.axis_size(NET)
     ny = lax.axis_size("y")
     nx = lax.axis_size("corner")
     core = lax.axis_index("core")
@@ -143,40 +185,72 @@
     held = seg_factor.shape[0] // seg_width
     owners = ny * nx
 
-    gathered = lax.all_gather(seg_factor, "net", axis=0, tiled=True)
-
+    near = nz // nx
+    far = [
+        (h * nx + x, (h + near * ((x + h) % nx)) % nz * nx + h // near)
+        for h in range(nz)
+        for x in range(nx)
+    ]
+    own_rows = lax.ppermute(seg_factor, NET + ("corner",), far)
+    slot_of, request = pl.pallas_call(
+        functools.partial(request_kernel, held=held, holders=nz, near=near),
+        in_specs=[pl.BlockSpec(memory_space=pltpu.SMEM)],
+        out_specs=[pl.BlockSpec(memory_space=pltpu.SMEM), pl.BlockSpec(memory_space=pltpu.VMEM)],
+        out_shape=[
+            jax.ShapeDtypeStruct((tiles,), jnp.int32),
+            jax.ShapeDtypeStruct((nx, near * CAP, 128), jnp.int32),
+        ],
+        cost_estimate=FREE,
+        name="requests",
+    )(tile_coords)
+    request = lax.all_to_all(request, "corner", 0, 0)[:, :, 0]
+    request = jnp.clip(request, 0, held - 1)
+    own_rows, request = lax.optimization_barrier((own_rows, request))
+    up = lax.ppermute(own_rows, NET, [((z + 1) % nz, z) for z in range(nz)])
+    two = lax.ppermute(own_rows, NET, [((z + (2 if z % 2 else -2)) % nz, z) for z in range(nz)])
+    down = lax.ppermute(own_rows, NET, [((z - 1) % nz, z) for z in range(nz)])
+    nseg = lax.axis_size(SEG)
     seg_part = lax.dot_general(
-        seg_factor, seg_factor, (((0,), (0,)), ((), ())), preferred_element_type=jnp.float32
+        own_rows, own_rows, (((0,), (0,)), ((), ())), preferred_element_type=jnp.float32
     )
-    nseg = ny * lax.axis_size("core")
-    mine = lax.dynamic_index_in_dim(seg_part.reshape(nseg, nx, -1, cols), xi, 1, keepdims=False)
-    chunk = jnp.sum(lax.all_to_all(mine, ("y", "core"), 0, 0), axis=0)
-    chunk = jnp.sum(lax.all_to_all(jnp.broadcast_to(chunk[None], (nz,) + chunk.shape), "net", 0, 0), axis=0)
+    shares = lax.all_to_all(seg_part.reshape(nseg * nx, -1, cols), SEG + ("corner",), 0, 0)
+    chunk = jnp.sum(shares, axis=0)
+    up, two, down, chunk = lax.optimization_barrier((up, two, down, chunk))
+    smem = pl.BlockSpec(memory_space=pltpu.SMEM)
+    vmem = pl.BlockSpec(memory_space=pltpu.VMEM)
+    chosen = pl.pallas_call(
+        select_kernel,
+        in_specs=[smem] + [vmem] * near,
+        out_specs=[vmem] * nx,
+        out_shape=[jax.ShapeDtypeStruct((near * CAP, seg_width, cols), seg_factor.dtype)] * nx,
+        compiler_params=pltpu.CompilerParams(vmem_limit_bytes=32 << 20),
+        cost_estimate=FREE,
+        name="select_blocks",
+    )(request, *(v.reshape(held, seg_width, cols) for v in (own_rows, up, two, down)))
+    chunk = jnp.sum(lax.all_to_all(jnp.broadcast_to(chunk[None], (near,) + chunk.shape), "zl", 0, 0), axis=0)
     crows = corner_factor.shape[0] // nseg
     own = lax.dynamic_slice_in_dim(corner_factor, seg_i * crows, crows, 0).astype(jnp.float32)
     packet = jnp.concatenate([chunk, jnp.pad(own, ((0, 8 - crows), (0, 0)))], axis=0)
     packet = jnp.broadcast_to(packet[None], (nseg * nx,) + packet.shape)
-    packet = lax.all_to_all(packet, ("y", "core", "corner"), 0, 0)
+    packet = lax.all_to_all(packet, SEG + ("corner",), 0, 0)
+    blocks = [chosen[0]] + [
+        lax.ppermute(chosen[k], "corner", [(x, (x + k) % nx) for x in range(nx)]) for k in range(1, nx)
+    ]
     inverse = pl.pallas_call(
         inverse_kernel,
         out_shape=jax.ShapeDtypeStruct((cols, cols), jnp.float32),
         compiler_params=pltpu.CompilerParams(vmem_limit_bytes=32 << 20),
+        cost_estimate=FREE,
         name="gram_inverse",
     )(packet)
-    gathered, inverse = lax.optimization_barrier((gathered, inverse))
-
+
+    blocks, inverse = lax.optimization_barrier((blocks, inverse))
     corner_ids = jnp.clip(tile_coords[:, 0] - xi * per_corner, 0, per_corner - 1)
-    seg_ids = jnp.clip(tile_coords[:, 2] - seg_i * (held * nz), 0, held * nz - 1)
     match = tile_coords[:, 1][:, None] == owner_map[None, :]
     slot = jnp.sum(jnp.where(match, jnp.arange(owner_map.shape[0], dtype=jnp.int32)[None, :], 0), axis=1)
     side_ids = ((slot // nx) % 2 != core).astype(jnp.int32)
     slot_ids = (slot // (2 * nx)) * nx + slot % nx
     live_ids = (jnp.arange(tiles, dtype=jnp.int32) < tile_count[0]).astype(jnp.int32)
-
-    blocks = gathered.reshape(-1, seg_width, cols)
-
-    def seg_spec(g):
-        return pl.BlockSpec((1, seg_width, cols), lambda t, ids, *_: (ids[t * GRP + g], 0, 0))
 
     keep, send = pl.pallas_call(
         contract_kernel,
@@ -185,7 +259,7 @@
             grid=(tiles // GRP,),
             in_specs=[
                 pl.BlockSpec((GRP, net_rows, width), lambda t, *_: (t, 0, 0)),
-                *[seg_spec(g) for g in range(GRP)],
+                *[vmem] * nx,
                 pl.BlockSpec((per_corner, CBLK, cols), lambda t, *_: (0, 0, 0)),
             ],
             out_specs=[
@@ -197,13 +271,13 @@
         compiler_params=pltpu.CompilerParams(vmem_limit_bytes=48 << 20),
         name="contract",
     )(
-        seg_ids,
+        slot_of,
         corner_ids,
         side_ids,
         slot_ids,
         live_ids,
         tile_values,
-        *[blocks] * GRP,
+        *blocks,
         corner_factor.reshape(per_corner, CBLK, cols),
     )
     received = lax.ppermute(send, "core", [(0, 1), (1, 0)])
@@ -219,7 +293,7 @@
 
 def solution(mesh):
     nz, seg, nx = mesh.devices.shape
-    split = Mesh(mesh.devices.reshape(nz, seg // 2, 2, nx), ALL)
+    split = Mesh(mesh.devices.reshape(nz // nx, nx, seg // 2, 2, nx), ALL)
     return jax.shard_map(
         body,
         mesh=split,
@@ -227,9 +301,9 @@
             P(ALL, None, None),
             P(ALL, None),
             P(ALL),
-            P("net"),
+            P(NET),
             P("corner", None),
-            P(("y", "core", "net"), None),
+            P(SEG + NET, None),
         ),
         out_specs=P(ALL, None),
         check_vma=False,

time: 145 us -> 157 us (1.083)
  starting transfers between devices: 31.8 us -> 66.9 us
  blocking collectives: 37.2 us -> 22.1 us
  between operations: 14.2 us -> 0.91 us
  Pallas kernels: 18.8 us -> 23.6 us
    ppermute x0 -> x7, starting transfers between devices: none -> 25.5 us  [the longest x1 9.59 us: body(): up = lax.ppermute(own_rows, NET, [((z + 1) % nz, z) for z in range(nz)])]
    all_to_all x2 -> x4, starting transfers between devices: 21.2 us -> 39.2 us  [the longest x1 18.6 us: body(): request = lax.all_to_all(request, 'corner', 0, 0)[:, :, 0]]
    all_to_all x1 -> x0, blocking collectives: 14.1 us -> none  [body(): chunk = jnp.sum(lax.all_to_all(mine, ('y', 'core'), 0, 0), axis=0)]
    all_gather x1 -> x0, waiting for transfers between devices: 11.2 us -> none  [body(): gathered = lax.all_gather(seg_factor, 'net', axis=0, tiled=True)]
    all_to_all x2 -> x4, waiting for transfers between devices: 21.2 us -> 31.7 us  [the longest x1 20.8 us: body(): packet = lax.all_to_all(packet, SEG + ('corner',), 0, 0)]
    ppermute x1, starting transfers between devices: 10.6 us -> 2.23 us  [body(): received = lax.ppermute(send, 'core', [(0, 1), (1, 0)])]
    pallas_call x0 -> x2, Pallas kernels: none -> 3.48 us  [the longest x1 1.79 us: body(): pl.pallas_call(functools.partial(request_kernel, held=held, holders=nz, n...]
  transfers between devices with their start and end apart: 4 -> 12, of which waited for: 4 -> 4; matrix products, arithmetic and copies ran while one was open for 3% -> 3% of each run, Pallas kernels for 7% -> 9%
where the time goes in v3:
time: 157 us; the launch traced here: 156 us
  starting transfers between devices  66.9 us (43%)
  waiting for transfers between devices  35.7 us (23%)
  Pallas kernels  23.6 us (15%)
  blocking collectives  22.1 us (14%)
  local copies, waits for them, and re-layouts  3.62 us (2%)
  other arithmetic  1.97 us (1%)
    all_to_all x1, blocking collectives, body(): shares = lax.all_to_all(solved, ('y', 'corner'), 0, 0)  22.1 us
    all_to_all x1, waiting for transfers between devices, body(): packet = lax.all_to_all(packet, SEG + ('corner',), 0, 0)  20.8 us
    all_to_all x1, starting transfers between devices, body(): request = lax.all_to_all(request, 'corner', 0, 0)[:, :, 0]  18.6 us
    all_to_all x1, starting transfers between devices, body(): lax.all_to_all(seg_part.reshape(nseg * nx, -1, cols), SEG + ('corner',),...  11.6 us
    pallas_call x1, Pallas kernels, body(): pl.pallas_call(inverse_kernel, out_shape=jax.ShapeDtypeStruct((cols, cols...  9.94 us
    ppermute x1, starting transfers between devices, body(): up = lax.ppermute(own_rows, NET, [((z + 1) % nz, z) for z in range(nz)])  9.59 us
    pallas_call x1, Pallas kernels, body(): pl.pallas_call(contract_kernel, grid_spec=pltpu.PrefetchScalarGridSpec(nu...  8.64 us
    ppermute x3, starting transfers between devices, body(): lax.ppermute(chosen[k], 'corner', [(x, (x + k) % nx) for x in range(nx)])  8.62 us
  transfers between devices with their start and end apart: 12, of which 4 were waited for; matrix products, arithmetic and copies ran while one was open for 3% of the time, Pallas kernels for 9%

profile of v3, /device:TPU:1, one launch (start us, length us, event | category | flops | bytes accessed | tf_op | source)
XLA Modules:
  0.0 155.8 jit_solution(7420991406833854835)
XLA Ops:
  0.0 1.6 %collective-permute-start = (bf16[512,256]{1,0:T(8,128)(2,1)}, bf16[512,256]{1,0:T(8,128)(2,1)S(1)}, u32[]{:S(2)}, u32[]{:S(2)}) collective-permute-start(bf16[512,256]{1,0:T(8,128)(2,1)} %param.11), channel_id=1, source_target_pairs={{0,0},{1,128},{2,256},{3,384},{32,160},{33,288},{34,416},{35,32},{... | collective-permute-start | bytes 786440 | tf_op jit(solution)/shard_map/ppermute | solution.py:194
  1.6 1.4 copy.9.coords_ref
  3.0 1.8 %requests.1 = (s32[16]{0:T(128)}, s32[4,8,128]{2,1,0:T(8,128)}) custom-call(s32[16,3]{1,0:T(8,128)} %copy.9.coords_ref), custom_call_target="tpu_custom_call" | custom-call | tf_op jit(solution)/shard_map/requests/pallas_call | solution.py:195
  4.7 18.6 %all-to-all-start = ((s32[4,8,128]{2,1,0:T(8,128)}), s32[4,8,128]{2,1,0:T(8,128)S(1)}, u32[]{:S(2)}, u32[]{:S(2)}) async-start(s32[4,8,128]{2,1,0:T(8,128)} %get-tuple-element.25), calls=%async_computation | async-start | bytes 32768 | tf_op jit(solution)/shard_map/all_to_all | solution.py:206
  23.4 4.2 %all-to-all-done = s32[4,8,128]{2,1,0:T(8,128)S(1)} async-done(((s32[4,8,128]{2,1,0:T(8,128)}), s32[4,8,128]{2,1,0:T(8,128)S(1)}, u32[]{:S(2)}, u32[]{:S(2)}) %all-to-all-start) | async-done | bytes 16416 | tf_op jit(solution)/shard_map/all_to_all | solution.py:206
  27.8 1.0 convolution_bitcast_fusion
  28.7 1.9 %collective-permute-start.3 = (bf16[512,256]{1,0:T(8,128)(2,1)S(1)}, bf16[512,256]{1,0:T(8,128)(2,1)S(1)}, u32[]{:S(2)}, u32[]{:S(2)}) collective-permute-start(bf16[512,256]{1,0:T(8,128)(2,1)S(1)} %collective-permute-done), channel_id=1, source_target_pairs={{480,0},{0,32},{32,64},{64,96},{96,128},{128,160},{160,192},{192,2... | collective-permute-start | bytes 786440 | tf_op jit(solution)/shard_map/ppermute | solution.py:211
  30.7 3.8 %collective-permute-start.2 = (bf16[512,256]{1,0:T(8,128)(2,1)S(1)}, bf16[512,256]{1,0:T(8,128)(2,1)S(1)}, u32[]{:S(2)}, u32[]{:S(2)}) collective-permute-start(bf16[512,256]{1,0:T(8,128)(2,1)S(1)} %collective-permute-done), channel_id=1, source_target_pairs={{448,0},{96,32},{0,64},{160,96},{64,128},{224,160},{128,192},{288,... | collective-permute-start | bytes 786440 | tf_op jit(solution)/shard_map/ppermute | solution.py:210
  34.4 9.6 %collective-permute-start.1 = (bf16[512,256]{1,0:T(8,128)(2,1)S(1)}, bf16[512,256]{1,0:T(8,128)(2,1)S(1)}, u32[]{:S(2)}, u32[]{:S(2)}) collective-permute-start(bf16[512,256]{1,0:T(8,128)(2,1)S(1)} %collective-permute-done), channel_id=1, source_target_pairs={{32,0},{64,32},{96,64},{128,96},{160,128},{192,160},{224,192},{256... | collective-permute-start | bytes 786440 | tf_op jit(solution)/shard_map/ppermute | solution.py:209
  44.0 11.6 %all-to-all-start.1 = ((f32[32,8,256]{2,1,0:T(8,128)}), f32[32,8,256]{2,1,0:T(8,128)S(1)}, u32[]{:S(2)}, u32[]{:S(2)}) async-start(f32[32,8,256]{2,1,0:T(8,128)} %convolution_bitcast_fusion), calls=%async_computation.1 | async-start | bytes 524288 | tf_op jit(solution)/shard_map/all_to_all | solution.py:216
  57.8 6.7 %all-to-all-done.1 = f32[32,8,256]{2,1,0:T(8,128)S(1)} async-done(((f32[32,8,256]{2,1,0:T(8,128)}), f32[32,8,256]{2,1,0:T(8,128)S(1)}, u32[]{:S(2)}, u32[]{:S(2)}) %all-to-all-start.1) | async-done | bytes 262176 | tf_op jit(solution)/shard_map/all_to_all | solution.py:216
  65.2 3.3 %all-to-all-start.2 = ((f32[4,8,256]{2,1,0:T(8,128)}), f32[4,8,256]{2,1,0:T(8,128)S(1)}, u32[]{:S(2)}, u32[]{:S(2)}) async-start(f32[4,8,256]{2,1,0:T(8,128)} %broadcast_in_dim.28), calls=%async_computation.2 | async-start | bytes 65536 | tf_op jit(solution)/shard_map/all_to_all | solution.py:230
  68.4 1.7 %select_blocks.1 = (bf16[8,128,256]{2,1,0:T(8,128)(2,1)S(1)}, bf16[8,128,256]{2,1,0:T(8,128)(2,1)}, bf16[8,128,256]{2,1,0:T(8,128)(2,1)}, bf16[8,128,256]{2,1,0:T(8,128)(2,1)S(1)}) custom-call(s32[4,8]{1,0:T(4,128)S(1)} %fusion.req_ref, bf16[4,128,256]{2,1,0:T(8,128)(2,1)S(1)} %bitcast.15, bf16[4,128,256]{2,1,0:T(8,128)(2,1)S(1)} %bitcast.18, ...), custom_call_target="tpu_custom_call" | custom-call | tf_op jit(solution)/shard_map/select_blocks/pallas_call | solution.py:221
  70.1 2.2 %collective-permute-start.4 = (bf16[8,128,256]{2,1,0:T(8,128)(2,1)}, bf16[8,128,256]{2,1,0:T(8,128)(2,1)S(1)}, u32[]{:S(2)}, u32[]{:S(2)}) collective-permute-start(bf16[8,128,256]{2,1,0:T(8,128)(2,1)} %get-tuple-element.32), channel_id=1, source_target_pairs={{0,1},{1,2},{2,3},{3,0},{4,5},{5,6},{6,7},{7,4},{8,9},{9,10},{10,1... | collective-permute-start | bytes 1572872 | tf_op jit(solution)/shard_map/ppermute | solution.py:237
  72.3 3.6 %collective-permute-start.5 = (bf16[8,128,256]{2,1,0:T(8,128)(2,1)}, bf16[8,128,256]{2,1,0:T(8,128)(2,1)S(1)}, u32[]{:S(2)}, u32[]{:S(2)}) collective-permute-start(bf16[8,128,256]{2,1,0:T(8,128)(2,1)} %get-tuple-element.33), channel_id=1, source_target_pairs={{0,2},{1,3},{2,0},{3,1},{4,6},{5,7},{6,4},{7,5},{8,10},{9,11},{10,... | collective-permute-start | bytes 1572872 | tf_op jit(solution)/shard_map/ppermute | solution.py:237
  76.0 2.8 %collective-permute-start.6 = (bf16[8,128,256]{2,1,0:T(8,128)(2,1)S(1)}, bf16[8,128,256]{2,1,0:T(8,128)(2,1)S(1)}, u32[]{:S(2)}, u32[]{:S(2)}) collective-permute-start(bf16[8,128,256]{2,1,0:T(8,128)(2,1)S(1)} %get-tuple-element.34), channel_id=1, source_target_pairs={{0,3},{1,0},{2,1},{3,2},{4,7},{5,4},{6,5},{7,6},{8,11},{9,8},{10,9... | collective-permute-start | bytes 1572872 | tf_op jit(solution)/shard_map/ppermute | solution.py:237
  79.7 5.8 %all-to-all-start.3 = ((f32[32,16,256]{2,1,0:T(8,128)}), f32[32,16,256]{2,1,0:T(8,128)S(1)}, u32[]{:S(2)}, u32[]{:S(2)}) async-start(f32[32,16,256]{2,1,0:T(8,128)} %broadcast_in_dim.29), calls=%async_computation.3 | async-start | bytes 1048576 | tf_op jit(solution)/shard_map/all_to_all | solution.py:235
  85.7 20.8 %all-to-all-done.3.packet_ref = f32[32,16,256]{2,1,0:T(8,128)S(1)} async-done(((f32[32,16,256]{2,1,0:T(8,128)}), f32[32,16,256]{2,1,0:T(8,128)S(1)}, u32[]{:S(2)}, u32[]{:S(2)}) %all-to-all-start.3) | async-done | bytes 524320 | tf_op jit(solution)/shard_map/all_to_all | solution.py:235
  106.5 9.9 %gram_inverse.1.inv_ref = f32[256,256]{1,0:T(8,128)S(1)} custom-call(f32[32,16,256]{2,1,0:T(8,128)S(1)} %all-to-all-done.3.packet_ref), custom_call_target="tpu_custom_call" | custom-call | tf_op jit(solution)/shard_map/gram_inverse/pallas_call | solution.py:239
  116.5 8.6 %contract.1 = (f32[16,128,256]{2,1,0:T(8,128)S(1)}, f32[16,128,256]{2,1,0:T(8,128)}) custom-call(s32[16]{0:T(128)S(1)} %copy-done.1, s32[16]{0:T(128)S(1)} %get-tuple-element.44.corner_ids, s32[16]{0:T(128)S(1)} %get-tuple-element.46.side_ids, s32[16]{0:T(128)S(1)} %fusion.1.slot_ids, s32[16]{0:T(128)S(1)} %get-tuple-element.45.live_ids, ...), custom_call_target="tpu_custom_call" | custom-call | tf_op jit(solution)/shard_map/contract/pallas_call | solution.py:255
  125.1 2.2 %collective-permute-start.7 = (f32[16,128,256]{2,1,0:T(8,128)}, f32[16,128,256]{2,1,0:T(8,128)S(1)}, u32[]{:S(2)}, u32[]{:S(2)}) collective-permute-start(f32[16,128,256]{2,1,0:T(8,128)} %get-tuple-element.41), channel_id=1, source_target_pairs={{0,4},{4,0},{1,5},{5,1},{2,6},{6,2},{3,7},{7,3},{8,12},{12,8},{9,1... | collective-permute-start | bytes 6291464 | tf_op jit(solution)/shard_map/ppermute | solution.py:283
  127.4 4.0 %collective-permute-done.7.recv_ref = f32[16,128,256]{2,1,0:T(8,128)S(1)} collective-permute-done((f32[16,128,256]{2,1,0:T(8,128)}, f32[16,128,256]{2,1,0:T(8,128)S(1)}, u32[]{:S(2)}, u32[]{:S(2)}) %collective-permute-start.7) | collective-permute-done | bytes 2097184 | tf_op jit(solution)/shard_map/ppermute | solution.py:283
  131.4 1.6 apply_inverse.1
  132.9 22.1 %all_to_all.25 = bf16[16,128,256]{2,1,0:T(8,128)(2,1)S(1)} all-to-all(bf16[16,128,256]{2,1,0:T(8,128)(2,1)S(1)} %apply_inverse.1), channel_id=1, replica_groups=mesh['zh'=4,'zl'=4,'y'=4,'core'=2,'corner'=4] {'y','corner'}, dimensions={0} | all-to-all | bytes 2097152 | tf_op jit(solution)/shard_map/all_to_all | solution.py:290
  (27 shorter events, 4.3 us)
Async XLA Ops:
  0.0 27.8 %collective-permute-start = (bf16[512,256]{1,0:T(8,128)(2,1)}, bf16[512,256]{1,0:T(8,128)(2,1)S(1)}, u32[]{:S(2)}, u32[]{:S(2)}) collective-permute-start(bf16[512,256]{1,0:T(8,128)(2,1)} %param.11), channel_id=1, source_target_pairs={{0,0},{1,128},{2,256},{3,384},{32,160},{33,288},{34,416},{35,32},{... | collective-permute-start | bytes 786440 | tf_op jit(solution)/shard_map/ppermute | solution.py:194
  4.7 22.9 %all-to-all-start = ((s32[4,8,128]{2,1,0:T(8,128)}), s32[4,8,128]{2,1,0:T(8,128)S(1)}, u32[]{:S(2)}, u32[]{:S(2)}) async-start(s32[4,8,128]{2,1,0:T(8,128)} %get-tuple-element.25), calls=%async_computation | async-start | bytes 32768 | tf_op jit(solution)/shard_map/all_to_all | solution.py:206
  27.7 57.7 %copy-start.2 = (s32[32]{0:T(128)S(1)}, s32[32]{0:T(128)}, u32[]{:S(2)}) copy-start(s32[32]{0:T(128)} %param.9) | copy-start | bytes 388
  28.7 35.8 %collective-permute-start.3 = (bf16[512,256]{1,0:T(8,128)(2,1)S(1)}, bf16[512,256]{1,0:T(8,128)(2,1)S(1)}, u32[]{:S(2)}, u32[]{:S(2)}) collective-permute-start(bf16[512,256]{1,0:T(8,128)(2,1)S(1)} %collective-permute-done), channel_id=1, source_target_pairs={{480,0},{0,32},{32,64},{64,96},{96,128},{128,160},{160,192},{192,2... | collective-permute-start | bytes 786440 | tf_op jit(solution)/shard_map/ppermute | solution.py:211
  30.7 33.9 %collective-permute-start.2 = (bf16[512,256]{1,0:T(8,128)(2,1)S(1)}, bf16[512,256]{1,0:T(8,128)(2,1)S(1)}, u32[]{:S(2)}, u32[]{:S(2)}) collective-permute-start(bf16[512,256]{1,0:T(8,128)(2,1)S(1)} %collective-permute-done), channel_id=1, source_target_pairs={{448,0},{96,32},{0,64},{160,96},{64,128},{224,160},{128,192},{288,... | collective-permute-start | bytes 786440 | tf_op jit(solution)/shard_map/ppermute | solution.py:210
  34.4 30.1 %collective-permute-start.1 = (bf16[512,256]{1,0:T(8,128)(2,1)S(1)}, bf16[512,256]{1,0:T(8,128)(2,1)S(1)}, u32[]{:S(2)}, u32[]{:S(2)}) collective-permute-start(bf16[512,256]{1,0:T(8,128)(2,1)S(1)} %collective-permute-done), channel_id=1, source_target_pairs={{32,0},{64,32},{96,64},{128,96},{160,128},{192,160},{224,192},{256... | collective-permute-start | bytes 786440 | tf_op jit(solution)/shard_map/ppermute | solution.py:209
  44.0 20.5 %all-to-all-start.1 = ((f32[32,8,256]{2,1,0:T(8,128)}), f32[32,8,256]{2,1,0:T(8,128)S(1)}, u32[]{:S(2)}, u32[]{:S(2)}) async-start(f32[32,8,256]{2,1,0:T(8,128)} %convolution_bitcast_fusion), calls=%async_computation.1 | async-start | bytes 524288 | tf_op jit(solution)/shard_map/all_to_all | solution.py:216
  55.6 60.9 %copy-start = (bf16[16,256]{1,0:T(8,128)(2,1)S(1)}, bf16[16,256]{1,0:T(8,128)(2,1)}, u32[]{:S(2)}) copy-start(bf16[16,256]{1,0:T(8,128)(2,1)} %param.10) | copy-start | bytes 24580
  55.6 60.9 %copy-start.1 = (s32[16]{0:T(128)S(1)}, s32[16]{0:T(128)}, u32[]{:S(2)}) copy-start(s32[16]{0:T(128)} %get-tuple-element.24.seg_ids) | copy-start | bytes 196
  65.2 13.6 %all-to-all-start.2 = ((f32[4,8,256]{2,1,0:T(8,128)}), f32[4,8,256]{2,1,0:T(8,128)S(1)}, u32[]{:S(2)}, u32[]{:S(2)}) async-start(f32[4,8,256]{2,1,0:T(8,128)} %broadcast_in_dim.28), calls=%async_computation.2 | async-start | bytes 65536 | tf_op jit(solution)/shard_map/all_to_all | solution.py:230
  70.1 46.3 %collective-permute-start.4 = (bf16[8,128,256]{2,1,0:T(8,128)(2,1)}, bf16[8,128,256]{2,1,0:T(8,128)(2,1)S(1)}, u32[]{:S(2)}, u32[]{:S(2)}) collective-permute-start(bf16[8,128,256]{2,1,0:T(8,128)(2,1)} %get-tuple-element.32), channel_id=1, source_target_pairs={{0,1},{1,2},{2,3},{3,0},{4,5},{5,6},{6,7},{7,4},{8,9},{9,10},{10,1... | collective-permute-start | bytes 1572872 | tf_op jit(solution)/shard_map/ppermute | solution.py:237
  72.3 44.1 %collective-permute-start.5 = (bf16[8,128,256]{2,1,0:T(8,128)(2,1)}, bf16[8,128,256]{2,1,0:T(8,128)(2,1)S(1)}, u32[]{:S(2)}, u32[]{:S(2)}) collective-permute-start(bf16[8,128,256]{2,1,0:T(8,128)(2,1)} %get-tuple-element.33), channel_id=1, source_target_pairs={{0,2},{1,3},{2,0},{3,1},{4,6},{5,7},{6,4},{7,5},{8,10},{9,11},{10,... | collective-permute-start | bytes 1572872 | tf_op jit(solution)/shard_map/ppermute | solution.py:237
  76.0 40.5 %collective-permute-start.6 = (bf16[8,128,256]{2,1,0:T(8,128)(2,1)S(1)}, bf16[8,128,256]{2,1,0:T(8,128)(2,1)S(1)}, u32[]{:S(2)}, u32[]{:S(2)}) collective-permute-start(bf16[8,128,256]{2,1,0:T(8,128)(2,1)S(1)} %get-tuple-element.34), channel_id=1, source_target_pairs={{0,3},{1,0},{2,1},{3,2},{4,7},{5,4},{6,5},{7,6},{8,11},{9,8},{10,9... | collective-permute-start | bytes 1572872 | tf_op jit(solution)/shard_map/ppermute | solution.py:237
  79.7 26.8 %all-to-all-start.3 = ((f32[32,16,256]{2,1,0:T(8,128)}), f32[32,16,256]{2,1,0:T(8,128)S(1)}, u32[]{:S(2)}, u32[]{:S(2)}) async-start(f32[32,16,256]{2,1,0:T(8,128)} %broadcast_in_dim.29), calls=%async_computation.3 | async-start | bytes 1048576 | tf_op jit(solution)/shard_map/all_to_all | solution.py:235
  125.1 6.3 %collective-permute-start.7 = (f32[16,128,256]{2,1,0:T(8,128)}, f32[16,128,256]{2,1,0:T(8,128)S(1)}, u32[]{:S(2)}, u32[]{:S(2)}) collective-permute-start(f32[16,128,256]{2,1,0:T(8,128)} %get-tuple-element.41), channel_id=1, source_target_pairs={{0,4},{4,0},{1,5},{5,1},{2,6},{6,2},{3,7},{7,3},{8,12},{12,8},{9,1... | collective-permute-start | bytes 6291464 | tf_op jit(solution)/shard_map/ppermute | solution.py:283

commit v4 on v2

--- a/solution.py
+++ b/solution.py
@@ -6,9 +6,11 @@
 from jax.sharding import Mesh, PartitionSpec as P
 
 CBLK = 8
-GRP = 4
+GRP = 8
 PIVOTS = 4
-ALL = ("net", "y", "core", "corner")
+NET = ("zh", "zl")
+SEG = ("y", "core")
+ALL = NET + SEG + ("corner",)
 HIGH = lax.Precision.HIGHEST
 
 
@@ -80,7 +82,7 @@
     out_ref[h:, h:] = q
 
 
-def contract_kernel(seg_ids, corner_ids, side_ids, slot_ids, live_ids, values_ref, *refs):
+def contract_kernel(seg_ids, corner_ids, keep_ids, send_ids, values_ref, *refs):
     seg_refs, (corner_ref, keep_ref, send_ref) = refs[:GRP], refs[GRP:]
     step = pl.program_id(0)
 
@@ -97,17 +99,8 @@
             [(corner_rows[a : a + 1, :] * seg_rows).astype(jnp.bfloat16) for a in range(CBLK)], axis=0
         )
         part = jnp.dot(values_ref[g], khatri, preferred_element_type=jnp.float32)
-        slot = slot_ids[t]
-        live = live_ids[t] == 1
-        kept = side_ids[t] == 0
-
-        @pl.when(live & kept)
-        def _(part=part, slot=slot):
-            keep_ref[slot] += part
-
-        @pl.when(live & jnp.logical_not(kept))
-        def _(part=part, slot=slot):
-            send_ref[slot] += part
+        keep_ref[keep_ids[t]] += part
+        send_ref[send_ids[t]] += part
 
 
 def split(x):
@@ -126,14 +119,14 @@
         out_ref[i] = out.astype(jnp.bfloat16)
         return carry
 
-    lax.fori_loop(0, keep_ref.shape[0], block, 0, unroll=4)
+    lax.fori_loop(0, out_ref.shape[0], block, 0, unroll=4)
 
 
 def body(tile_values, tile_coords, tile_count, owner_map, corner_factor, seg_factor):
     tiles, net_rows, width = tile_values.shape
     cols = corner_factor.shape[1]
     seg_width = width // CBLK
-    nz = lax.axis_size("net")
+    nz = lax.axis_size(NET)
     ny = lax.axis_size("y")
     nx = lax.axis_size("corner")
     core = lax.axis_index("core")
@@ -143,20 +136,22 @@
     held = seg_factor.shape[0] // seg_width
     owners = ny * nx
 
-    gathered = lax.all_gather(seg_factor, "net", axis=0, tiled=True)
+    gathered = lax.all_gather(seg_factor, NET, axis=0, tiled=True)
 
     seg_part = lax.dot_general(
         seg_factor, seg_factor, (((0,), (0,)), ((), ())), preferred_element_type=jnp.float32
     )
     nseg = ny * lax.axis_size("core")
     mine = lax.dynamic_index_in_dim(seg_part.reshape(nseg, nx, -1, cols), xi, 1, keepdims=False)
-    chunk = jnp.sum(lax.all_to_all(mine, ("y", "core"), 0, 0), axis=0)
-    chunk = jnp.sum(lax.all_to_all(jnp.broadcast_to(chunk[None], (nz,) + chunk.shape), "net", 0, 0), axis=0)
+    chunk = jnp.sum(lax.all_to_all(mine, SEG, 0, 0), axis=0)
+    for axis in NET:
+        spread = jnp.broadcast_to(chunk[None], (lax.axis_size(axis),) + chunk.shape)
+        chunk = jnp.sum(lax.all_to_all(spread, axis, 0, 0), axis=0)
     crows = corner_factor.shape[0] // nseg
     own = lax.dynamic_slice_in_dim(corner_factor, seg_i * crows, crows, 0).astype(jnp.float32)
     packet = jnp.concatenate([chunk, jnp.pad(own, ((0, 8 - crows), (0, 0)))], axis=0)
     packet = jnp.broadcast_to(packet[None], (nseg * nx,) + packet.shape)
-    packet = lax.all_to_all(packet, ("y", "core", "corner"), 0, 0)
+    packet = lax.all_to_all(packet, SEG + ("corner",), 0, 0)
     inverse = pl.pallas_call(
         inverse_kernel,
         out_shape=jax.ShapeDtypeStruct((cols, cols), jnp.float32),
@@ -169,9 +164,11 @@
     seg_ids = jnp.clip(tile_coords[:, 2] - seg_i * (held * nz), 0, held * nz - 1)
     match = tile_coords[:, 1][:, None] == owner_map[None, :]
     slot = jnp.sum(jnp.where(match, jnp.arange(owner_map.shape[0], dtype=jnp.int32)[None, :], 0), axis=1)
-    side_ids = ((slot // nx) % 2 != core).astype(jnp.int32)
-    slot_ids = (slot // (2 * nx)) * nx + slot % nx
-    live_ids = (jnp.arange(tiles, dtype=jnp.int32) < tile_count[0]).astype(jnp.int32)
+    place = (slot // (2 * nx)) * nx + slot % nx
+    live = jnp.arange(tiles, dtype=jnp.int32) < tile_count[0]
+    here = (slot // nx) % 2 == core
+    keep_ids = jnp.where(live & here, place, owners)
+    send_ids = jnp.where(live & jnp.logical_not(here), place, owners)
 
     blocks = gathered.reshape(-1, seg_width, cols)
 
@@ -181,7 +178,7 @@
     keep, send = pl.pallas_call(
         contract_kernel,
         grid_spec=pltpu.PrefetchScalarGridSpec(
-            num_scalar_prefetch=5,
+            num_scalar_prefetch=4,
             grid=(tiles // GRP,),
             in_specs=[
                 pl.BlockSpec((GRP, net_rows, width), lambda t, *_: (t, 0, 0)),
@@ -189,19 +186,18 @@
                 pl.BlockSpec((per_corner, CBLK, cols), lambda t, *_: (0, 0, 0)),
             ],
             out_specs=[
-                pl.BlockSpec((owners, net_rows, cols), lambda t, *_: (0, 0, 0)),
-                pl.BlockSpec((owners, net_rows, cols), lambda t, *_: (0, 0, 0)),
+                pl.BlockSpec((owners + 1, net_rows, cols), lambda t, *_: (0, 0, 0)),
+                pl.BlockSpec((owners + 1, net_rows, cols), lambda t, *_: (0, 0, 0)),
             ],
         ),
-        out_shape=[jax.ShapeDtypeStruct((owners, net_rows, cols), jnp.float32)] * 2,
+        out_shape=[jax.ShapeDtypeStruct((owners + 1, net_rows, cols), jnp.float32)] * 2,
         compiler_params=pltpu.CompilerParams(vmem_limit_bytes=48 << 20),
         name="contract",
     )(
         seg_ids,
         corner_ids,
-        side_ids,
-        slot_ids,
-        live_ids,
+        keep_ids,
+        send_ids,
         tile_values,
         *[blocks] * GRP,
         corner_factor.reshape(per_corner, CBLK, cols),
@@ -219,7 +215,7 @@
 
 def solution(mesh):
     nz, seg, nx = mesh.devices.shape
-    split = Mesh(mesh.devices.reshape(nz, seg // 2, 2, nx), ALL)
+    split = Mesh(mesh.devices.reshape(4, nz // 4, seg // 2, 2, nx), ALL)
     return jax.shard_map(
         body,
         mesh=split,
@@ -227,9 +223,9 @@
             P(ALL, None, None),
             P(ALL, None),
             P(ALL),
-            P("net"),
+            P(NET),
             P("corner", None),
-            P(("y", "core", "net"), None),
+            P(SEG + NET, None),
         ),
         out_specs=P(ALL, None),
         check_vma=False,

time: 145 us -> 139 us (0.959)
  blocking collectives: 37.2 us -> 22.3 us
  starting transfers between devices: 31.8 us -> 43 us
  Pallas kernels: 18.8 us -> 16.6 us
  waiting for transfers between devices: 36.9 us -> 35.3 us
    all_to_all x1 -> x0, blocking collectives: 14.1 us -> none  [body(): chunk = jnp.sum(lax.all_to_all(mine, ('y', 'core'), 0, 0), axis=0)]
    all_gather x1, waiting for transfers between devices: 11.2 us -> 0.02 us  [body(): gathered = lax.all_gather(seg_factor, NET, axis=0, tiled=True)]
    all_to_all x2 -> x4, starting transfers between devices: 21.2 us -> 32.2 us  [the longest x2 13.9 us: body(): chunk = jnp.sum(lax.all_to_all(spread, axis, 0, 0), axis=0)]
    all_to_all x2 -> x4, waiting for transfers between devices: 21.2 us -> 30.6 us  [the longest x2 16.1 us: body(): chunk = jnp.sum(lax.all_to_all(spread, axis, 0, 0), axis=0)]
    pallas_call x1, Pallas kernels: 7.22 us -> 5.06 us  [body(): pl.pallas_call(contract_kernel, grid_spec=pltpu.PrefetchScalarGridSpec(nu...]
  transfers between devices with their start and end apart: 4 -> 6, of which waited for: 4 -> 5; matrix products, arithmetic and copies ran while one was open for 3% -> 4% of each run, Pallas kernels for 7% -> 7%
where the time goes in v4:
time: 139 us; the launch traced here: 138 us
  starting transfers between devices  43 us (31%)
  waiting for transfers between devices  35.3 us (25%)
  blocking collectives  22.3 us (16%)
  Pallas kernels  16.6 us (12%)
  between operations  14.2 us (10%)
  local copies, waits for them, and re-layouts  3.43 us (2%)
  other arithmetic  1.84 us (1%)
    all_to_all x1, blocking collectives, body(): shares = lax.all_to_all(solved, ('y', 'corner'), 0, 0)  22.3 us
    all_to_all x2, waiting for transfers between devices, body(): chunk = jnp.sum(lax.all_to_all(spread, axis, 0, 0), axis=0)  16.1 us
    all_to_all x2, starting transfers between devices, body(): chunk = jnp.sum(lax.all_to_all(spread, axis, 0, 0), axis=0)  13.9 us
    all_to_all x1, waiting for transfers between devices, body(): packet = lax.all_to_all(packet, SEG + ('corner',), 0, 0)  11.2 us
    ppermute x1, starting transfers between devices, body(): received = lax.ppermute(send, 'core', [(0, 1), (1, 0)])  10.9 us
    all_to_all x1, starting transfers between devices, body(): chunk = jnp.sum(lax.all_to_all(mine, SEG, 0, 0), axis=0)  10.1 us
    pallas_call x1, Pallas kernels, body(): pl.pallas_call(inverse_kernel, out_shape=jax.ShapeDtypeStruct((cols, cols...  9.94 us
    all_to_all x1, starting transfers between devices, body(): packet = lax.all_to_all(packet, SEG + ('corner',), 0, 0)  8.16 us
  transfers between devices with their start and end apart: 6, of which 5 were waited for; matrix products, arithmetic and copies ran while one was open for 4% of the time, Pallas kernels for 7%

profile of v4, /device:TPU:1, one launch (start us, length us, event | category | flops | bytes accessed | tf_op | source)
XLA Modules:
  0.0 138.1 jit_solution(1940553817217384789)
XLA Ops:
  6.5 0.7 all-gather.2.cloned.1.call-update
  7.3 1.3 fusion.3
  8.6 0.6 dynamic-slice_bitcast_fusion
  9.2 10.1 %all-to-all-start = ((f32[8,8,256]{2,1,0:T(8,128)}), f32[8,8,256]{2,1,0:T(8,128)S(1)}, u32[]{:S(2)}, u32[]{:S(2)}) async-start(f32[8,8,256]{2,1,0:T(8,128)} %dynamic-slice_bitcast_fusion), calls=%async_computation | async-start | bytes 131072 | tf_op jit(solution)/shard_map/all_to_all | solution.py:146
  19.4 0.8 slice_bitcast_fusion
  20.8 3.4 %all-to-all-done = f32[8,8,256]{2,1,0:T(8,128)S(1)} async-done(((f32[8,8,256]{2,1,0:T(8,128)}), f32[8,8,256]{2,1,0:T(8,128)S(1)}, u32[]{:S(2)}, u32[]{:S(2)}) %all-to-all-start) | async-done | bytes 65568 | tf_op jit(solution)/shard_map/all_to_all | solution.py:146
  24.3 0.6 broadcast_in_dim.40
  24.9 10.6 %all-to-all-start.1 = ((f32[4,8,256]{2,1,0:T(8,128)}), f32[4,8,256]{2,1,0:T(8,128)S(1)}, u32[]{:S(2)}, u32[]{:S(2)}) async-start(f32[4,8,256]{2,1,0:T(8,128)} %broadcast_in_dim.40), calls=%async_computation.1 | async-start | bytes 65536 | tf_op jit(solution)/shard_map/all_to_all | solution.py:149
  35.5 0.7 constant_dynamic-slice_fusion
  36.2 11.5 %all-to-all-done.1 = f32[4,8,256]{2,1,0:T(8,128)S(1)} async-done(((f32[4,8,256]{2,1,0:T(8,128)}), f32[4,8,256]{2,1,0:T(8,128)S(1)}, u32[]{:S(2)}, u32[]{:S(2)}) %all-to-all-start.1) | async-done | bytes 32800 | tf_op jit(solution)/shard_map/all_to_all | solution.py:149
  47.7 0.6 broadcast_in_dim.41
  48.3 3.3 %all-to-all-start.2 = ((f32[4,8,256]{2,1,0:T(8,128)}), f32[4,8,256]{2,1,0:T(8,128)S(1)}, u32[]{:S(2)}, u32[]{:S(2)}) async-start(f32[4,8,256]{2,1,0:T(8,128)} %broadcast_in_dim.41), calls=%async_computation.2 | async-start | bytes 65536 | tf_op jit(solution)/shard_map/all_to_all | solution.py:149
  51.6 4.6 %all-to-all-done.2 = f32[4,8,256]{2,1,0:T(8,128)S(1)} async-done(((f32[4,8,256]{2,1,0:T(8,128)}), f32[4,8,256]{2,1,0:T(8,128)S(1)}, u32[]{:S(2)}, u32[]{:S(2)}) %all-to-all-start.2) | async-done | bytes 32800 | tf_op jit(solution)/shard_map/all_to_all | solution.py:149
  56.2 0.9 broadcast_in_dim.42
  57.1 8.2 %all-to-all-start.3 = ((f32[32,16,256]{2,1,0:T(8,128)}), f32[32,16,256]{2,1,0:T(8,128)S(1)}, u32[]{:S(2)}, u32[]{:S(2)}) async-start(f32[32,16,256]{2,1,0:T(8,128)} %broadcast_in_dim.42), calls=%async_computation.3 | async-start | bytes 1048576 | tf_op jit(solution)/shard_map/all_to_all | solution.py:154
  65.2 0.2 select_reduce_fusion
  65.4 11.2 %all-to-all-done.3.packet_ref = f32[32,16,256]{2,1,0:T(8,128)S(1)} async-done(((f32[32,16,256]{2,1,0:T(8,128)}), f32[32,16,256]{2,1,0:T(8,128)S(1)}, u32[]{:S(2)}, u32[]{:S(2)}) %all-to-all-start.3) | async-done | bytes 524320 | tf_op jit(solution)/shard_map/all_to_all | solution.py:154
  76.6 9.9 %gram_inverse.1.inv_ref = f32[256,256]{1,0:T(8,128)S(1)} custom-call(f32[32,16,256]{2,1,0:T(8,128)S(1)} %all-to-all-done.3.packet_ref), custom_call_target="tpu_custom_call" | custom-call | tf_op jit(solution)/shard_map/gram_inverse/pallas_call | solution.py:155
  86.6 5.1 %contract.1 = (f32[17,128,256]{2,1,0:T(8,128)S(1)}, f32[17,128,256]{2,1,0:T(8,128)S(1)}) custom-call(s32[16]{0:T(128)S(1)} %get-tuple-element.17.seg_ids, s32[16]{0:T(128)S(1)} %get-tuple-element.18.corner_ids, s32[16]{0:T(128)S(1)} %and_select_fusion.3.keep_ids, s32[16]{0:T(128)S(1)} %get-tuple-element.13.send_ids, bf16[16,128,1024]{2,1,0:T(8,128)(2,1)} %values_ref.1, ...), custom_call_target="tpu_custom_call" | custom-call | tf_op jit(solution)/shard_map/contract/pallas_call | solution.py:178
  91.7 10.9 %collective-permute-start = (f32[17,128,256]{2,1,0:T(8,128)S(1)}, f32[17,128,256]{2,1,0:T(8,128)S(1)}, u32[]{:S(2)}, u32[]{:S(2)}) collective-permute-start(f32[17,128,256]{2,1,0:T(8,128)S(1)} %get-tuple-element.11), channel_id=1, source_target_pairs={{0,4},{4,0},{1,5},{5,1},{2,6},{6,2},{3,7},{7,3},{8,12},{12,8},{9,1... | collective-permute-start | bytes 6684680 | tf_op jit(solution)/shard_map/ppermute | solution.py:205
  102.5 4.0 %collective-permute-done.recv_ref = f32[17,128,256]{2,1,0:T(8,128)S(1)} collective-permute-done((f32[17,128,256]{2,1,0:T(8,128)S(1)}, f32[17,128,256]{2,1,0:T(8,128)S(1)}, u32[]{:S(2)}, u32[]{:S(2)}) %collective-permute-start) | collective-permute-done | bytes 2228256 | tf_op jit(solution)/shard_map/ppermute | solution.py:205
  106.5 1.6 %apply_inverse.1 = bf16[16,128,256]{2,1,0:T(8,128)(2,1)S(1)} custom-call(f32[17,128,256]{2,1,0:T(8,128)S(1)} %get-tuple-element.10.keep_ref, f32[17,128,256]{2,1,0:T(8,128)S(1)} %collective-permute-done.recv_ref, f32[256,256]{1,0:T(8,128)S(1)} %gram_inverse.1.inv_ref), custom_call_target="tpu_custom_call" | custom-call | tf_op jit(solution)/shard_map/apply_inverse/pallas_call | solution.py:206
  108.1 22.3 %all_to_all.25 = bf16[16,128,256]{2,1,0:T(8,128)(2,1)S(1)} all-to-all(bf16[16,128,256]{2,1,0:T(8,128)(2,1)S(1)} %apply_inverse.1), channel_id=1, replica_groups=mesh['zh'=4,'zl'=4,'y'=4,'core'=2,'corner'=4] {'y','corner'}, dimensions={0} | all-to-all | bytes 2097152 | tf_op jit(solution)/shard_map/all_to_all | solution.py:212
  130.4 0.8 convert_reduce_fusion
  (13 shorter events, 0.1 us)
Async XLA Ops:
  6.5 80.1 %copy-start = (bf16[16,256]{1,0:T(8,128)(2,1)S(1)}, bf16[16,256]{1,0:T(8,128)(2,1)}, u32[]{:S(2)}) copy-start(bf16[16,256]{1,0:T(8,128)(2,1)} %param.10) | copy-start | bytes 24580
  6.5 58.7 %copy-start.1 = (s32[32]{0:T(128)S(1)}, s32[32]{0:T(128)}, u32[]{:S(2)}) copy-start(s32[32]{0:T(128)} %param.9) | copy-start | bytes 388
  6.5 80.0 %all-gather.2.cloned.1.call-start = ((), (), s32[]{:S(2)}) async-start(), calls=%async_computation.5 | async-start | bytes 4456448 | tf_op jit(solution)/shard_map/all_gather | solution.py:139
  9.2 15.0 %all-to-all-start = ((f32[8,8,256]{2,1,0:T(8,128)}), f32[8,8,256]{2,1,0:T(8,128)S(1)}, u32[]{:S(2)}, u32[]{:S(2)}) async-start(f32[8,8,256]{2,1,0:T(8,128)} %dynamic-slice_bitcast_fusion), calls=%async_computation | async-start | bytes 131072 | tf_op jit(solution)/shard_map/all_to_all | solution.py:146
  24.9 22.8 %all-to-all-start.1 = ((f32[4,8,256]{2,1,0:T(8,128)}), f32[4,8,256]{2,1,0:T(8,128)S(1)}, u32[]{:S(2)}, u32[]{:S(2)}) async-start(f32[4,8,256]{2,1,0:T(8,128)} %broadcast_in_dim.40), calls=%async_computation.1 | async-start | bytes 65536 | tf_op jit(solution)/shard_map/all_to_all | solution.py:149
  48.3 7.9 %all-to-all-start.2 = ((f32[4,8,256]{2,1,0:T(8,128)}), f32[4,8,256]{2,1,0:T(8,128)S(1)}, u32[]{:S(2)}, u32[]{:S(2)}) async-start(f32[4,8,256]{2,1,0:T(8,128)} %broadcast_in_dim.41), calls=%async_computation.2 | async-start | bytes 65536 | tf_op jit(solution)/shard_map/all_to_all | solution.py:149
  57.1 19.6 %all-to-all-start.3 = ((f32[32,16,256]{2,1,0:T(8,128)}), f32[32,16,256]{2,1,0:T(8,128)S(1)}, u32[]{:S(2)}, u32[]{:S(2)}) async-start(f32[32,16,256]{2,1,0:T(8,128)} %broadcast_in_dim.42), calls=%async_computation.3 | async-start | bytes 1048576 | tf_op jit(solution)/shard_map/all_to_all | solution.py:154
  91.7 14.8 %collective-permute-start = (f32[17,128,256]{2,1,0:T(8,128)S(1)}, f32[17,128,256]{2,1,0:T(8,128)S(1)}, u32[]{:S(2)}, u32[]{:S(2)}) collective-permute-start(f32[17,128,256]{2,1,0:T(8,128)S(1)} %get-tuple-element.11), channel_id=1, source_target_pairs={{0,4},{4,0},{1,5},{5,1},{2,6},{6,2},{3,7},{7,3},{8,12},{12,8},{9,1... | collective-permute-start | bytes 6684680 | tf_op jit(solution)/shard_map/ppermute | solution.py:205
Sparse Core Ops, SparseCore 0:
  9.4 76.6 all-gather.1

commit v5 on v4

v5 whole, which is shorter than its diff:
```python
import functools

import jax
import jax.numpy as jnp
from jax import lax
from jax.experimental import pallas as pl
from jax.experimental.pallas import tpu as pltpu
from jax.sharding import Mesh, PartitionSpec as P

CBLK = 8
CAP = 2
PIVOTS = 4
GRP = 8
NET = ("zh", "zl")
SEG = ("y", "core")
PLANE = SEG + ("corner",)
ALL = NET + PLANE
FREE = pl.CostEstimate(flops=0, transcendentals=0, bytes_accessed=0)
HIGH = lax.Precision.HIGHEST


def mm(a, b):
    return jnp.dot(a, b, precision=HIGH, preferred_element_type=jnp.float32)


def invert_pivot(p):
    m = len(p)
    if m == 2:
        inv = 1.0 / (p[0][0] * p[1][1] - p[0][1] * p[0][1])
        off = -p[0][1] * inv
        return [[p[1][1] * inv, off], [off, p[0][0] * inv]]
    h = m // 2
    r = range(h)
    ai = invert_pivot([row[:h] for row in p[:h]])
    b = [row[h:] for row in p[:h]]
    w = [[sum(ai[i][l] * b[l][j] for l in r) for j in r] for i in r]
    s = [[p[h + i][h + j] - sum(b[l][min(i, j)] * w[l][max(i, j)] for l in r) for j in r] for i in r]
    q = invert_pivot(s)
    wq = [[sum(w[i][l] * q[l][j] for l in r) for j in r] for i in r]
    top = [[ai[i][j] + sum(wq[i][l] * w[j][l] for l in r) for j in r] for i in r]
    return [top[i] + [-x for x in wq[i]] for i in r] + [[-wq[j][i] for j in r] + q[i] for i in r]


def invert_block(a):
    n = a.shape[0]
    m = PIVOTS
    lane = lax.broadcasted_iota(jnp.int32, (1, n), 1)
    sub = lax.broadcasted_iota(jnp.int32, (n, 1), 0)
    for k in range(0, n, m):
        rows = [a[k + i : k + i + 1, :] for i in range(m)]
        p = [[None] * m for _ in range(m)]
        for i in range(m):
            for j in range(i, m):
                p[i][j] = p[j][i] = jnp.broadcast_to(rows[i][:, k + j : k + j + 1], (1, n))
        q = invert_pivot(p)
        in_lane = (lane >= k) & (lane < k + m)
        in_sub = (sub >= k) & (sub < k + m)
        new = jnp.where(in_lane | in_sub, 0.0, a)
        for i in range(m):
            row = sum(q[i][j] * rows[j] for j in range(m))
            for j in range(m):
                row = jnp.where(lane == k + j, q[i][j], row)
            col = jnp.where(in_sub, jnp.where(sub == k + i, -1.0, 0.0), a[:, k + i : k + i + 1])
            new = new - col * row
        a = new
    return a


def split(x):
    high = x.astype(jnp.bfloat16)
    return high, (x - high.astype(jnp.float32)).astype(jnp.bfloat16)


def product(a, b):
    out = jnp.dot(a[0], b[1], preferred_element_type=jnp.float32)
    out += jnp.dot(a[1], b[0], preferred_element_type=jnp.float32)
    return out + jnp.dot(a[0], b[0], preferred_element_type=jnp.float32)


def prepare_kernel(coords_ref, seg_ref, corner_ref, slot_ref, out_ref, *, held, holders, near):
    xi = lax.axis_index("corner")
    seg_i = lax.axis_index("y") * lax.axis_size("core") + lax.axis_index("core")
    cols = seg_ref.shape[1]
    seg = seg_ref[...]
    gram = lax.dot_general(seg, seg, (((0,), (0,)), ((), ())), preferred_element_type=jnp.float32)
    lane = lax.broadcasted_iota(jnp.int32, (1, cols), 1)
    rows = [jnp.zeros((1, cols), jnp.float32) for _ in range(near)]
    seen = []
    for t in range(coords_ref.shape[0]):
        local = jnp.clip(coords_ref[t, 2] - seg_i * (held * holders), 0, held * holders - 1)
        holder = local // held
        rank = jnp.int32(0)
        for other in seen:
            rank += (other == holder).astype(jnp.int32)
        rank = jnp.minimum(rank, CAP - 1)
        seen.append(holder)
        place = holder * CAP + rank
        shift = lax.rem(xi - holder // near + near, near)
        slot_ref[t] = shift * (near * CAP) + (holder % near) * CAP + rank
        for c in range(near):
            rows[c] = jnp.where(lane == place - c * near * CAP, (local % held).astype(jnp.float32), rows[c])
    corner = corner_ref[...].astype(jnp.float32)
    nseg = out_ref.shape[0] // near
    per = corner.shape[0] // nseg
    own = jnp.zeros((per, cols), jnp.float32)
    for s in range(nseg):
        own = jnp.where(seg_i == s, corner[s * per : (s + 1) * per], own)
    split_rows = 8 // near
    gram = gram.reshape(out_ref.shape[0], 8, cols)
    piece = jnp.zeros((out_ref.shape[0], split_rows, cols), jnp.float32)
    for c in range(near):
        piece = jnp.where(xi == c, gram[:, c * split_rows : (c + 1) * split_rows], piece)
    pad = jnp.zeros((8 - split_rows - 1 - per, cols), jnp.float32)
    for p in range(out_ref.shape[0]):
        out_ref[p] = jnp.concatenate([piece[p], rows[p % near], own, pad], axis=0)


def select_kernel(req_ref, *refs):
    hold = len(refs) // 2
    parts, outs = refs[:hold], refs[hold:]
    zl = lax.axis_index("zl")
    xi = lax.axis_index("corner")
    for offset in range(hold):
        residue = lax.rem(zl + offset, hold)
        for shift in range(hold):
            dest = lax.rem(xi + shift, hold)
            for rank in range(CAP):
                slot = residue * CAP + rank
                outs[shift][slot] = parts[offset][req_ref[dest, slot]]


def scale_kernel(corner_ref, out_ref):
    corner = corner_ref[...]
    n, cols = corner.shape
    wide = jnp.concatenate([corner, jnp.zeros((128 - n, cols), jnp.float32)], axis=0) if n < 128 else corner
    n = wide.shape[0]
    d = 1.0 / jnp.sum(wide * wide, axis=0, keepdims=True)
    scaled = wide * d
    eye = lax.broadcasted_iota(jnp.int32, (n, n), 0) == lax.broadcasted_iota(jnp.int32, (n, n), 1)
    inner = jnp.where(eye, 1.0, 0.0) + lax.dot_general(
        scaled, wide, (((1,), (1,)), ((), ())), precision=HIGH, preferred_element_type=jnp.float32
    )
    small = mm(invert_block(inner), scaled)
    low = lax.dot_general(
        scaled, small, (((0,), (0,)), ((), ())), precision=HIGH, preferred_element_type=jnp.float32
    )
    diag = lax.broadcasted_iota(jnp.int32, (cols, cols), 0) == lax.broadcasted_iota(jnp.int32, (cols, cols), 1)
    out_ref[...] = jnp.where(diag, d, 0.0) - low


def contract_kernel(seg_ids, corner_ids, keep_ids, send_ids, values_ref, *refs):
    seg_refs, (corner_ref, keep_ref, send_ref) = refs[:-3], refs[-3:]
    per = seg_refs[0].shape[0]
    step = pl.program_id(0)

    @pl.when(step == 0)
    def _():
        keep_ref[...] = jnp.zeros_like(keep_ref)
        send_ref[...] = jnp.zeros_like(send_ref)

    for g in range(values_ref.shape[0]):
        t = step * values_ref.shape[0] + g
        at = lax.rem(seg_ids[t], per)
        source = seg_ids[t] // per
        seg_rows = seg_refs[0][at]
        for k in range(1, len(seg_refs)):
            seg_rows = jnp.where(source == k, seg_refs[k][at], seg_rows)
        seg_rows = seg_rows.astype(jnp.float32)
        corner_rows = corner_ref[corner_ids[t]].astype(jnp.float32)
        khatri = jnp.concatenate(
            [(corner_rows[a : a + 1, :] * seg_rows).astype(jnp.bfloat16) for a in range(CBLK)], axis=0
        )
        part = jnp.dot(values_ref[g], khatri, preferred_element_type=jnp.float32)
        keep_ref[keep_ids[t]] += part
        send_ref[send_ids[t]] += part


def scaled_kernel(keep_ref, recv_ref, scale_ref, out_ref):
    scale = split(scale_ref[...])

    def block(i, carry):
        out_ref[i] = product(split(keep_ref[i] + recv_ref[i]), scale).astype(jnp.bfloat16)
        return carry

    lax.fori_loop(0, out_ref.shape[0], block, 0, unroll=4)


def inverse_kernel(seg_gram_ref, corner_ref, out_ref):
    cols = out_ref.shape[1]
    corner = corner_ref[...]
    low = corner.astype(jnp.bfloat16)
    corner_gram = lax.dot_general(low, low, (((0,), (0,)), ((), ())), preferred_element_type=jnp.float32)
    gram = seg_gram_ref[...].reshape(cols, cols) * corner_gram
    h = cols // 2
    a12 = gram[:h, h:]
    a21 = gram[h:, :h]
    p = invert_block(gram[:h, :h])
    w = mm(p, a12)
    v = mm(a21, p)
    q = invert_block(gram[h:, h:] - mm(a21, w))
    wq = mm(w, q)
    top = jnp.concatenate([p + mm(wq, v), -wq], axis=1)
    bottom = jnp.concatenate([-mm(q, v), q], axis=1)
    inverse = jnp.concatenate([top, bottom], axis=0)
    diag = lax.broadcasted_iota(jnp.int32, (cols, cols), 0) == lax.broadcasted_iota(jnp.int32, (cols, cols), 1)
    d = jnp.sum(corner * corner, axis=0, keepdims=True)
    out_ref[...] = mm(corner_gram + jnp.where(diag, d, 0.0), inverse)


def final_kernel(shares_ref, right_ref, out_ref):
    total = shares_ref[0].astype(jnp.float32)
    for i in range(1, shares_ref.shape[0]):
        total += shares_ref[i].astype(jnp.float32)
    out_ref[...] = product(split(total), split(right_ref[...]))


def call(kernel, name, out_shape, in_specs, out_specs, *operands, scratch=()):
    return pl.pallas_call(
        kernel,
        in_specs=in_specs,
        out_specs=out_specs,
        out_shape=out_shape,
        scratch_shapes=scratch,
        compiler_params=pltpu.CompilerParams(vmem_limit_bytes=32 << 20),
        cost_estimate=FREE,
        name=name,
    )(*operands)


def body(tile_values, tile_coords, tile_count, owner_map, corner_factor, seg_factor):
    tiles, net_rows, width = tile_values.shape
    cols = corner_factor.shape[1]
    seg_width = width // CBLK
    nz = lax.axis_size(NET)
    nx = lax.axis_size("corner")
    nseg = lax.axis_size(SEG)
    core = lax.axis_index("core")
    xi = lax.axis_index("corner")
    seg_i = lax.axis_index(SEG)
    per_corner = corner_factor.shape[0] // CBLK
    held = seg_factor.shape[0] // seg_width
    owners = lax.axis_size("y") * nx
    near = nz // nx
    f32 = functools.partial(jax.ShapeDtypeStruct, dtype=jnp.float32)
    smem = pl.BlockSpec(memory_space=pltpu.SMEM)
    vmem = pl.BlockSpec(memory_space=pltpu.VMEM)

    far = [
        (h * nx + x, (h + near * ((x + h) % nx)) % nz * nx + h // near)
        for h in range(nz)
        for x in range(nx)
    ]
    own_rows = lax.ppermute(seg_factor, NET + ("corner",), far)
    slot_of, packet = call(
        functools.partial(prepare_kernel, held=held, holders=nz, near=near),
        "prepare",
        [jax.ShapeDtypeStruct((tiles,), jnp.int32), f32((nseg * nx, 8, cols))],
        [smem, vmem, vmem],
        [smem, vmem],
        tile_coords,
        seg_factor,
        corner_factor,
    )
    packet = lax.all_to_all(packet, PLANE, 0, 0)
    own_rows, packet = lax.optimization_barrier((own_rows, packet))
    up = lax.ppermute(own_rows, NET, [((z + 1) % nz, z) for z in range(nz)])
    two = lax.ppermute(own_rows, NET, [((z + (2 if z % 2 else -2)) % nz, z) for z in range(nz)])
    down = lax.ppermute(own_rows, NET, [((z - 1) % nz, z) for z in range(nz)])
    packet = packet.reshape(nseg, nx, 8, cols)
    cut = 8 // nx
    corner_all = packet[:, :, cut + 1 : cut + 1 + corner_factor.shape[0] // nseg].reshape(-1, cols)
    request = lax.dynamic_index_in_dim(packet[:, :, cut, : near * CAP], seg_i, 0, keepdims=False)
    request = jnp.clip(request.astype(jnp.int32), 0, held - 1)
    chunk = jnp.sum(packet[:, :, :cut], axis=0).reshape(8, cols)
    chunk = jnp.sum(lax.all_to_all(jnp.broadcast_to(chunk[None], (nz // near, 8, cols)), "zh", 0, 0), axis=0)
    up, two, down, chunk, request = lax.optimization_barrier((up, two, down, chunk, request))
    chosen = call(
        select_kernel,
        "select_blocks",
        [jax.ShapeDtypeStruct((near * CAP, seg_width, cols), seg_factor.dtype)] * nx,
        [smem] + [vmem] * near,
        [vmem] * nx,
        request,
        *(v.reshape(held, seg_width, cols) for v in (own_rows, up, two, down)),
    )
    blocks = [chosen[0]] + [
        lax.ppermute(chosen[k], "corner", [(x, (x + k) % nx) for x in range(nx)]) for k in range(1, nx)
    ]
    chunk, corner_all = lax.optimization_barrier((chunk, corner_all))
    scale = call(scale_kernel, "corner_scale", f32((cols, cols)), [vmem], vmem, corner_all)
    chunk = jnp.sum(lax.all_to_all(jnp.broadcast_to(chunk[None], (near, 8, cols)), "zl", 0, 0), axis=0)
    seg_gram = lax.all_to_all(jnp.broadcast_to(chunk[None], (nseg * nx, 8, cols)), PLANE, 0, 0)
    blocks, seg_gram, scale = lax.optimization_barrier((blocks, seg_gram, scale))

    corner_ids = jnp.clip(tile_coords[:, 0] - xi * per_corner, 0, per_corner - 1)
    match = tile_coords[:, 1][:, None] == owner_map[None, :]
    slot = jnp.sum(jnp.where(match, jnp.arange(owner_map.shape[0], dtype=jnp.int32)[None, :], 0), axis=1)
    place = (slot // (2 * nx)) * nx + slot % nx
    live = jnp.arange(tiles, dtype=jnp.int32) < tile_count[0]
    here = (slot // nx) % 2 == core
    keep_ids = jnp.where(live & here, place, owners)
    send_ids = jnp.where(live & jnp.logical_not(here), place, owners)
    keep, send = pl.pallas_call(
        contract_kernel,
        grid_spec=pltpu.PrefetchScalarGridSpec(
            num_scalar_prefetch=4,
            grid=(tiles // GRP,),
            in_specs=[pl.BlockSpec((GRP, net_rows, width), lambda t, *_: (t, 0, 0))]
            + [vmem] * nx
            + [pl.BlockSpec((per_corner, CBLK, cols), lambda t, *_: (0, 0, 0))],
            out_specs=[pl.BlockSpec((owners + 1, net_rows, cols), lambda t, *_: (0, 0, 0))] * 2,
        ),
        out_shape=[f32((owners + 1, net_rows, cols))] * 2,
        compiler_params=pltpu.CompilerParams(vmem_limit_bytes=48 << 20),
        name="contract",
    )(
        slot_of,
        corner_ids,
        keep_ids,
        send_ids,
        tile_values,
        *blocks,
        corner_factor.reshape(per_corner, CBLK, cols),
    )
    received = lax.ppermute(send, "core", [(0, 1), (1, 0)])
    solved = call(
        scaled_kernel,
        "apply_scale",
        jax.ShapeDtypeStruct((owners, net_rows, cols), jnp.bfloat16),
        [vmem] * 3,
        vmem,
        keep,
        received,
        scale,
    )
    solved, seg_gram = lax.optimization_barrier((solved, seg_gram))
    shares = lax.all_to_all(solved, ("y", "corner"), 0, 0)
    right = call(inverse_kernel, "gram_inverse", f32((cols, cols)), [vmem] * 2, vmem, seg_gram, corner_all)
    return call(final_kernel, "final", f32((net_rows, cols)), [vmem] * 2, vmem, shares, right)


def solution(mesh):
    nz, seg, nx = mesh.devices.shape
    axes = Mesh(mesh.devices.reshape(nx, nz // nx, seg // 2, 2, nx), ALL)
    return jax.shard_map(
        body,
        mesh=axes,
        in_specs=(
            P(ALL, None, None),
            P(ALL, None),
            P(ALL),
            P(NET),
            P("corner", None),
            P(SEG + NET, None),
        ),
        out_specs=P(ALL, None),
        check_vma=False,
    )
```

time: 139 us -> 145 us (1.043)
  starting transfers between devices: 43 us -> 68.4 us
  blocking collectives: 22.3 us -> 0 us
  between operations: 14.2 us -> 0.85 us
  Pallas kernels: 16.6 us -> 29.2 us
  waiting for transfers between devices: 35.3 us -> 39.6 us
    all_to_all x1 -> x0, blocking collectives: 22.3 us -> none  [body(): shares = lax.all_to_all(solved, ('y', 'corner'), 0, 0)]
    ppermute x0 -> x7, starting transfers between devices: none -> 20.2 us  [the longest x3 10.1 us: body(): lax.ppermute(chosen[k], 'corner', [(x, (x + k) % nx) for x in range(nx)])]
    all_to_all x4 -> x5, starting transfers between devices: 32.2 us -> 44.9 us  [the longest x1 22.7 us: body(): packet = lax.all_to_all(packet, PLANE, 0, 0)]
    pallas_call x2 -> x6, Pallas kernels: 11.6 us -> 23.4 us  [call(): pl.pallas_call(kernel, in_specs=in_specs, out_specs=out_specs, out_shape=...]
    ppermute x1, starting transfers between devices: 10.9 us -> 3.2 us  [body(): received = lax.ppermute(send, 'core', [(0, 1), (1, 0)])]
    all_to_all x4 -> x5, waiting for transfers between devices: 30.6 us -> 35.4 us  [the longest x1 11.7 us: body(): lax.all_to_all(jnp.broadcast_to(chunk[None], (nz // near, 8, cols)), 'zh'...]
    unnamed x4 -> x9, local copies, waits for them, and re-layouts: 0.01 us -> 2.41 us
  transfers between devices with their start and end apart: 6 -> 13, of which waited for: 5 -> 5; matrix products, arithmetic and copies ran while one was open for 4% -> 2% of each run, Pallas kernels for 7% -> 14%
where the time goes in v5:
time: 145 us; the launch traced here: 143 us
  starting transfers between devices  68.4 us (47%)
  waiting for transfers between devices  39.6 us (27%)
  Pallas kernels  29.2 us (20%)
  local copies, waits for them, and re-layouts  4.44 us (3%)
    pallas_call x6, Pallas kernels, call(): pl.pallas_call(kernel, in_specs=in_specs, out_specs=out_specs, out_shape=...  23.4 us
    all_to_all x1, starting transfers between devices, body(): packet = lax.all_to_all(packet, PLANE, 0, 0)  22.7 us
    all_to_all x1, waiting for transfers between devices, body(): lax.all_to_all(jnp.broadcast_to(chunk[None], (nz // near, 8, cols)), 'zh'...  11.7 us
    all_to_all x1, waiting for transfers between devices, body(): lax.all_to_all(jnp.broadcast_to(chunk[None], (nseg * nx, 8, cols)), PLANE...  10.3 us
    ppermute x3, starting transfers between devices, body(): lax.ppermute(chosen[k], 'corner', [(x, (x + k) % nx) for x in range(nx)])  10.1 us
    all_to_all x1, starting transfers between devices, body(): lax.all_to_all(jnp.broadcast_to(chunk[None], (nseg * nx, 8, cols)), PLANE...  7.75 us
    all_to_all x1, waiting for transfers between devices, body(): packet = lax.all_to_all(packet, PLANE, 0, 0)  7.47 us
    all_to_all x1, starting transfers between devices, body(): lax.all_to_all(jnp.broadcast_to(chunk[None], (nz // near, 8, cols)), 'zh'...  6.26 us
  transfers between devices with their start and end apart: 13, of which 5 were waited for; matrix products, arithmetic and copies ran while one was open for 2% of the time, Pallas kernels for 14%

profile of v5, /device:TPU:1, one launch (start us, length us, event | category | flops | bytes accessed | tf_op | source)
XLA Modules:
  0.0 143.5 jit_solution(15079726872478563171)
XLA Ops:
  0.0 1.7 %collective-permute-start = (bf16[512,256]{1,0:T(8,128)(2,1)}, bf16[512,256]{1,0:T(8,128)(2,1)S(1)}, u32[]{:S(2)}, u32[]{:S(2)}) collective-permute-start(bf16[512,256]{1,0:T(8,128)(2,1)} %seg_ref.1), channel_id=1, source_target_pairs={{0,0},{1,128},{2,256},{3,384},{32,160},{33,288},{34,416},{35,32},{... | collective-permute-start | bytes 786440 | tf_op jit(solution)/shard_map/ppermute | solution.py:253
  4.1 1.8 %prepare.1 = (s32[16]{0:T(128)S(1)}, f32[32,8,256]{2,1,0:T(8,128)}) custom-call(s32[16,3]{1,0:T(8,128)S(1)} %copy.9.coords_ref, bf16[512,256]{1,0:T(8,128)(2,1)S(1)} %copy-done, bf16[16,256]{1,0:T(8,128)(2,1)S(1)} %copy-done.1), custom_call_target="tpu_custom_call" | custom-call | tf_op jit(solution)/shard_map/prepare/pallas_call | solution.py:218
  6.0 22.7 %all-to-all-start = ((f32[32,8,256]{2,1,0:T(8,128)}), f32[32,8,256]{2,1,0:T(8,128)S(1)}, u32[]{:S(2)}, u32[]{:S(2)}) async-start(f32[32,8,256]{2,1,0:T(8,128)} %get-tuple-element.31), calls=%async_computation | async-start | bytes 524288 | tf_op jit(solution)/shard_map/all_to_all | solution.py:264
  30.1 7.5 %all-to-all-done = f32[32,8,256]{2,1,0:T(8,128)S(1)} async-done(((f32[32,8,256]{2,1,0:T(8,128)}), f32[32,8,256]{2,1,0:T(8,128)S(1)}, u32[]{:S(2)}, u32[]{:S(2)}) %all-to-all-start) | async-done | bytes 262176 | tf_op jit(solution)/shard_map/all_to_all | solution.py:264
  37.6 1.9 %collective-permute-start.3 = (bf16[512,256]{1,0:T(8,128)(2,1)S(1)}, bf16[512,256]{1,0:T(8,128)(2,1)S(1)}, u32[]{:S(2)}, u32[]{:S(2)}) collective-permute-start(bf16[512,256]{1,0:T(8,128)(2,1)S(1)} %collective-permute-done), channel_id=1, source_target_pairs={{480,0},{0,32},{32,64},{64,96},{96,128},{128,160},{160,192},{192,2... | collective-permute-start | bytes 786440 | tf_op jit(solution)/shard_map/ppermute | solution.py:268
  39.6 3.5 %collective-permute-start.2 = (bf16[512,256]{1,0:T(8,128)(2,1)S(1)}, bf16[512,256]{1,0:T(8,128)(2,1)S(1)}, u32[]{:S(2)}, u32[]{:S(2)}) collective-permute-start(bf16[512,256]{1,0:T(8,128)(2,1)S(1)} %collective-permute-done), channel_id=1, source_target_pairs={{448,0},{96,32},{0,64},{160,96},{64,128},{224,160},{128,192},{288,... | collective-permute-start | bytes 786440 | tf_op jit(solution)/shard_map/ppermute | solution.py:267
  43.1 3.0 %collective-permute-start.1 = (bf16[512,256]{1,0:T(8,128)(2,1)S(1)}, bf16[512,256]{1,0:T(8,128)(2,1)S(1)}, u32[]{:S(2)}, u32[]{:S(2)}) collective-permute-start(bf16[512,256]{1,0:T(8,128)(2,1)S(1)} %collective-permute-done), channel_id=1, source_target_pairs={{32,0},{64,32},{96,64},{128,96},{160,128},{192,160},{224,192},{256... | collective-permute-start | bytes 786440 | tf_op jit(solution)/shard_map/ppermute | solution.py:266
  46.7 6.3 %all-to-all-start.1 = ((f32[4,8,256]{2,1,0:T(8,128)}), f32[4,8,256]{2,1,0:T(8,128)S(1)}, u32[]{:S(2)}, u32[]{:S(2)}) async-start(f32[4,8,256]{2,1,0:T(8,128)} %broadcast_in_dim.42), calls=%async_computation.1 | async-start | bytes 65536 | tf_op jit(solution)/shard_map/all_to_all | solution.py:275
  53.0 11.7 %all-to-all-done.1 = f32[4,8,256]{2,1,0:T(8,128)S(1)} async-done(((f32[4,8,256]{2,1,0:T(8,128)}), f32[4,8,256]{2,1,0:T(8,128)S(1)}, u32[]{:S(2)}, u32[]{:S(2)}) %all-to-all-start.1) | async-done | bytes 32800 | tf_op jit(solution)/shard_map/all_to_all | solution.py:275
  65.4 3.6 %all-to-all-start.2 = ((f32[4,8,256]{2,1,0:T(8,128)}), f32[4,8,256]{2,1,0:T(8,128)S(1)}, u32[]{:S(2)}, u32[]{:S(2)}) async-start(f32[4,8,256]{2,1,0:T(8,128)} %broadcast_in_dim.43), calls=%async_computation.2 | async-start | bytes 65536 | tf_op jit(solution)/shard_map/all_to_all | solution.py:291
  69.0 1.9 %select_blocks.1 = (bf16[8,128,256]{2,1,0:T(8,128)(2,1)S(1)}, bf16[8,128,256]{2,1,0:T(8,128)(2,1)}, bf16[8,128,256]{2,1,0:T(8,128)(2,1)}, bf16[8,128,256]{2,1,0:T(8,128)(2,1)}) custom-call(s32[4,8]{1,0:T(4,128)S(1)} %clamp_bitcast_fusion.req_ref, bf16[4,128,256]{2,1,0:T(8,128)(2,1)S(1)} %bitcast.17, bf16[4,128,256]{2,1,0:T(8,128)(2,1)S(1)} %bitcast.20, ...), custom_call_target="tpu_custom_call" | custom-call | tf_op jit(solution)/shard_map/select_blocks/pallas_call | solution.py:218
  70.9 2.3 %collective-permute-start.4 = (bf16[8,128,256]{2,1,0:T(8,128)(2,1)}, bf16[8,128,256]{2,1,0:T(8,128)(2,1)S(1)}, u32[]{:S(2)}, u32[]{:S(2)}) collective-permute-start(bf16[8,128,256]{2,1,0:T(8,128)(2,1)} %get-tuple-element.39), channel_id=1, source_target_pairs={{0,1},{1,2},{2,3},{3,0},{4,5},{5,6},{6,7},{7,4},{8,9},{9,10},{10,1... | collective-permute-start | bytes 1572872 | tf_op jit(solution)/shard_map/ppermute | solution.py:287
  73.2 5.9 %collective-permute-start.5 = (bf16[8,128,256]{2,1,0:T(8,128)(2,1)}, bf16[8,128,256]{2,1,0:T(8,128)(2,1)S(1)}, u32[]{:S(2)}, u32[]{:S(2)}) collective-permute-start(bf16[8,128,256]{2,1,0:T(8,128)(2,1)} %get-tuple-element.40), channel_id=1, source_target_pairs={{0,2},{1,3},{2,0},{3,1},{4,6},{5,7},{6,4},{7,5},{8,10},{9,11},{10,... | collective-permute-start | bytes 1572872 | tf_op jit(solution)/shard_map/ppermute | solution.py:287
  79.1 1.9 %collective-permute-start.6 = (bf16[8,128,256]{2,1,0:T(8,128)(2,1)}, bf16[8,128,256]{2,1,0:T(8,128)(2,1)S(1)}, u32[]{:S(2)}, u32[]{:S(2)}) collective-permute-start(bf16[8,128,256]{2,1,0:T(8,128)(2,1)} %get-tuple-element.41), channel_id=1, source_target_pairs={{0,3},{1,0},{2,1},{3,2},{4,7},{5,4},{6,5},{7,6},{8,11},{9,8},{10,9... | collective-permute-start | bytes 1572872 | tf_op jit(solution)/shard_map/ppermute | solution.py:287
  81.9 7.7 %all-to-all-start.3 = ((f32[32,8,256]{2,1,0:T(8,128)}), f32[32,8,256]{2,1,0:T(8,128)S(1)}, u32[]{:S(2)}, u32[]{:S(2)}) async-start(f32[32,8,256]{2,1,0:T(8,128)} %broadcast_in_dim.44), calls=%async_computation.3 | async-start | bytes 524288 | tf_op jit(solution)/shard_map/all_to_all | solution.py:292
  89.7 5.7 %corner_scale.1.scale_ref = f32[256,256]{1,0:T(8,128)S(1)} custom-call(f32[64,256]{1,0:T(8,128)S(1)} %reshape.41.corner_ref), custom_call_target="tpu_custom_call" | custom-call | tf_op jit(solution)/shard_map/corner_scale/pallas_call | solution.py:218
  95.4 10.3 %all-to-all-done.3.seg_gram_ref = f32[32,8,256]{2,1,0:T(8,128)S(1)} async-done(((f32[32,8,256]{2,1,0:T(8,128)}), f32[32,8,256]{2,1,0:T(8,128)S(1)}, u32[]{:S(2)}, u32[]{:S(2)}) %all-to-all-start.3) | async-done | bytes 262176 | tf_op jit(solution)/shard_map/all_to_all | solution.py:292
  105.7 5.8 %contract.1 = (f32[17,128,256]{2,1,0:T(8,128)S(1)}, f32[17,128,256]{2,1,0:T(8,128)}) custom-call(s32[16]{0:T(128)S(1)} %get-tuple-element.30.seg_ids, s32[16]{0:T(128)S(1)} %get-tuple-element.61.corner_ids, s32[16]{0:T(128)S(1)} %and_select_fusion.3.keep_ids, s32[16]{0:T(128)S(1)} %get-tuple-element.55.send_ids, bf16[16,128,1024]{2,1,0:T(8,128)(2,1)} %values_ref.1, ...), custom_call_target="tpu_custom_call" | custom-call | tf_op jit(solution)/shard_map/contract/pallas_call | solution.py:303
  111.5 3.2 %collective-permute-start.7 = (f32[17,128,256]{2,1,0:T(8,128)}, f32[17,128,256]{2,1,0:T(8,128)S(1)}, u32[]{:S(2)}, u32[]{:S(2)}) collective-permute-start(f32[17,128,256]{2,1,0:T(8,128)} %get-tuple-element.50), channel_id=1, source_target_pairs={{0,4},{4,0},{1,5},{5,1},{2,6},{6,2},{3,7},{7,3},{8,12},{12,8},{9,1... | collective-permute-start | bytes 6684680 | tf_op jit(solution)/shard_map/ppermute | solution.py:325
  114.7 4.2 %collective-permute-done.7.recv_ref = f32[17,128,256]{2,1,0:T(8,128)S(1)} collective-permute-done((f32[17,128,256]{2,1,0:T(8,128)}, f32[17,128,256]{2,1,0:T(8,128)S(1)}, u32[]{:S(2)}, u32[]{:S(2)}) %collective-permute-start.7) | collective-permute-done | bytes 2228256 | tf_op jit(solution)/shard_map/ppermute | solution.py:325
  118.8 2.6 %apply_scale.1 = bf16[16,128,256]{2,1,0:T(8,128)(2,1)} custom-call(f32[17,128,256]{2,1,0:T(8,128)S(1)} %get-tuple-element.49.keep_ref, f32[17,128,256]{2,1,0:T(8,128)S(1)} %collective-permute-done.7.recv_ref, f32[256,256]{1,0:T(8,128)S(1)} %corner_scale.1.scale_ref), custom_call_target="tpu_custom_call" | custom-call | tf_op jit(solution)/shard_map/apply_scale/pallas_call | solution.py:218
  121.5 4.7 %all-to-all-start.4 = ((bf16[16,128,256]{2,1,0:T(8,128)(2,1)}), bf16[16,128,256]{2,1,0:T(8,128)(2,1)S(1)}, u32[]{:S(2)}, u32[]{:S(2)}) async-start(bf16[16,128,256]{2,1,0:T(8,128)(2,1)} %apply_scale.1), calls=%async_computation.4 | async-start | bytes 2097152 | tf_op jit(solution)/shard_map/all_to_all | solution.py:337
  126.2 10.4 %gram_inverse.1.right_ref = f32[256,256]{1,0:T(8,128)S(1)} custom-call(f32[32,8,256]{2,1,0:T(8,128)S(1)} %all-to-all-done.3.seg_gram_ref, f32[64,256]{1,0:T(8,128)S(1)} %reshape.41.corner_ref), custom_call_target="tpu_custom_call" | custom-call | tf_op jit(solution)/shard_map/gram_inverse/pallas_call | solution.py:218
  136.6 5.9 %all-to-all-done.4.shares_ref = bf16[16,128,256]{2,1,0:T(8,128)(2,1)S(1)} async-done(((bf16[16,128,256]{2,1,0:T(8,128)(2,1)}), bf16[16,128,256]{2,1,0:T(8,128)(2,1)S(1)}, u32[]{:S(2)}, u32[]{:S(2)}) %all-to-all-start.4) | async-done | bytes 1048608 | tf_op jit(solution)/shard_map/all_to_all | solution.py:337
  (33 shorter events, 6.5 us)
Async XLA Ops:
  0.0 105.7 %copy-start.2 = (bf16[16,256]{1,0:T(8,128)(2,1)S(1)}, bf16[16,256]{1,0:T(8,128)(2,1)}, u32[]{:S(2)}) copy-start(bf16[16,256]{1,0:T(8,128)(2,1)} %corner_ref.1) | copy-start | bytes 24580
  0.0 81.0 %copy-start.3 = (s32[32]{0:T(128)S(1)}, s32[32]{0:T(128)}, u32[]{:S(2)}) copy-start(s32[32]{0:T(128)} %param.9) | copy-start | bytes 388
  0.0 37.5 %collective-permute-start = (bf16[512,256]{1,0:T(8,128)(2,1)}, bf16[512,256]{1,0:T(8,128)(2,1)S(1)}, u32[]{:S(2)}, u32[]{:S(2)}) collective-permute-start(bf16[512,256]{1,0:T(8,128)(2,1)} %seg_ref.1), channel_id=1, source_target_pairs={{0,0},{1,128},{2,256},{3,384},{32,160},{33,288},{34,416},{35,32},{... | collective-permute-start | bytes 786440 | tf_op jit(solution)/shard_map/ppermute | solution.py:253
  2.5 0.9 copy-start
  3.4 0.7 copy-start.1
  6.0 31.6 %all-to-all-start = ((f32[32,8,256]{2,1,0:T(8,128)}), f32[32,8,256]{2,1,0:T(8,128)S(1)}, u32[]{:S(2)}, u32[]{:S(2)}) async-start(f32[32,8,256]{2,1,0:T(8,128)} %get-tuple-element.31), calls=%async_computation | async-start | bytes 524288 | tf_op jit(solution)/shard_map/all_to_all | solution.py:264
  37.6 27.2 %collective-permute-start.3 = (bf16[512,256]{1,0:T(8,128)(2,1)S(1)}, bf16[512,256]{1,0:T(8,128)(2,1)S(1)}, u32[]{:S(2)}, u32[]{:S(2)}) collective-permute-start(bf16[512,256]{1,0:T(8,128)(2,1)S(1)} %collective-permute-done), channel_id=1, source_target_pairs={{480,0},{0,32},{32,64},{64,96},{96,128},{128,160},{160,192},{192,2... | collective-permute-start | bytes 786440 | tf_op jit(solution)/shard_map/ppermute | solution.py:268
  39.6 25.2 %collective-permute-start.2 = (bf16[512,256]{1,0:T(8,128)(2,1)S(1)}, bf16[512,256]{1,0:T(8,128)(2,1)S(1)}, u32[]{:S(2)}, u32[]{:S(2)}) collective-permute-start(bf16[512,256]{1,0:T(8,128)(2,1)S(1)} %collective-permute-done), channel_id=1, source_target_pairs={{448,0},{96,32},{0,64},{160,96},{64,128},{224,160},{128,192},{288,... | collective-permute-start | bytes 786440 | tf_op jit(solution)/shard_map/ppermute | solution.py:267
  43.1 21.7 %collective-permute-start.1 = (bf16[512,256]{1,0:T(8,128)(2,1)S(1)}, bf16[512,256]{1,0:T(8,128)(2,1)S(1)}, u32[]{:S(2)}, u32[]{:S(2)}) collective-permute-start(bf16[512,256]{1,0:T(8,128)(2,1)S(1)} %collective-permute-done), channel_id=1, source_target_pairs={{32,0},{64,32},{96,64},{128,96},{160,128},{192,160},{224,192},{256... | collective-permute-start | bytes 786440 | tf_op jit(solution)/shard_map/ppermute | solution.py:266
  46.7 18.1 %all-to-all-start.1 = ((f32[4,8,256]{2,1,0:T(8,128)}), f32[4,8,256]{2,1,0:T(8,128)S(1)}, u32[]{:S(2)}, u32[]{:S(2)}) async-start(f32[4,8,256]{2,1,0:T(8,128)} %broadcast_in_dim.42), calls=%async_computation.1 | async-start | bytes 65536 | tf_op jit(solution)/shard_map/all_to_all | solution.py:275
  65.4 15.8 %all-to-all-start.2 = ((f32[4,8,256]{2,1,0:T(8,128)}), f32[4,8,256]{2,1,0:T(8,128)S(1)}, u32[]{:S(2)}, u32[]{:S(2)}) async-start(f32[4,8,256]{2,1,0:T(8,128)} %broadcast_in_dim.43), calls=%async_computation.2 | async-start | bytes 65536 | tf_op jit(solution)/shard_map/all_to_all | solution.py:291
  70.9 34.8 %collective-permute-start.4 = (bf16[8,128,256]{2,1,0:T(8,128)(2,1)}, bf16[8,128,256]{2,1,0:T(8,128)(2,1)S(1)}, u32[]{:S(2)}, u32[]{:S(2)}) collective-permute-start(bf16[8,128,256]{2,1,0:T(8,128)(2,1)} %get-tuple-element.39), channel_id=1, source_target_pairs={{0,1},{1,2},{2,3},{3,0},{4,5},{5,6},{6,7},{7,4},{8,9},{9,10},{10,1... | collective-permute-start | bytes 1572872 | tf_op jit(solution)/shard_map/ppermute | solution.py:287
  73.2 32.5 %collective-permute-start.5 = (bf16[8,128,256]{2,1,0:T(8,128)(2,1)}, bf16[8,128,256]{2,1,0:T(8,128)(2,1)S(1)}, u32[]{:S(2)}, u32[]{:S(2)}) collective-permute-start(bf16[8,128,256]{2,1,0:T(8,128)(2,1)} %get-tuple-element.40), channel_id=1, source_target_pairs={{0,2},{1,3},{2,0},{3,1},{4,6},{5,7},{6,4},{7,5},{8,10},{9,11},{10,... | collective-permute-start | bytes 1572872 | tf_op jit(solution)/shard_map/ppermute | solution.py:287
  79.1 26.6 %collective-permute-start.6 = (bf16[8,128,256]{2,1,0:T(8,128)(2,1)}, bf16[8,128,256]{2,1,0:T(8,128)(2,1)S(1)}, u32[]{:S(2)}, u32[]{:S(2)}) collective-permute-start(bf16[8,128,256]{2,1,0:T(8,128)(2,1)} %get-tuple-element.41), channel_id=1, source_target_pairs={{0,3},{1,0},{2,1},{3,2},{4,7},{5,4},{6,5},{7,6},{8,11},{9,8},{10,9... | collective-permute-start | bytes 1572872 | tf_op jit(solution)/shard_map/ppermute | solution.py:287
  81.9 23.7 %all-to-all-start.3 = ((f32[32,8,256]{2,1,0:T(8,128)}), f32[32,8,256]{2,1,0:T(8,128)S(1)}, u32[]{:S(2)}, u32[]{:S(2)}) async-start(f32[32,8,256]{2,1,0:T(8,128)} %broadcast_in_dim.44), calls=%async_computation.3 | async-start | bytes 524288 | tf_op jit(solution)/shard_map/all_to_all | solution.py:292
  111.5 7.4 %collective-permute-start.7 = (f32[17,128,256]{2,1,0:T(8,128)}, f32[17,128,256]{2,1,0:T(8,128)S(1)}, u32[]{:S(2)}, u32[]{:S(2)}) collective-permute-start(f32[17,128,256]{2,1,0:T(8,128)} %get-tuple-element.50), channel_id=1, source_target_pairs={{0,4},{4,0},{1,5},{5,1},{2,6},{6,2},{3,7},{7,3},{8,12},{12,8},{9,1... | collective-permute-start | bytes 6684680 | tf_op jit(solution)/shard_map/ppermute | solution.py:325
  121.5 21.0 %all-to-all-start.4 = ((bf16[16,128,256]{2,1,0:T(8,128)(2,1)}), bf16[16,128,256]{2,1,0:T(8,128)(2,1)S(1)}, u32[]{:S(2)}, u32[]{:S(2)}) async-start(bf16[16,128,256]{2,1,0:T(8,128)(2,1)} %apply_scale.1), calls=%async_computation.4 | async-start | bytes 2097152 | tf_op jit(solution)/shard_map/all_to_all | solution.py:337

commit v6 on v5

--- a/solution.py
+++ b/solution.py
@@ -272,7 +272,7 @@
     request = lax.dynamic_index_in_dim(packet[:, :, cut, : near * CAP], seg_i, 0, keepdims=False)
     request = jnp.clip(request.astype(jnp.int32), 0, held - 1)
     chunk = jnp.sum(packet[:, :, :cut], axis=0).reshape(8, cols)
-    chunk = jnp.sum(lax.all_to_all(jnp.broadcast_to(chunk[None], (nz // near, 8, cols)), "zh", 0, 0), axis=0)
+    chunk = jnp.sum(lax.all_to_all(jnp.broadcast_to(chunk[None], (near, 8, cols)), "zl", 0, 0), axis=0)
     up, two, down, chunk, request = lax.optimization_barrier((up, two, down, chunk, request))
     chosen = call(
         select_kernel,
@@ -283,12 +283,12 @@
         request,
         *(v.reshape(held, seg_width, cols) for v in (own_rows, up, two, down)),
     )
+    _, chunk, corner_all = lax.optimization_barrier((chosen[1], chunk, corner_all))
     blocks = [chosen[0]] + [
         lax.ppermute(chosen[k], "corner", [(x, (x + k) % nx) for x in range(nx)]) for k in range(1, nx)
     ]
-    chunk, corner_all = lax.optimization_barrier((chunk, corner_all))
     scale = call(scale_kernel, "corner_scale", f32((cols, cols)), [vmem], vmem, corner_all)
-    chunk = jnp.sum(lax.all_to_all(jnp.broadcast_to(chunk[None], (near, 8, cols)), "zl", 0, 0), axis=0)
+    chunk = jnp.sum(lax.all_to_all(jnp.broadcast_to(chunk[None], (nz // near, 8, cols)), "zh", 0, 0), axis=0)
     seg_gram = lax.all_to_all(jnp.broadcast_to(chunk[None], (nseg * nx, 8, cols)), PLANE, 0, 0)
     blocks, seg_gram, scale = lax.optimization_barrier((blocks, seg_gram, scale))
 

time: 145 us -> 141 us (0.972)
  waiting for transfers between devices: 39.6 us -> 35.7 us
    all_to_all x1, waiting for transfers between devices: 0.01 us -> 7.71 us  [body(): lax.all_to_all(jnp.broadcast_to(chunk[None], (near, 8, cols)), 'zl', 0, 0)]
    all_to_all x1, waiting for transfers between devices: 11.7 us -> 5.16 us  [body(): lax.all_to_all(jnp.broadcast_to(chunk[None], (nz // near, 8, cols)), 'zh'...]
    all_to_all x1, waiting for transfers between devices: 10.3 us -> 5.28 us  [body(): lax.all_to_all(jnp.broadcast_to(chunk[None], (nseg * nx, 8, cols)), PLANE...]
    ppermute x3, starting transfers between devices: 10.1 us -> 8.58 us  [body(): lax.ppermute(chosen[k], 'corner', [(x, (x + k) % nx) for x in range(nx)])]
    all_to_all x1, starting transfers between devices: 3.57 us -> 5.06 us  [body(): lax.all_to_all(jnp.broadcast_to(chunk[None], (near, 8, cols)), 'zl', 0, 0)]
    unnamed x9 -> x11, local copies, waits for them, and re-layouts: 2.41 us -> 3.23 us
  transfers between devices with their start and end apart: 13 -> 13, of which waited for: 5 -> 6; matrix products, arithmetic and copies ran while one was open for 2% -> 3% of each run, Pallas kernels for 14% -> 13%
where the time goes in v6:
time: 141 us; the launch traced here: 140 us
  starting transfers between devices  68.3 us (48%)
  waiting for transfers between devices  35.7 us (25%)
  Pallas kernels  29 us (21%)
  local copies, waits for them, and re-layouts  5.26 us (4%)
    pallas_call x6, Pallas kernels, call(): pl.pallas_call(kernel, in_specs=in_specs, out_specs=out_specs, out_shape=...  23.2 us
    all_to_all x1, starting transfers between devices, body(): packet = lax.all_to_all(packet, PLANE, 0, 0)  22.7 us
    ppermute x3, starting transfers between devices, body(): lax.ppermute(chosen[k], 'corner', [(x, (x + k) % nx) for x in range(nx)])  8.58 us
    all_to_all x1, starting transfers between devices, body(): lax.all_to_all(jnp.broadcast_to(chunk[None], (nseg * nx, 8, cols)), PLANE...  8.54 us
    all_to_all x1, waiting for transfers between devices, body(): lax.all_to_all(jnp.broadcast_to(chunk[None], (near, 8, cols)), 'zl', 0, 0)  7.71 us
    all_to_all x1, waiting for transfers between devices, body(): packet = lax.all_to_all(packet, PLANE, 0, 0)  7.47 us
    all_to_all x1, waiting for transfers between devices, body(): shares = lax.all_to_all(solved, ('y', 'corner'), 0, 0)  5.89 us
    pallas_call x1, Pallas kernels, body(): pl.pallas_call(contract_kernel, grid_spec=pltpu.PrefetchScalarGridSpec(nu...  5.78 us
  transfers between devices with their start and end apart: 13, of which 6 were waited for; matrix products, arithmetic and copies ran while one was open for 3% of the time, Pallas kernels for 13%

profile of v6, /device:TPU:1, one launch (start us, length us, event | category | flops | bytes accessed | tf_op | source)
XLA Modules:
  0.0 140.1 jit_solution(1564265880674401723)
XLA Ops:
  0.0 1.7 %collective-permute-start = (bf16[512,256]{1,0:T(8,128)(2,1)}, bf16[512,256]{1,0:T(8,128)(2,1)S(1)}, u32[]{:S(2)}, u32[]{:S(2)}) collective-permute-start(bf16[512,256]{1,0:T(8,128)(2,1)} %seg_ref.1), channel_id=1, source_target_pairs={{0,0},{1,128},{2,256},{3,384},{32,160},{33,288},{34,416},{35,32},{... | collective-permute-start | bytes 786440 | tf_op jit(solution)/shard_map/ppermute | solution.py:253
  4.1 1.8 %prepare.1 = (s32[16]{0:T(128)S(1)}, f32[32,8,256]{2,1,0:T(8,128)}) custom-call(s32[16,3]{1,0:T(8,128)S(1)} %copy.9.coords_ref, bf16[512,256]{1,0:T(8,128)(2,1)S(1)} %copy-done, bf16[16,256]{1,0:T(8,128)(2,1)S(1)} %copy-done.1), custom_call_target="tpu_custom_call" | custom-call | tf_op jit(solution)/shard_map/prepare/pallas_call | solution.py:218
  6.0 22.7 %all-to-all-start = ((f32[32,8,256]{2,1,0:T(8,128)}), f32[32,8,256]{2,1,0:T(8,128)S(1)}, u32[]{:S(2)}, u32[]{:S(2)}) async-start(f32[32,8,256]{2,1,0:T(8,128)} %get-tuple-element.31), calls=%async_computation | async-start | bytes 524288 | tf_op jit(solution)/shard_map/all_to_all | solution.py:264
  30.1 7.5 %all-to-all-done = f32[32,8,256]{2,1,0:T(8,128)S(1)} async-done(((f32[32,8,256]{2,1,0:T(8,128)}), f32[32,8,256]{2,1,0:T(8,128)S(1)}, u32[]{:S(2)}, u32[]{:S(2)}) %all-to-all-start) | async-done | bytes 262176 | tf_op jit(solution)/shard_map/all_to_all | solution.py:264
  37.6 1.9 %collective-permute-start.3 = (bf16[512,256]{1,0:T(8,128)(2,1)S(1)}, bf16[512,256]{1,0:T(8,128)(2,1)S(1)}, u32[]{:S(2)}, u32[]{:S(2)}) collective-permute-start(bf16[512,256]{1,0:T(8,128)(2,1)S(1)} %collective-permute-done), channel_id=1, source_target_pairs={{480,0},{0,32},{32,64},{64,96},{96,128},{128,160},{160,192},{192,2... | collective-permute-start | bytes 786440 | tf_op jit(solution)/shard_map/ppermute | solution.py:268
  39.6 3.5 %collective-permute-start.2 = (bf16[512,256]{1,0:T(8,128)(2,1)S(1)}, bf16[512,256]{1,0:T(8,128)(2,1)S(1)}, u32[]{:S(2)}, u32[]{:S(2)}) collective-permute-start(bf16[512,256]{1,0:T(8,128)(2,1)S(1)} %collective-permute-done), channel_id=1, source_target_pairs={{448,0},{96,32},{0,64},{160,96},{64,128},{224,160},{128,192},{288,... | collective-permute-start | bytes 786440 | tf_op jit(solution)/shard_map/ppermute | solution.py:267
  43.1 3.0 %collective-permute-start.1 = (bf16[512,256]{1,0:T(8,128)(2,1)S(1)}, bf16[512,256]{1,0:T(8,128)(2,1)S(1)}, u32[]{:S(2)}, u32[]{:S(2)}) collective-permute-start(bf16[512,256]{1,0:T(8,128)(2,1)S(1)} %collective-permute-done), channel_id=1, source_target_pairs={{32,0},{64,32},{96,64},{128,96},{160,128},{192,160},{224,192},{256... | collective-permute-start | bytes 786440 | tf_op jit(solution)/shard_map/ppermute | solution.py:266
  46.7 5.1 %all-to-all-start.1 = ((f32[4,8,256]{2,1,0:T(8,128)}), f32[4,8,256]{2,1,0:T(8,128)S(1)}, u32[]{:S(2)}, u32[]{:S(2)}) async-start(f32[4,8,256]{2,1,0:T(8,128)} %broadcast_in_dim.42), calls=%async_computation.1 | async-start | bytes 65536 | tf_op jit(solution)/shard_map/all_to_all | solution.py:275
  51.8 7.7 %all-to-all-done.1 = f32[4,8,256]{2,1,0:T(8,128)S(1)} async-done(((f32[4,8,256]{2,1,0:T(8,128)}), f32[4,8,256]{2,1,0:T(8,128)S(1)}, u32[]{:S(2)}, u32[]{:S(2)}) %all-to-all-start.1) | async-done | bytes 32800 | tf_op jit(solution)/shard_map/all_to_all | solution.py:275
  62.1 2.4 %collective-permute-start.4 = (bf16[8,128,256]{2,1,0:T(8,128)(2,1)}, bf16[8,128,256]{2,1,0:T(8,128)(2,1)S(1)}, u32[]{:S(2)}, u32[]{:S(2)}) collective-permute-start(bf16[8,128,256]{2,1,0:T(8,128)(2,1)} %get-tuple-element.39), channel_id=1, source_target_pairs={{0,1},{1,2},{2,3},{3,0},{4,5},{5,6},{6,7},{7,4},{8,9},{9,10},{10,1... | collective-permute-start | bytes 1572872 | tf_op jit(solution)/shard_map/ppermute | solution.py:288
  65.1 5.0 %all-to-all-start.2 = ((f32[4,8,256]{2,1,0:T(8,128)}), f32[4,8,256]{2,1,0:T(8,128)S(1)}, u32[]{:S(2)}, u32[]{:S(2)}) async-start(f32[4,8,256]{2,1,0:T(8,128)} %broadcast_in_dim.43), calls=%async_computation.2 | async-start | bytes 65536 | tf_op jit(solution)/shard_map/all_to_all | solution.py:291
  70.1 3.7 %collective-permute-start.5 = (bf16[8,128,256]{2,1,0:T(8,128)(2,1)}, bf16[8,128,256]{2,1,0:T(8,128)(2,1)S(1)}, u32[]{:S(2)}, u32[]{:S(2)}) collective-permute-start(bf16[8,128,256]{2,1,0:T(8,128)(2,1)} %get-tuple-element.40), channel_id=1, source_target_pairs={{0,2},{1,3},{2,0},{3,1},{4,6},{5,7},{6,4},{7,5},{8,10},{9,11},{10,... | collective-permute-start | bytes 1572872 | tf_op jit(solution)/shard_map/ppermute | solution.py:288
  73.8 2.5 %collective-permute-start.6 = (bf16[8,128,256]{2,1,0:T(8,128)(2,1)}, bf16[8,128,256]{2,1,0:T(8,128)(2,1)S(1)}, u32[]{:S(2)}, u32[]{:S(2)}) collective-permute-start(bf16[8,128,256]{2,1,0:T(8,128)(2,1)} %copy-done.3), channel_id=1, source_target_pairs={{0,3},{1,0},{2,1},{3,2},{4,7},{5,4},{6,5},{7,6},{8,11},{9,8},{10,9... | collective-permute-start | bytes 1572872 | tf_op jit(solution)/shard_map/ppermute | solution.py:288
  76.5 5.2 %all-to-all-done.2 = f32[4,8,256]{2,1,0:T(8,128)S(1)} async-done(((f32[4,8,256]{2,1,0:T(8,128)}), f32[4,8,256]{2,1,0:T(8,128)S(1)}, u32[]{:S(2)}, u32[]{:S(2)}) %all-to-all-start.2) | async-done | bytes 32800 | tf_op jit(solution)/shard_map/all_to_all | solution.py:291
  82.4 8.5 %all-to-all-start.3 = ((f32[32,8,256]{2,1,0:T(8,128)}), f32[32,8,256]{2,1,0:T(8,128)S(1)}, u32[]{:S(2)}, u32[]{:S(2)}) async-start(f32[32,8,256]{2,1,0:T(8,128)} %broadcast_in_dim.44), calls=%async_computation.3 | async-start | bytes 524288 | tf_op jit(solution)/shard_map/all_to_all | solution.py:292
  91.0 5.7 %corner_scale.1.scale_ref = f32[256,256]{1,0:T(8,128)S(1)} custom-call(f32[64,256]{1,0:T(8,128)S(1)} %reshape.41.corner_ref), custom_call_target="tpu_custom_call" | custom-call | tf_op jit(solution)/shard_map/corner_scale/pallas_call | solution.py:218
  96.7 5.3 %all-to-all-done.3.seg_gram_ref = f32[32,8,256]{2,1,0:T(8,128)S(1)} async-done(((f32[32,8,256]{2,1,0:T(8,128)}), f32[32,8,256]{2,1,0:T(8,128)S(1)}, u32[]{:S(2)}, u32[]{:S(2)}) %all-to-all-start.3) | async-done | bytes 262176 | tf_op jit(solution)/shard_map/all_to_all | solution.py:292
  102.0 5.8 %contract.1 = (f32[17,128,256]{2,1,0:T(8,128)S(1)}, f32[17,128,256]{2,1,0:T(8,128)}) custom-call(s32[16]{0:T(128)S(1)} %get-tuple-element.30.seg_ids, s32[16]{0:T(128)S(1)} %get-tuple-element.61.corner_ids, s32[16]{0:T(128)S(1)} %and_select_fusion.3.keep_ids, s32[16]{0:T(128)S(1)} %get-tuple-element.55.send_ids, bf16[16,128,1024]{2,1,0:T(8,128)(2,1)} %values_ref.1, ...), custom_call_target="tpu_custom_call" | custom-call | tf_op jit(solution)/shard_map/contract/pallas_call | solution.py:303
  107.8 3.2 %collective-permute-start.7 = (f32[17,128,256]{2,1,0:T(8,128)}, f32[17,128,256]{2,1,0:T(8,128)S(1)}, u32[]{:S(2)}, u32[]{:S(2)}) collective-permute-start(f32[17,128,256]{2,1,0:T(8,128)} %get-tuple-element.50), channel_id=1, source_target_pairs={{0,4},{4,0},{1,5},{5,1},{2,6},{6,2},{3,7},{7,3},{8,12},{12,8},{9,1... | collective-permute-start | bytes 6684680 | tf_op jit(solution)/shard_map/ppermute | solution.py:325
  111.0 4.2 %collective-permute-done.7.recv_ref = f32[17,128,256]{2,1,0:T(8,128)S(1)} collective-permute-done((f32[17,128,256]{2,1,0:T(8,128)}, f32[17,128,256]{2,1,0:T(8,128)S(1)}, u32[]{:S(2)}, u32[]{:S(2)}) %collective-permute-start.7) | collective-permute-done | bytes 2228256 | tf_op jit(solution)/shard_map/ppermute | solution.py:325
  115.1 2.6 %apply_scale.1 = bf16[16,128,256]{2,1,0:T(8,128)(2,1)} custom-call(f32[17,128,256]{2,1,0:T(8,128)S(1)} %get-tuple-element.49.keep_ref, f32[17,128,256]{2,1,0:T(8,128)S(1)} %collective-permute-done.7.recv_ref, f32[256,256]{1,0:T(8,128)S(1)} %corner_scale.1.scale_ref), custom_call_target="tpu_custom_call" | custom-call | tf_op jit(solution)/shard_map/apply_scale/pallas_call | solution.py:218
  117.7 5.1 %all-to-all-start.4 = ((bf16[16,128,256]{2,1,0:T(8,128)(2,1)}), bf16[16,128,256]{2,1,0:T(8,128)(2,1)S(1)}, u32[]{:S(2)}, u32[]{:S(2)}) async-start(bf16[16,128,256]{2,1,0:T(8,128)(2,1)} %apply_scale.1), calls=%async_computation.4 | async-start | bytes 2097152 | tf_op jit(solution)/shard_map/all_to_all | solution.py:337
  122.8 10.4 %gram_inverse.1.right_ref = f32[256,256]{1,0:T(8,128)S(1)} custom-call(f32[32,8,256]{2,1,0:T(8,128)S(1)} %all-to-all-done.3.seg_gram_ref, f32[64,256]{1,0:T(8,128)S(1)} %reshape.41.corner_ref), custom_call_target="tpu_custom_call" | custom-call | tf_op jit(solution)/shard_map/gram_inverse/pallas_call | solution.py:218
  133.2 5.9 %all-to-all-done.4.shares_ref = bf16[16,128,256]{2,1,0:T(8,128)(2,1)S(1)} async-done(((bf16[16,128,256]{2,1,0:T(8,128)(2,1)}), bf16[16,128,256]{2,1,0:T(8,128)(2,1)S(1)}, u32[]{:S(2)}, u32[]{:S(2)}) %all-to-all-start.4) | async-done | bytes 1048608 | tf_op jit(solution)/shard_map/all_to_all | solution.py:337
  (35 shorter events, 9.0 us)
Async XLA Ops:
  0.0 102.0 %copy-start.2 = (bf16[16,256]{1,0:T(8,128)(2,1)S(1)}, bf16[16,256]{1,0:T(8,128)(2,1)}, u32[]{:S(2)}) copy-start(bf16[16,256]{1,0:T(8,128)(2,1)} %corner_ref.1) | copy-start | bytes 24580
  0.0 76.3 %copy-start.4 = (s32[32]{0:T(128)S(1)}, s32[32]{0:T(128)}, u32[]{:S(2)}) copy-start(s32[32]{0:T(128)} %param.9) | copy-start | bytes 388
  0.0 37.5 %collective-permute-start = (bf16[512,256]{1,0:T(8,128)(2,1)}, bf16[512,256]{1,0:T(8,128)(2,1)S(1)}, u32[]{:S(2)}, u32[]{:S(2)}) collective-permute-start(bf16[512,256]{1,0:T(8,128)(2,1)} %seg_ref.1), channel_id=1, source_target_pairs={{0,0},{1,128},{2,256},{3,384},{32,160},{33,288},{34,416},{35,32},{... | collective-permute-start | bytes 786440 | tf_op jit(solution)/shard_map/ppermute | solution.py:253
  2.5 0.9 copy-start
  3.4 0.7 copy-start.1
  6.0 31.6 %all-to-all-start = ((f32[32,8,256]{2,1,0:T(8,128)}), f32[32,8,256]{2,1,0:T(8,128)S(1)}, u32[]{:S(2)}, u32[]{:S(2)}) async-start(f32[32,8,256]{2,1,0:T(8,128)} %get-tuple-element.31), calls=%async_computation | async-start | bytes 524288 | tf_op jit(solution)/shard_map/all_to_all | solution.py:264
  37.6 21.9 %collective-permute-start.3 = (bf16[512,256]{1,0:T(8,128)(2,1)S(1)}, bf16[512,256]{1,0:T(8,128)(2,1)S(1)}, u32[]{:S(2)}, u32[]{:S(2)}) collective-permute-start(bf16[512,256]{1,0:T(8,128)(2,1)S(1)} %collective-permute-done), channel_id=1, source_target_pairs={{480,0},{0,32},{32,64},{64,96},{96,128},{128,160},{160,192},{192,2... | collective-permute-start | bytes 786440 | tf_op jit(solution)/shard_map/ppermute | solution.py:268
  39.6 20.0 %collective-permute-start.2 = (bf16[512,256]{1,0:T(8,128)(2,1)S(1)}, bf16[512,256]{1,0:T(8,128)(2,1)S(1)}, u32[]{:S(2)}, u32[]{:S(2)}) collective-permute-start(bf16[512,256]{1,0:T(8,128)(2,1)S(1)} %collective-permute-done), channel_id=1, source_target_pairs={{448,0},{96,32},{0,64},{160,96},{64,128},{224,160},{128,192},{288,... | collective-permute-start | bytes 786440 | tf_op jit(solution)/shard_map/ppermute | solution.py:267
  43.1 16.5 %collective-permute-start.1 = (bf16[512,256]{1,0:T(8,128)(2,1)S(1)}, bf16[512,256]{1,0:T(8,128)(2,1)S(1)}, u32[]{:S(2)}, u32[]{:S(2)}) collective-permute-start(bf16[512,256]{1,0:T(8,128)(2,1)S(1)} %collective-permute-done), channel_id=1, source_target_pairs={{32,0},{64,32},{96,64},{128,96},{160,128},{192,160},{224,192},{256... | collective-permute-start | bytes 786440 | tf_op jit(solution)/shard_map/ppermute | solution.py:266
  46.7 12.8 %all-to-all-start.1 = ((f32[4,8,256]{2,1,0:T(8,128)}), f32[4,8,256]{2,1,0:T(8,128)S(1)}, u32[]{:S(2)}, u32[]{:S(2)}) async-start(f32[4,8,256]{2,1,0:T(8,128)} %broadcast_in_dim.42), calls=%async_computation.1 | async-start | bytes 65536 | tf_op jit(solution)/shard_map/all_to_all | solution.py:275
  61.3 0.8 copy-start.3
  62.1 39.9 %collective-permute-start.4 = (bf16[8,128,256]{2,1,0:T(8,128)(2,1)}, bf16[8,128,256]{2,1,0:T(8,128)(2,1)S(1)}, u32[]{:S(2)}, u32[]{:S(2)}) collective-permute-start(bf16[8,128,256]{2,1,0:T(8,128)(2,1)} %get-tuple-element.39), channel_id=1, source_target_pairs={{0,1},{1,2},{2,3},{3,0},{4,5},{5,6},{6,7},{7,4},{8,9},{9,10},{10,1... | collective-permute-start | bytes 1572872 | tf_op jit(solution)/shard_map/ppermute | solution.py:288
  65.1 16.6 %all-to-all-start.2 = ((f32[4,8,256]{2,1,0:T(8,128)}), f32[4,8,256]{2,1,0:T(8,128)S(1)}, u32[]{:S(2)}, u32[]{:S(2)}) async-start(f32[4,8,256]{2,1,0:T(8,128)} %broadcast_in_dim.43), calls=%async_computation.2 | async-start | bytes 65536 | tf_op jit(solution)/shard_map/all_to_all | solution.py:291
  70.1 31.9 %collective-permute-start.5 = (bf16[8,128,256]{2,1,0:T(8,128)(2,1)}, bf16[8,128,256]{2,1,0:T(8,128)(2,1)S(1)}, u32[]{:S(2)}, u32[]{:S(2)}) collective-permute-start(bf16[8,128,256]{2,1,0:T(8,128)(2,1)} %get-tuple-element.40), channel_id=1, source_target_pairs={{0,2},{1,3},{2,0},{3,1},{4,6},{5,7},{6,4},{7,5},{8,10},{9,11},{10,... | collective-permute-start | bytes 1572872 | tf_op jit(solution)/shard_map/ppermute | solution.py:288
  73.8 28.2 %collective-permute-start.6 = (bf16[8,128,256]{2,1,0:T(8,128)(2,1)}, bf16[8,128,256]{2,1,0:T(8,128)(2,1)S(1)}, u32[]{:S(2)}, u32[]{:S(2)}) collective-permute-start(bf16[8,128,256]{2,1,0:T(8,128)(2,1)} %copy-done.3), channel_id=1, source_target_pairs={{0,3},{1,0},{2,1},{3,2},{4,7},{5,4},{6,5},{7,6},{8,11},{9,8},{10,9... | collective-permute-start | bytes 1572872 | tf_op jit(solution)/shard_map/ppermute | solution.py:288
  82.4 19.5 %all-to-all-start.3 = ((f32[32,8,256]{2,1,0:T(8,128)}), f32[32,8,256]{2,1,0:T(8,128)S(1)}, u32[]{:S(2)}, u32[]{:S(2)}) async-start(f32[32,8,256]{2,1,0:T(8,128)} %broadcast_in_dim.44), calls=%async_computation.3 | async-start | bytes 524288 | tf_op jit(solution)/shard_map/all_to_all | solution.py:292
  107.8 7.4 %collective-permute-start.7 = (f32[17,128,256]{2,1,0:T(8,128)}, f32[17,128,256]{2,1,0:T(8,128)S(1)}, u32[]{:S(2)}, u32[]{:S(2)}) collective-permute-start(f32[17,128,256]{2,1,0:T(8,128)} %get-tuple-element.50), channel_id=1, source_target_pairs={{0,4},{4,0},{1,5},{5,1},{2,6},{6,2},{3,7},{7,3},{8,12},{12,8},{9,1... | collective-permute-start | bytes 6684680 | tf_op jit(solution)/shard_map/ppermute | solution.py:325
  117.7 21.4 %all-to-all-start.4 = ((bf16[16,128,256]{2,1,0:T(8,128)(2,1)}), bf16[16,128,256]{2,1,0:T(8,128)(2,1)S(1)}, u32[]{:S(2)}, u32[]{:S(2)}) async-start(bf16[16,128,256]{2,1,0:T(8,128)(2,1)} %apply_scale.1), calls=%async_computation.4 | async-start | bytes 2097152 | tf_op jit(solution)/shard_map/all_to_all | solution.py:337

commit v7 on v6

--- a/solution.py
+++ b/solution.py
@@ -273,7 +273,8 @@
     request = jnp.clip(request.astype(jnp.int32), 0, held - 1)
     chunk = jnp.sum(packet[:, :, :cut], axis=0).reshape(8, cols)
     chunk = jnp.sum(lax.all_to_all(jnp.broadcast_to(chunk[None], (near, 8, cols)), "zl", 0, 0), axis=0)
-    up, two, down, chunk, request = lax.optimization_barrier((up, two, down, chunk, request))
+    scale = call(scale_kernel, "corner_scale", f32((cols, cols)), [vmem], vmem, corner_all)
+    up, two, down, chunk, request, scale = lax.optimization_barrier((up, two, down, chunk, request, scale))
     chosen = call(
         select_kernel,
         "select_blocks",
@@ -283,14 +284,11 @@
         request,
         *(v.reshape(held, seg_width, cols) for v in (own_rows, up, two, down)),
     )
-    _, chunk, corner_all = lax.optimization_barrier((chosen[1], chunk, corner_all))
+    _, chunk = lax.optimization_barrier((chosen[1], chunk))
     blocks = [chosen[0]] + [
         lax.ppermute(chosen[k], "corner", [(x, (x + k) % nx) for x in range(nx)]) for k in range(1, nx)
     ]
-    scale = call(scale_kernel, "corner_scale", f32((cols, cols)), [vmem], vmem, corner_all)
     chunk = jnp.sum(lax.all_to_all(jnp.broadcast_to(chunk[None], (nz // near, 8, cols)), "zh", 0, 0), axis=0)
-    seg_gram = lax.all_to_all(jnp.broadcast_to(chunk[None], (nseg * nx, 8, cols)), PLANE, 0, 0)
-    blocks, seg_gram, scale = lax.optimization_barrier((blocks, seg_gram, scale))
 
     corner_ids = jnp.clip(tile_coords[:, 0] - xi * per_corner, 0, per_corner - 1)
     match = tile_coords[:, 1][:, None] == owner_map[None, :]
@@ -299,6 +297,8 @@
     live = jnp.arange(tiles, dtype=jnp.int32) < tile_count[0]
     here = (slot // nx) % 2 == core
     keep_ids = jnp.where(live & here, place, owners)
+    keep_ids, chunk = lax.optimization_barrier((keep_ids, chunk))
+    seg_gram = lax.all_to_all(jnp.broadcast_to(chunk[None], (nseg * nx, 8, cols)), PLANE, 0, 0)
     send_ids = jnp.where(live & jnp.logical_not(here), place, owners)
     keep, send = pl.pallas_call(
         contract_kernel,
@@ -311,7 +311,7 @@
             out_specs=[pl.BlockSpec((owners + 1, net_rows, cols), lambda t, *_: (0, 0, 0))] * 2,
         ),
         out_shape=[f32((owners + 1, net_rows, cols))] * 2,
-        compiler_params=pltpu.CompilerParams(vmem_limit_bytes=48 << 20),
+        compiler_params=pltpu.CompilerParams(vmem_limit_bytes=50 << 20),
         name="contract",
     )(
         slot_of,
@@ -322,6 +322,7 @@
         *blocks,
         corner_factor.reshape(per_corner, CBLK, cols),
     )
+    send, seg_gram = lax.optimization_barrier((send, seg_gram))
     received = lax.ppermute(send, "core", [(0, 1), (1, 0)])
     solved = call(
         scaled_kernel,
@@ -333,7 +334,6 @@
         received,
         scale,
     )
-    solved, seg_gram = lax.optimization_barrier((solved, seg_gram))
     shares = lax.all_to_all(solved, ("y", "corner"), 0, 0)
     right = call(inverse_kernel, "gram_inverse", f32((cols, cols)), [vmem] * 2, vmem, seg_gram, corner_all)
     return call(final_kernel, "final", f32((net_rows, cols)), [vmem] * 2, vmem, shares, right)

time: 141 us -> 140 us (level)
  waiting for transfers between devices: 35.7 us -> 32.9 us
    all_to_all x1, waiting for transfers between devices: 5.16 us -> 11.6 us  [body(): lax.all_to_all(jnp.broadcast_to(chunk[None], (nz // near, 8, cols)), 'zh'...]
    all_to_all x1, waiting for transfers between devices: 7.71 us -> 2.03 us  [body(): lax.all_to_all(jnp.broadcast_to(chunk[None], (near, 8, cols)), 'zl', 0, 0)]
    all_to_all x1, waiting for transfers between devices: 5.28 us -> 2.33 us  [body(): lax.all_to_all(jnp.broadcast_to(chunk[None], (nseg * nx, 8, cols)), PLANE...]
    unnamed x11 -> x9, local copies, waits for them, and re-layouts: 3.23 us -> 4.03 us
  transfers between devices with their start and end apart: 13 -> 13, of which waited for: 6 -> 6; matrix products, arithmetic and copies ran while one was open for 3% -> 3% of each run, Pallas kernels for 13% -> 18%
where the time goes in v7:
time: 140 us; the launch traced here: 139 us
  starting transfers between devices  67.8 us (48%)
  waiting for transfers between devices  32.9 us (24%)
  Pallas kernels  30 us (21%)
  local copies, waits for them, and re-layouts  6.07 us (4%)
  other arithmetic  1.7 us (1%)
    pallas_call x6, Pallas kernels, call(): pl.pallas_call(kernel, in_specs=in_specs, out_specs=out_specs, out_shape=...  23.4 us
    all_to_all x1, starting transfers between devices, body(): packet = lax.all_to_all(packet, PLANE, 0, 0)  22.7 us
    all_to_all x1, waiting for transfers between devices, body(): lax.all_to_all(jnp.broadcast_to(chunk[None], (nz // near, 8, cols)), 'zh'...  11.6 us
    all_to_all x1, starting transfers between devices, body(): lax.all_to_all(jnp.broadcast_to(chunk[None], (nseg * nx, 8, cols)), PLANE...  9.92 us
    ppermute x3, starting transfers between devices, body(): lax.ppermute(chosen[k], 'corner', [(x, (x + k) % nx) for x in range(nx)])  8.65 us
    all_to_all x1, waiting for transfers between devices, body(): packet = lax.all_to_all(packet, PLANE, 0, 0)  6.64 us
    pallas_call x1, Pallas kernels, body(): pl.pallas_call(contract_kernel, grid_spec=pltpu.PrefetchScalarGridSpec(nu...  6.52 us
    all_to_all x1, waiting for transfers between devices, body(): shares = lax.all_to_all(solved, ('y', 'corner'), 0, 0)  5.91 us
  transfers between devices with their start and end apart: 13, of which 6 were waited for; matrix products, arithmetic and copies ran while one was open for 3% of the time, Pallas kernels for 18%

profile of v7, /device:TPU:1, one launch (start us, length us, event | category | flops | bytes accessed | tf_op | source)
XLA Modules:
  0.0 139.2 jit_solution(17517879904338431790)
XLA Ops:
  4.1 1.8 %prepare.1 = (s32[16]{0:T(128)S(1)}, f32[32,8,256]{2,1,0:T(8,128)}) custom-call(s32[16,3]{1,0:T(8,128)S(1)} %copy.9.coords_ref, bf16[512,256]{1,0:T(8,128)(2,1)S(1)} %copy-done.1, bf16[16,256]{1,0:T(8,128)(2,1)S(1)} %copy-done.2), custom_call_target="tpu_custom_call" | custom-call | tf_op jit(solution)/shard_map/prepare/pallas_call | solution.py:218
  6.0 22.7 %all-to-all-start = ((f32[32,8,256]{2,1,0:T(8,128)}), f32[32,8,256]{2,1,0:T(8,128)S(1)}, u32[]{:S(2)}, u32[]{:S(2)}) async-start(f32[32,8,256]{2,1,0:T(8,128)} %get-tuple-element.27), calls=%async_computation | async-start | bytes 524288 | tf_op jit(solution)/shard_map/all_to_all | solution.py:264
  30.9 6.6 %all-to-all-done = f32[32,8,256]{2,1,0:T(8,128)S(1)} async-done(((f32[32,8,256]{2,1,0:T(8,128)}), f32[32,8,256]{2,1,0:T(8,128)S(1)}, u32[]{:S(2)}, u32[]{:S(2)}) %all-to-all-start) | async-done | bytes 262176 | tf_op jit(solution)/shard_map/all_to_all | solution.py:264
  37.6 1.9 %collective-permute-start.3 = (bf16[512,256]{1,0:T(8,128)(2,1)S(1)}, bf16[512,256]{1,0:T(8,128)(2,1)S(1)}, u32[]{:S(2)}, u32[]{:S(2)}) collective-permute-start(bf16[512,256]{1,0:T(8,128)(2,1)S(1)} %collective-permute-done), channel_id=1, source_target_pairs={{480,0},{0,32},{32,64},{64,96},{96,128},{128,160},{160,192},{192,2... | collective-permute-start | bytes 786440 | tf_op jit(solution)/shard_map/ppermute | solution.py:268
  39.6 3.5 %collective-permute-start.2 = (bf16[512,256]{1,0:T(8,128)(2,1)S(1)}, bf16[512,256]{1,0:T(8,128)(2,1)S(1)}, u32[]{:S(2)}, u32[]{:S(2)}) collective-permute-start(bf16[512,256]{1,0:T(8,128)(2,1)S(1)} %collective-permute-done), channel_id=1, source_target_pairs={{448,0},{96,32},{0,64},{160,96},{64,128},{224,160},{128,192},{288,... | collective-permute-start | bytes 786440 | tf_op jit(solution)/shard_map/ppermute | solution.py:267
  43.1 3.0 %collective-permute-start.1 = (bf16[512,256]{1,0:T(8,128)(2,1)S(1)}, bf16[512,256]{1,0:T(8,128)(2,1)S(1)}, u32[]{:S(2)}, u32[]{:S(2)}) collective-permute-start(bf16[512,256]{1,0:T(8,128)(2,1)S(1)} %collective-permute-done), channel_id=1, source_target_pairs={{32,0},{64,32},{96,64},{128,96},{160,128},{192,160},{224,192},{256... | collective-permute-start | bytes 786440 | tf_op jit(solution)/shard_map/ppermute | solution.py:266
  46.7 5.1 %all-to-all-start.1 = ((f32[4,8,256]{2,1,0:T(8,128)}), f32[4,8,256]{2,1,0:T(8,128)S(1)}, u32[]{:S(2)}, u32[]{:S(2)}) async-start(f32[4,8,256]{2,1,0:T(8,128)} %broadcast_in_dim.42), calls=%async_computation.1 | async-start | bytes 65536 | tf_op jit(solution)/shard_map/all_to_all | solution.py:275
  51.8 5.7 %corner_scale.1.scale_ref = f32[256,256]{1,0:T(8,128)S(1)} custom-call(f32[64,256]{1,0:T(8,128)S(1)} %reshape.37.corner_ref), custom_call_target="tpu_custom_call" | custom-call | tf_op jit(solution)/shard_map/corner_scale/pallas_call | solution.py:218
  57.5 2.0 %all-to-all-done.1 = f32[4,8,256]{2,1,0:T(8,128)S(1)} async-done(((f32[4,8,256]{2,1,0:T(8,128)}), f32[4,8,256]{2,1,0:T(8,128)S(1)}, u32[]{:S(2)}, u32[]{:S(2)}) %all-to-all-start.1) | async-done | bytes 32800 | tf_op jit(solution)/shard_map/all_to_all | solution.py:275
  59.6 1.9 %select_blocks.1 = (bf16[8,128,256]{2,1,0:T(8,128)(2,1)S(1)}, bf16[8,128,256]{2,1,0:T(8,128)(2,1)}, bf16[8,128,256]{2,1,0:T(8,128)(2,1)}, bf16[8,128,256]{2,1,0:T(8,128)(2,1)}) custom-call(s32[4,8]{1,0:T(4,128)S(1)} %clamp_bitcast_fusion.req_ref, bf16[4,128,256]{2,1,0:T(8,128)(2,1)S(1)} %bitcast.17, bf16[4,128,256]{2,1,0:T(8,128)(2,1)S(1)} %bitcast.20, ...), custom_call_target="tpu_custom_call" | custom-call | tf_op jit(solution)/shard_map/select_blocks/pallas_call | solution.py:218
  61.4 1.9 %collective-permute-start.5 = (bf16[8,128,256]{2,1,0:T(8,128)(2,1)}, bf16[8,128,256]{2,1,0:T(8,128)(2,1)S(1)}, u32[]{:S(2)}, u32[]{:S(2)}) collective-permute-start(bf16[8,128,256]{2,1,0:T(8,128)(2,1)} %get-tuple-element.39), channel_id=1, source_target_pairs={{0,2},{1,3},{2,0},{3,1},{4,6},{5,7},{6,4},{7,5},{8,10},{9,11},{10,... | collective-permute-start | bytes 1572872 | tf_op jit(solution)/shard_map/ppermute | solution.py:289
  63.4 4.8 %collective-permute-start.6 = (bf16[8,128,256]{2,1,0:T(8,128)(2,1)}, bf16[8,128,256]{2,1,0:T(8,128)(2,1)S(1)}, u32[]{:S(2)}, u32[]{:S(2)}) collective-permute-start(bf16[8,128,256]{2,1,0:T(8,128)(2,1)} %get-tuple-element.40), channel_id=1, source_target_pairs={{0,3},{1,0},{2,1},{3,2},{4,7},{5,4},{6,5},{7,6},{8,11},{9,8},{10,9... | collective-permute-start | bytes 1572872 | tf_op jit(solution)/shard_map/ppermute | solution.py:289
  68.1 2.0 %collective-permute-start.4 = (bf16[8,128,256]{2,1,0:T(8,128)(2,1)}, bf16[8,128,256]{2,1,0:T(8,128)(2,1)S(1)}, u32[]{:S(2)}, u32[]{:S(2)}) collective-permute-start(bf16[8,128,256]{2,1,0:T(8,128)(2,1)} %get-tuple-element.34), channel_id=1, source_target_pairs={{0,1},{1,2},{2,3},{3,0},{4,5},{5,6},{6,7},{7,4},{8,9},{9,10},{10,1... | collective-permute-start | bytes 1572872 | tf_op jit(solution)/shard_map/ppermute | solution.py:289
  70.8 4.9 %all-to-all-start.2 = ((f32[4,8,256]{2,1,0:T(8,128)}), f32[4,8,256]{2,1,0:T(8,128)S(1)}, u32[]{:S(2)}, u32[]{:S(2)}) async-start(f32[4,8,256]{2,1,0:T(8,128)} %broadcast_in_dim.43), calls=%async_computation.2 | async-start | bytes 65536 | tf_op jit(solution)/shard_map/all_to_all | solution.py:291
  75.7 11.6 %all-to-all-done.2 = f32[4,8,256]{2,1,0:T(8,128)S(1)} async-done(((f32[4,8,256]{2,1,0:T(8,128)}), f32[4,8,256]{2,1,0:T(8,128)S(1)}, u32[]{:S(2)}, u32[]{:S(2)}) %all-to-all-start.2) | async-done | bytes 32800 | tf_op jit(solution)/shard_map/all_to_all | solution.py:291
  88.0 9.9 %all-to-all-start.3 = ((f32[32,8,256]{2,1,0:T(8,128)}), f32[32,8,256]{2,1,0:T(8,128)S(1)}, u32[]{:S(2)}, u32[]{:S(2)}) async-start(f32[32,8,256]{2,1,0:T(8,128)} %broadcast_in_dim.44), calls=%async_computation.3 | async-start | bytes 524288 | tf_op jit(solution)/shard_map/all_to_all | solution.py:301
  98.0 6.5 %contract.1 = (f32[17,128,256]{2,1,0:T(8,128)}, f32[17,128,256]{2,1,0:T(8,128)}) custom-call(s32[16]{0:T(128)S(1)} %get-tuple-element.26.seg_ids, s32[16]{0:T(128)S(1)} %get-tuple-element.53.corner_ids, s32[16]{0:T(128)S(1)} %and_select_fusion.3.keep_ids, s32[16]{0:T(128)S(1)} %get-tuple-element.47.send_ids, bf16[16,128,1024]{2,1,0:T(8,128)(2,1)} %values_ref.1, ...), custom_call_target="tpu_custom_call" | custom-call | tf_op jit(solution)/shard_map/contract/pallas_call | solution.py:303
  104.5 2.3 %all-to-all-done.3.seg_gram_ref = f32[32,8,256]{2,1,0:T(8,128)S(1)} async-done(((f32[32,8,256]{2,1,0:T(8,128)}), f32[32,8,256]{2,1,0:T(8,128)S(1)}, u32[]{:S(2)}, u32[]{:S(2)}) %all-to-all-start.3) | async-done | bytes 262176 | tf_op jit(solution)/shard_map/all_to_all | solution.py:301
  106.8 2.0 %collective-permute-start.7 = (f32[17,128,256]{2,1,0:T(8,128)}, f32[17,128,256]{2,1,0:T(8,128)S(1)}, u32[]{:S(2)}, u32[]{:S(2)}) collective-permute-start(f32[17,128,256]{2,1,0:T(8,128)} %get-tuple-element.44), channel_id=1, source_target_pairs={{0,4},{4,0},{1,5},{5,1},{2,6},{6,2},{3,7},{7,3},{8,12},{12,8},{9,1... | collective-permute-start | bytes 6684680 | tf_op jit(solution)/shard_map/ppermute | solution.py:326
  108.9 4.4 %collective-permute-done.7.recv_ref = f32[17,128,256]{2,1,0:T(8,128)S(1)} collective-permute-done((f32[17,128,256]{2,1,0:T(8,128)}, f32[17,128,256]{2,1,0:T(8,128)S(1)}, u32[]{:S(2)}, u32[]{:S(2)}) %collective-permute-start.7) | collective-permute-done | bytes 2228256 | tf_op jit(solution)/shard_map/ppermute | solution.py:326
  114.9 2.6 %apply_scale.1 = bf16[16,128,256]{2,1,0:T(8,128)(2,1)} custom-call(f32[17,128,256]{2,1,0:T(8,128)S(1)} %copy-done, f32[17,128,256]{2,1,0:T(8,128)S(1)} %collective-permute-done.7.recv_ref, f32[256,256]{1,0:T(8,128)S(1)} %corner_scale.1.scale_ref), custom_call_target="tpu_custom_call" | custom-call | tf_op jit(solution)/shard_map/apply_scale/pallas_call | solution.py:218
  117.6 4.4 %all-to-all-start.4 = ((bf16[16,128,256]{2,1,0:T(8,128)(2,1)}), bf16[16,128,256]{2,1,0:T(8,128)(2,1)S(1)}, u32[]{:S(2)}, u32[]{:S(2)}) async-start(bf16[16,128,256]{2,1,0:T(8,128)(2,1)} %apply_scale.1), calls=%async_computation.4 | async-start | bytes 2097152 | tf_op jit(solution)/shard_map/all_to_all | solution.py:337
  121.9 10.4 %gram_inverse.1.right_ref = f32[256,256]{1,0:T(8,128)S(1)} custom-call(f32[32,8,256]{2,1,0:T(8,128)S(1)} %all-to-all-done.3.seg_gram_ref, f32[64,256]{1,0:T(8,128)S(1)} %reshape.37.corner_ref), custom_call_target="tpu_custom_call" | custom-call | tf_op jit(solution)/shard_map/gram_inverse/pallas_call | solution.py:218
  132.3 5.9 %all-to-all-done.4.shares_ref = bf16[16,128,256]{2,1,0:T(8,128)(2,1)S(1)} async-done(((bf16[16,128,256]{2,1,0:T(8,128)(2,1)}), bf16[16,128,256]{2,1,0:T(8,128)(2,1)S(1)}, u32[]{:S(2)}, u32[]{:S(2)}) %all-to-all-start.4) | async-done | bytes 1048608 | tf_op jit(solution)/shard_map/all_to_all | solution.py:337
  (33 shorter events, 10.5 us)
Async XLA Ops:
  0.0 98.0 %copy-start.3 = (bf16[16,256]{1,0:T(8,128)(2,1)S(1)}, bf16[16,256]{1,0:T(8,128)(2,1)}, u32[]{:S(2)}) copy-start(bf16[16,256]{1,0:T(8,128)(2,1)} %corner_ref.1) | copy-start | bytes 24580
  0.0 37.5 %collective-permute-start = (bf16[512,256]{1,0:T(8,128)(2,1)}, bf16[512,256]{1,0:T(8,128)(2,1)S(1)}, u32[]{:S(2)}, u32[]{:S(2)}) collective-permute-start(bf16[512,256]{1,0:T(8,128)(2,1)} %seg_ref.1), channel_id=1, source_target_pairs={{0,0},{1,128},{2,256},{3,384},{32,160},{33,288},{34,416},{35,32},{... | collective-permute-start | bytes 786440 | tf_op jit(solution)/shard_map/ppermute | solution.py:253
  2.5 0.9 copy-start.1
  3.4 0.7 copy-start.2
  6.0 31.6 %all-to-all-start = ((f32[32,8,256]{2,1,0:T(8,128)}), f32[32,8,256]{2,1,0:T(8,128)S(1)}, u32[]{:S(2)}, u32[]{:S(2)}) async-start(f32[32,8,256]{2,1,0:T(8,128)} %get-tuple-element.27), calls=%async_computation | async-start | bytes 524288 | tf_op jit(solution)/shard_map/all_to_all | solution.py:264
  37.6 21.9 %collective-permute-start.3 = (bf16[512,256]{1,0:T(8,128)(2,1)S(1)}, bf16[512,256]{1,0:T(8,128)(2,1)S(1)}, u32[]{:S(2)}, u32[]{:S(2)}) collective-permute-start(bf16[512,256]{1,0:T(8,128)(2,1)S(1)} %collective-permute-done), channel_id=1, source_target_pairs={{480,0},{0,32},{32,64},{64,96},{96,128},{128,160},{160,192},{192,2... | collective-permute-start | bytes 786440 | tf_op jit(solution)/shard_map/ppermute | solution.py:268
  39.6 20.0 %collective-permute-start.2 = (bf16[512,256]{1,0:T(8,128)(2,1)S(1)}, bf16[512,256]{1,0:T(8,128)(2,1)S(1)}, u32[]{:S(2)}, u32[]{:S(2)}) collective-permute-start(bf16[512,256]{1,0:T(8,128)(2,1)S(1)} %collective-permute-done), channel_id=1, source_target_pairs={{448,0},{96,32},{0,64},{160,96},{64,128},{224,160},{128,192},{288,... | collective-permute-start | bytes 786440 | tf_op jit(solution)/shard_map/ppermute | solution.py:267
  43.1 16.5 %collective-permute-start.1 = (bf16[512,256]{1,0:T(8,128)(2,1)S(1)}, bf16[512,256]{1,0:T(8,128)(2,1)S(1)}, u32[]{:S(2)}, u32[]{:S(2)}) collective-permute-start(bf16[512,256]{1,0:T(8,128)(2,1)S(1)} %collective-permute-done), channel_id=1, source_target_pairs={{32,0},{64,32},{96,64},{128,96},{160,128},{192,160},{224,192},{256... | collective-permute-start | bytes 786440 | tf_op jit(solution)/shard_map/ppermute | solution.py:266
  46.7 12.8 %all-to-all-start.1 = ((f32[4,8,256]{2,1,0:T(8,128)}), f32[4,8,256]{2,1,0:T(8,128)S(1)}, u32[]{:S(2)}, u32[]{:S(2)}) async-start(f32[4,8,256]{2,1,0:T(8,128)} %broadcast_in_dim.42), calls=%async_computation.1 | async-start | bytes 65536 | tf_op jit(solution)/shard_map/all_to_all | solution.py:275
  61.4 36.5 %collective-permute-start.5 = (bf16[8,128,256]{2,1,0:T(8,128)(2,1)}, bf16[8,128,256]{2,1,0:T(8,128)(2,1)S(1)}, u32[]{:S(2)}, u32[]{:S(2)}) collective-permute-start(bf16[8,128,256]{2,1,0:T(8,128)(2,1)} %get-tuple-element.39), channel_id=1, source_target_pairs={{0,2},{1,3},{2,0},{3,1},{4,6},{5,7},{6,4},{7,5},{8,10},{9,11},{10,... | collective-permute-start | bytes 1572872 | tf_op jit(solution)/shard_map/ppermute | solution.py:289
  63.4 34.6 %collective-permute-start.6 = (bf16[8,128,256]{2,1,0:T(8,128)(2,1)}, bf16[8,128,256]{2,1,0:T(8,128)(2,1)S(1)}, u32[]{:S(2)}, u32[]{:S(2)}) collective-permute-start(bf16[8,128,256]{2,1,0:T(8,128)(2,1)} %get-tuple-element.40), channel_id=1, source_target_pairs={{0,3},{1,0},{2,1},{3,2},{4,7},{5,4},{6,5},{7,6},{8,11},{9,8},{10,9... | collective-permute-start | bytes 1572872 | tf_op jit(solution)/shard_map/ppermute | solution.py:289
  68.1 29.8 %collective-permute-start.4 = (bf16[8,128,256]{2,1,0:T(8,128)(2,1)}, bf16[8,128,256]{2,1,0:T(8,128)(2,1)S(1)}, u32[]{:S(2)}, u32[]{:S(2)}) collective-permute-start(bf16[8,128,256]{2,1,0:T(8,128)(2,1)} %get-tuple-element.34), channel_id=1, source_target_pairs={{0,1},{1,2},{2,3},{3,0},{4,5},{5,6},{6,7},{7,4},{8,9},{9,10},{10,1... | collective-permute-start | bytes 1572872 | tf_op jit(solution)/shard_map/ppermute | solution.py:289
  70.8 16.5 %all-to-all-start.2 = ((f32[4,8,256]{2,1,0:T(8,128)}), f32[4,8,256]{2,1,0:T(8,128)S(1)}, u32[]{:S(2)}, u32[]{:S(2)}) async-start(f32[4,8,256]{2,1,0:T(8,128)} %broadcast_in_dim.43), calls=%async_computation.2 | async-start | bytes 65536 | tf_op jit(solution)/shard_map/all_to_all | solution.py:291
  88.0 18.8 %all-to-all-start.3 = ((f32[32,8,256]{2,1,0:T(8,128)}), f32[32,8,256]{2,1,0:T(8,128)S(1)}, u32[]{:S(2)}, u32[]{:S(2)}) async-start(f32[32,8,256]{2,1,0:T(8,128)} %broadcast_in_dim.44), calls=%async_computation.3 | async-start | bytes 524288 | tf_op jit(solution)/shard_map/all_to_all | solution.py:301
  106.8 6.4 %collective-permute-start.7 = (f32[17,128,256]{2,1,0:T(8,128)}, f32[17,128,256]{2,1,0:T(8,128)S(1)}, u32[]{:S(2)}, u32[]{:S(2)}) collective-permute-start(f32[17,128,256]{2,1,0:T(8,128)} %get-tuple-element.44), channel_id=1, source_target_pairs={{0,4},{4,0},{1,5},{5,1},{2,6},{6,2},{3,7},{7,3},{8,12},{12,8},{9,1... | collective-permute-start | bytes 6684680 | tf_op jit(solution)/shard_map/ppermute | solution.py:326
  113.3 1.6 %copy-start = (f32[17,128,256]{2,1,0:T(8,128)S(1)}, f32[17,128,256]{2,1,0:T(8,128)}, u32[]{:S(2)}) copy-start(f32[17,128,256]{2,1,0:T(8,128)} %get-tuple-element.41.keep_ref) | copy-start | bytes 6684676
  117.6 20.7 %all-to-all-start.4 = ((bf16[16,128,256]{2,1,0:T(8,128)(2,1)}), bf16[16,128,256]{2,1,0:T(8,128)(2,1)S(1)}, u32[]{:S(2)}, u32[]{:S(2)}) async-start(bf16[16,128,256]{2,1,0:T(8,128)(2,1)} %apply_scale.1), calls=%async_computation.4 | async-start | bytes 2097152 | tf_op jit(solution)/shard_map/all_to_all | solution.py:337

commit v8 on v4

--- a/solution.py
+++ b/solution.py
@@ -85,6 +85,7 @@
 def contract_kernel(seg_ids, corner_ids, keep_ids, send_ids, values_ref, *refs):
     seg_refs, (corner_ref, keep_ref, send_ref) = refs[:GRP], refs[GRP:]
     step = pl.program_id(0)
+    owners = send_ref.shape[0]
 
     @pl.when(step == 0)
     def _():
@@ -100,7 +101,8 @@
         )
         part = jnp.dot(values_ref[g], khatri, preferred_element_type=jnp.float32)
         keep_ref[keep_ids[t]] += part
-        send_ref[send_ids[t]] += part
+        slot = send_ids[t]
+        send_ref[jnp.minimum(slot, owners - 1)] += jnp.where(slot < owners, part, 0.0)
 
 
 def split(x):
@@ -119,7 +121,7 @@
         out_ref[i] = out.astype(jnp.bfloat16)
         return carry
 
-    lax.fori_loop(0, out_ref.shape[0], block, 0, unroll=4)
+    lax.fori_loop(0, out_ref.shape[0], block, 0, unroll=True)
 
 
 def body(tile_values, tile_coords, tile_count, owner_map, corner_factor, seg_factor):
@@ -187,10 +189,13 @@
             ],
             out_specs=[
                 pl.BlockSpec((owners + 1, net_rows, cols), lambda t, *_: (0, 0, 0)),
-                pl.BlockSpec((owners + 1, net_rows, cols), lambda t, *_: (0, 0, 0)),
+                pl.BlockSpec((owners, net_rows, cols), lambda t, *_: (0, 0, 0)),
             ],
         ),
-        out_shape=[jax.ShapeDtypeStruct((owners + 1, net_rows, cols), jnp.float32)] * 2,
+        out_shape=[
+            jax.ShapeDtypeStruct((owners + 1, net_rows, cols), jnp.float32),
+            jax.ShapeDtypeStruct((owners, net_rows, cols), jnp.float32),
+        ],
         compiler_params=pltpu.CompilerParams(vmem_limit_bytes=48 << 20),
         name="contract",
     )(

time: 139 us -> 138 us (level)
  no operation moved by 1% of the time
where the time goes in v8:
time: 138 us; the launch traced here: 137 us
  starting transfers between devices  42.9 us (31%)
  waiting for transfers between devices  35.1 us (25%)
  blocking collectives  22.8 us (17%)
  Pallas kernels  15.8 us (11%)
  between operations  14.2 us (10%)
  local copies, waits for them, and re-layouts  3.43 us (2%)
  other arithmetic  1.84 us (1%)
    all_to_all x1, blocking collectives, body(): shares = lax.all_to_all(solved, ('y', 'corner'), 0, 0)  22.8 us
    all_to_all x2, waiting for transfers between devices, body(): chunk = jnp.sum(lax.all_to_all(spread, axis, 0, 0), axis=0)  16.1 us
    all_to_all x2, starting transfers between devices, body(): chunk = jnp.sum(lax.all_to_all(spread, axis, 0, 0), axis=0)  13.9 us
    all_to_all x1, waiting for transfers between devices, body(): packet = lax.all_to_all(packet, SEG + ('corner',), 0, 0)  11.2 us
    ppermute x1, starting transfers between devices, body(): received = lax.ppermute(send, 'core', [(0, 1), (1, 0)])  10.7 us
    all_to_all x1, starting transfers between devices, body(): chunk = jnp.sum(lax.all_to_all(mine, SEG, 0, 0), axis=0)  10.1 us
    pallas_call x1, Pallas kernels, body(): pl.pallas_call(inverse_kernel, out_shape=jax.ShapeDtypeStruct((cols, cols...  9.94 us
    all_to_all x1, starting transfers between devices, body(): packet = lax.all_to_all(packet, SEG + ('corner',), 0, 0)  8.16 us
  transfers between devices with their start and end apart: 6, of which 5 were waited for; matrix products, arithmetic and copies ran while one was open for 4% of the time, Pallas kernels for 7%

profile of v8, /device:TPU:1, one launch (start us, length us, event | category | flops | bytes accessed | tf_op | source)
XLA Modules:
  0.0 137.4 jit_solution(12690428014052961530)
XLA Ops:
  6.5 0.7 all-gather.2.cloned.1.call-update
  7.3 1.3 fusion.3
  8.6 0.6 dynamic-slice_bitcast_fusion
  9.2 10.1 %all-to-all-start = ((f32[8,8,256]{2,1,0:T(8,128)}), f32[8,8,256]{2,1,0:T(8,128)S(1)}, u32[]{:S(2)}, u32[]{:S(2)}) async-start(f32[8,8,256]{2,1,0:T(8,128)} %dynamic-slice_bitcast_fusion), calls=%async_computation | async-start | bytes 131072 | tf_op jit(solution)/shard_map/all_to_all | solution.py:148
  19.4 0.8 slice_bitcast_fusion
  20.8 3.4 %all-to-all-done = f32[8,8,256]{2,1,0:T(8,128)S(1)} async-done(((f32[8,8,256]{2,1,0:T(8,128)}), f32[8,8,256]{2,1,0:T(8,128)S(1)}, u32[]{:S(2)}, u32[]{:S(2)}) %all-to-all-start) | async-done | bytes 65568 | tf_op jit(solution)/shard_map/all_to_all | solution.py:148
  24.3 0.6 broadcast_in_dim.40
  24.9 10.6 %all-to-all-start.1 = ((f32[4,8,256]{2,1,0:T(8,128)}), f32[4,8,256]{2,1,0:T(8,128)S(1)}, u32[]{:S(2)}, u32[]{:S(2)}) async-start(f32[4,8,256]{2,1,0:T(8,128)} %broadcast_in_dim.40), calls=%async_computation.1 | async-start | bytes 65536 | tf_op jit(solution)/shard_map/all_to_all | solution.py:151
  35.5 0.7 constant_dynamic-slice_fusion
  36.2 11.5 %all-to-all-done.1 = f32[4,8,256]{2,1,0:T(8,128)S(1)} async-done(((f32[4,8,256]{2,1,0:T(8,128)}), f32[4,8,256]{2,1,0:T(8,128)S(1)}, u32[]{:S(2)}, u32[]{:S(2)}) %all-to-all-start.1) | async-done | bytes 32800 | tf_op jit(solution)/shard_map/all_to_all | solution.py:151
  47.7 0.6 broadcast_in_dim.41
  48.3 3.3 %all-to-all-start.2 = ((f32[4,8,256]{2,1,0:T(8,128)}), f32[4,8,256]{2,1,0:T(8,128)S(1)}, u32[]{:S(2)}, u32[]{:S(2)}) async-start(f32[4,8,256]{2,1,0:T(8,128)} %broadcast_in_dim.41), calls=%async_computation.2 | async-start | bytes 65536 | tf_op jit(solution)/shard_map/all_to_all | solution.py:151
  51.6 4.6 %all-to-all-done.2 = f32[4,8,256]{2,1,0:T(8,128)S(1)} async-done(((f32[4,8,256]{2,1,0:T(8,128)}), f32[4,8,256]{2,1,0:T(8,128)S(1)}, u32[]{:S(2)}, u32[]{:S(2)}) %all-to-all-start.2) | async-done | bytes 32800 | tf_op jit(solution)/shard_map/all_to_all | solution.py:151
  56.2 0.9 broadcast_in_dim.42
  57.1 8.2 %all-to-all-start.3 = ((f32[32,16,256]{2,1,0:T(8,128)}), f32[32,16,256]{2,1,0:T(8,128)S(1)}, u32[]{:S(2)}, u32[]{:S(2)}) async-start(f32[32,16,256]{2,1,0:T(8,128)} %broadcast_in_dim.42), calls=%async_computation.3 | async-start | bytes 1048576 | tf_op jit(solution)/shard_map/all_to_all | solution.py:156
  65.2 0.2 select_reduce_fusion
  65.4 11.2 %all-to-all-done.3.packet_ref = f32[32,16,256]{2,1,0:T(8,128)S(1)} async-done(((f32[32,16,256]{2,1,0:T(8,128)}), f32[32,16,256]{2,1,0:T(8,128)S(1)}, u32[]{:S(2)}, u32[]{:S(2)}) %all-to-all-start.3) | async-done | bytes 524320 | tf_op jit(solution)/shard_map/all_to_all | solution.py:156
  76.6 9.9 %gram_inverse.1.inv_ref = f32[256,256]{1,0:T(8,128)S(1)} custom-call(f32[32,16,256]{2,1,0:T(8,128)S(1)} %all-to-all-done.3.packet_ref), custom_call_target="tpu_custom_call" | custom-call | tf_op jit(solution)/shard_map/gram_inverse/pallas_call | solution.py:157
  86.6 4.7 %contract.1 = (f32[17,128,256]{2,1,0:T(8,128)S(1)}, f32[16,128,256]{2,1,0:T(8,128)S(1)}) custom-call(s32[16]{0:T(128)S(1)} %get-tuple-element.17.seg_ids, s32[16]{0:T(128)S(1)} %get-tuple-element.18.corner_ids, s32[16]{0:T(128)S(1)} %and_select_fusion.3.keep_ids, s32[16]{0:T(128)S(1)} %get-tuple-element.13.send_ids, bf16[16,128,1024]{2,1,0:T(8,128)(2,1)} %values_ref.1, ...), custom_call_target="tpu_custom_call" | custom-call | tf_op jit(solution)/shard_map/contract/pallas_call | solution.py:180
  91.3 10.7 %collective-permute-start = (f32[16,128,256]{2,1,0:T(8,128)S(1)}, f32[16,128,256]{2,1,0:T(8,128)S(1)}, u32[]{:S(2)}, u32[]{:S(2)}) collective-permute-start(f32[16,128,256]{2,1,0:T(8,128)S(1)} %get-tuple-element.11), channel_id=1, source_target_pairs={{0,4},{4,0},{1,5},{5,1},{2,6},{6,2},{3,7},{7,3},{8,12},{12,8},{9,1... | collective-permute-start | bytes 6291464 | tf_op jit(solution)/shard_map/ppermute | solution.py:210
  102.1 3.8 %collective-permute-done.recv_ref = f32[16,128,256]{2,1,0:T(8,128)S(1)} collective-permute-done((f32[16,128,256]{2,1,0:T(8,128)S(1)}, f32[16,128,256]{2,1,0:T(8,128)S(1)}, u32[]{:S(2)}, u32[]{:S(2)}) %collective-permute-start) | collective-permute-done | bytes 2097184 | tf_op jit(solution)/shard_map/ppermute | solution.py:210
  105.9 1.1 apply_inverse.1
  107.0 22.8 %all_to_all.25 = bf16[16,128,256]{2,1,0:T(8,128)(2,1)S(1)} all-to-all(bf16[16,128,256]{2,1,0:T(8,128)(2,1)S(1)} %apply_inverse.1), channel_id=1, replica_groups=mesh['zh'=4,'zl'=4,'y'=4,'core'=2,'corner'=4] {'y','corner'}, dimensions={0} | all-to-all | bytes 2097152 | tf_op jit(solution)/shard_map/all_to_all | solution.py:217
  129.7 0.8 convert_reduce_fusion
  (13 shorter events, 0.1 us)
Async XLA Ops:
  6.5 80.1 %copy-start = (bf16[16,256]{1,0:T(8,128)(2,1)S(1)}, bf16[16,256]{1,0:T(8,128)(2,1)}, u32[]{:S(2)}) copy-start(bf16[16,256]{1,0:T(8,128)(2,1)} %param.10) | copy-start | bytes 24580
  6.5 58.7 %copy-start.1 = (s32[32]{0:T(128)S(1)}, s32[32]{0:T(128)}, u32[]{:S(2)}) copy-start(s32[32]{0:T(128)} %param.9) | copy-start | bytes 388
  6.5 80.0 %all-gather.2.cloned.1.call-start = ((), (), s32[]{:S(2)}) async-start(), calls=%async_computation.5 | async-start | bytes 4456448 | tf_op jit(solution)/shard_map/all_gather | solution.py:141
  9.2 15.0 %all-to-all-start = ((f32[8,8,256]{2,1,0:T(8,128)}), f32[8,8,256]{2,1,0:T(8,128)S(1)}, u32[]{:S(2)}, u32[]{:S(2)}) async-start(f32[8,8,256]{2,1,0:T(8,128)} %dynamic-slice_bitcast_fusion), calls=%async_computation | async-start | bytes 131072 | tf_op jit(solution)/shard_map/all_to_all | solution.py:148
  24.9 22.8 %all-to-all-start.1 = ((f32[4,8,256]{2,1,0:T(8,128)}), f32[4,8,256]{2,1,0:T(8,128)S(1)}, u32[]{:S(2)}, u32[]{:S(2)}) async-start(f32[4,8,256]{2,1,0:T(8,128)} %broadcast_in_dim.40), calls=%async_computation.1 | async-start | bytes 65536 | tf_op jit(solution)/shard_map/all_to_all | solution.py:151
  48.3 7.9 %all-to-all-start.2 = ((f32[4,8,256]{2,1,0:T(8,128)}), f32[4,8,256]{2,1,0:T(8,128)S(1)}, u32[]{:S(2)}, u32[]{:S(2)}) async-start(f32[4,8,256]{2,1,0:T(8,128)} %broadcast_in_dim.41), calls=%async_computation.2 | async-start | bytes 65536 | tf_op jit(solution)/shard_map/all_to_all | solution.py:151
  57.1 19.6 %all-to-all-start.3 = ((f32[32,16,256]{2,1,0:T(8,128)}), f32[32,16,256]{2,1,0:T(8,128)S(1)}, u32[]{:S(2)}, u32[]{:S(2)}) async-start(f32[32,16,256]{2,1,0:T(8,128)} %broadcast_in_dim.42), calls=%async_computation.3 | async-start | bytes 1048576 | tf_op jit(solution)/shard_map/all_to_all | solution.py:156
  91.3 14.5 %collective-permute-start = (f32[16,128,256]{2,1,0:T(8,128)S(1)}, f32[16,128,256]{2,1,0:T(8,128)S(1)}, u32[]{:S(2)}, u32[]{:S(2)}) collective-permute-start(f32[16,128,256]{2,1,0:T(8,128)S(1)} %get-tuple-element.11), channel_id=1, source_target_pairs={{0,4},{4,0},{1,5},{5,1},{2,6},{6,2},{3,7},{7,3},{8,12},{12,8},{9,1... | collective-permute-start | bytes 6291464 | tf_op jit(solution)/shard_map/ppermute | solution.py:210
Sparse Core Ops, SparseCore 0:
  9.4 76.6 all-gather.1

commit v9 on v8

--- a/solution.py
+++ b/solution.py
@@ -94,10 +94,10 @@
 
     for g in range(GRP):
         t = step * GRP + g
-        seg_rows = seg_refs[g][0].astype(jnp.float32)
-        corner_rows = corner_ref[corner_ids[t]].astype(jnp.float32)
+        seg_rows = seg_refs[g][0]
+        corner_rows = corner_ref[corner_ids[t]]
         khatri = jnp.concatenate(
-            [(corner_rows[a : a + 1, :] * seg_rows).astype(jnp.bfloat16) for a in range(CBLK)], axis=0
+            [corner_rows[a : a + 1, :] * seg_rows for a in range(CBLK)], axis=0
         )
         part = jnp.dot(values_ref[g], khatri, preferred_element_type=jnp.float32)
         keep_ref[keep_ids[t]] += part

time: 138 us -> 138 us (level)
  no operation moved by 1% of the time
where the time goes in v9:
time: 138 us; the launch traced here: 137 us
  starting transfers between devices  42.9 us (31%)
  waiting for transfers between devices  35.1 us (25%)
  blocking collectives  21.9 us (16%)
  Pallas kernels  16 us (12%)
  between operations  14.2 us (10%)
  local copies, waits for them, and re-layouts  3.43 us (2%)
  other arithmetic  1.84 us (1%)
    all_to_all x1, blocking collectives, body(): shares = lax.all_to_all(solved, ('y', 'corner'), 0, 0)  21.9 us
    all_to_all x2, waiting for transfers between devices, body(): chunk = jnp.sum(lax.all_to_all(spread, axis, 0, 0), axis=0)  16.1 us
    all_to_all x2, starting transfers between devices, body(): chunk = jnp.sum(lax.all_to_all(spread, axis, 0, 0), axis=0)  13.9 us
    all_to_all x1, waiting for transfers between devices, body(): packet = lax.all_to_all(packet, SEG + ('corner',), 0, 0)  11.2 us
    ppermute x1, starting transfers between devices, body(): received = lax.ppermute(send, 'core', [(0, 1), (1, 0)])  10.8 us
    all_to_all x1, starting transfers between devices, body(): chunk = jnp.sum(lax.all_to_all(mine, SEG, 0, 0), axis=0)  10.1 us
    pallas_call x1, Pallas kernels, body(): pl.pallas_call(inverse_kernel, out_shape=jax.ShapeDtypeStruct((cols, cols...  9.94 us
    all_to_all x1, starting transfers between devices, body(): packet = lax.all_to_all(packet, SEG + ('corner',), 0, 0)  8.16 us
  transfers between devices with their start and end apart: 6, of which 5 were waited for; matrix products, arithmetic and copies ran while one was open for 4% of the time, Pallas kernels for 7%

profile of v9, /device:TPU:1, one launch (start us, length us, event | category | flops | bytes accessed | tf_op | source)
XLA Modules:
  0.0 136.8 jit_solution(3275806846703086180)
XLA Ops:
  6.5 0.7 all-gather.2.cloned.1.call-update
  7.3 1.3 fusion.3
  8.6 0.6 dynamic-slice_bitcast_fusion
  9.2 10.1 %all-to-all-start = ((f32[8,8,256]{2,1,0:T(8,128)}), f32[8,8,256]{2,1,0:T(8,128)S(1)}, u32[]{:S(2)}, u32[]{:S(2)}) async-start(f32[8,8,256]{2,1,0:T(8,128)} %dynamic-slice_bitcast_fusion), calls=%async_computation | async-start | bytes 131072 | tf_op jit(solution)/shard_map/all_to_all | solution.py:148
  19.4 0.8 slice_bitcast_fusion
  20.8 3.4 %all-to-all-done = f32[8,8,256]{2,1,0:T(8,128)S(1)} async-done(((f32[8,8,256]{2,1,0:T(8,128)}), f32[8,8,256]{2,1,0:T(8,128)S(1)}, u32[]{:S(2)}, u32[]{:S(2)}) %all-to-all-start) | async-done | bytes 65568 | tf_op jit(solution)/shard_map/all_to_all | solution.py:148
  24.3 0.6 broadcast_in_dim.40
  24.9 10.6 %all-to-all-start.1 = ((f32[4,8,256]{2,1,0:T(8,128)}), f32[4,8,256]{2,1,0:T(8,128)S(1)}, u32[]{:S(2)}, u32[]{:S(2)}) async-start(f32[4,8,256]{2,1,0:T(8,128)} %broadcast_in_dim.40), calls=%async_computation.1 | async-start | bytes 65536 | tf_op jit(solution)/shard_map/all_to_all | solution.py:151
  35.5 0.7 constant_dynamic-slice_fusion
  36.2 11.5 %all-to-all-done.1 = f32[4,8,256]{2,1,0:T(8,128)S(1)} async-done(((f32[4,8,256]{2,1,0:T(8,128)}), f32[4,8,256]{2,1,0:T(8,128)S(1)}, u32[]{:S(2)}, u32[]{:S(2)}) %all-to-all-start.1) | async-done | bytes 32800 | tf_op jit(solution)/shard_map/all_to_all | solution.py:151
  47.7 0.6 broadcast_in_dim.41
  48.3 3.3 %all-to-all-start.2 = ((f32[4,8,256]{2,1,0:T(8,128)}), f32[4,8,256]{2,1,0:T(8,128)S(1)}, u32[]{:S(2)}, u32[]{:S(2)}) async-start(f32[4,8,256]{2,1,0:T(8,128)} %broadcast_in_dim.41), calls=%async_computation.2 | async-start | bytes 65536 | tf_op jit(solution)/shard_map/all_to_all | solution.py:151
  51.6 4.6 %all-to-all-done.2 = f32[4,8,256]{2,1,0:T(8,128)S(1)} async-done(((f32[4,8,256]{2,1,0:T(8,128)}), f32[4,8,256]{2,1,0:T(8,128)S(1)}, u32[]{:S(2)}, u32[]{:S(2)}) %all-to-all-start.2) | async-done | bytes 32800 | tf_op jit(solution)/shard_map/all_to_all | solution.py:151
  56.2 0.9 broadcast_in_dim.42
  57.1 8.2 %all-to-all-start.3 = ((f32[32,16,256]{2,1,0:T(8,128)}), f32[32,16,256]{2,1,0:T(8,128)S(1)}, u32[]{:S(2)}, u32[]{:S(2)}) async-start(f32[32,16,256]{2,1,0:T(8,128)} %broadcast_in_dim.42), calls=%async_computation.3 | async-start | bytes 1048576 | tf_op jit(solution)/shard_map/all_to_all | solution.py:156
  65.2 0.2 select_reduce_fusion
  65.4 11.2 %all-to-all-done.3.packet_ref = f32[32,16,256]{2,1,0:T(8,128)S(1)} async-done(((f32[32,16,256]{2,1,0:T(8,128)}), f32[32,16,256]{2,1,0:T(8,128)S(1)}, u32[]{:S(2)}, u32[]{:S(2)}) %all-to-all-start.3) | async-done | bytes 524320 | tf_op jit(solution)/shard_map/all_to_all | solution.py:156
  76.6 9.9 %gram_inverse.1.inv_ref = f32[256,256]{1,0:T(8,128)S(1)} custom-call(f32[32,16,256]{2,1,0:T(8,128)S(1)} %all-to-all-done.3.packet_ref), custom_call_target="tpu_custom_call" | custom-call | tf_op jit(solution)/shard_map/gram_inverse/pallas_call | solution.py:157
  86.6 5.0 %contract.1 = (f32[17,128,256]{2,1,0:T(8,128)S(1)}, f32[16,128,256]{2,1,0:T(8,128)S(1)}) custom-call(s32[16]{0:T(128)S(1)} %get-tuple-element.17.seg_ids, s32[16]{0:T(128)S(1)} %get-tuple-element.18.corner_ids, s32[16]{0:T(128)S(1)} %and_select_fusion.3.keep_ids, s32[16]{0:T(128)S(1)} %get-tuple-element.13.send_ids, bf16[16,128,1024]{2,1,0:T(8,128)(2,1)} %values_ref.1, ...), custom_call_target="tpu_custom_call" | custom-call | tf_op jit(solution)/shard_map/contract/pallas_call | solution.py:180
  91.6 10.8 %collective-permute-start = (f32[16,128,256]{2,1,0:T(8,128)S(1)}, f32[16,128,256]{2,1,0:T(8,128)S(1)}, u32[]{:S(2)}, u32[]{:S(2)}) collective-permute-start(f32[16,128,256]{2,1,0:T(8,128)S(1)} %get-tuple-element.11), channel_id=1, source_target_pairs={{0,4},{4,0},{1,5},{5,1},{2,6},{6,2},{3,7},{7,3},{8,12},{12,8},{9,1... | collective-permute-start | bytes 6291464 | tf_op jit(solution)/shard_map/ppermute | solution.py:210
  102.4 3.8 %collective-permute-done.recv_ref = f32[16,128,256]{2,1,0:T(8,128)S(1)} collective-permute-done((f32[16,128,256]{2,1,0:T(8,128)S(1)}, f32[16,128,256]{2,1,0:T(8,128)S(1)}, u32[]{:S(2)}, u32[]{:S(2)}) %collective-permute-start) | collective-permute-done | bytes 2097184 | tf_op jit(solution)/shard_map/ppermute | solution.py:210
  106.1 1.1 apply_inverse.1
  107.2 21.9 %all_to_all.25 = bf16[16,128,256]{2,1,0:T(8,128)(2,1)S(1)} all-to-all(bf16[16,128,256]{2,1,0:T(8,128)(2,1)S(1)} %apply_inverse.1), channel_id=1, replica_groups=mesh['zh'=4,'zl'=4,'y'=4,'core'=2,'corner'=4] {'y','corner'}, dimensions={0} | all-to-all | bytes 2097152 | tf_op jit(solution)/shard_map/all_to_all | solution.py:217
  129.1 0.8 convert_reduce_fusion
  (13 shorter events, 0.1 us)
Async XLA Ops:
  6.5 80.1 %copy-start = (bf16[16,256]{1,0:T(8,128)(2,1)S(1)}, bf16[16,256]{1,0:T(8,128)(2,1)}, u32[]{:S(2)}) copy-start(bf16[16,256]{1,0:T(8,128)(2,1)} %param.10) | copy-start | bytes 24580
  6.5 58.7 %copy-start.1 = (s32[32]{0:T(128)S(1)}, s32[32]{0:T(128)}, u32[]{:S(2)}) copy-start(s32[32]{0:T(128)} %param.9) | copy-start | bytes 388
  6.5 80.0 %all-gather.2.cloned.1.call-start = ((), (), s32[]{:S(2)}) async-start(), calls=%async_computation.5 | async-start | bytes 4456448 | tf_op jit(solution)/shard_map/all_gather | solution.py:141
  9.2 15.0 %all-to-all-start = ((f32[8,8,256]{2,1,0:T(8,128)}), f32[8,8,256]{2,1,0:T(8,128)S(1)}, u32[]{:S(2)}, u32[]{:S(2)}) async-start(f32[8,8,256]{2,1,0:T(8,128)} %dynamic-slice_bitcast_fusion), calls=%async_computation | async-start | bytes 131072 | tf_op jit(solution)/shard_map/all_to_all | solution.py:148
  24.9 22.8 %all-to-all-start.1 = ((f32[4,8,256]{2,1,0:T(8,128)}), f32[4,8,256]{2,1,0:T(8,128)S(1)}, u32[]{:S(2)}, u32[]{:S(2)}) async-start(f32[4,8,256]{2,1,0:T(8,128)} %broadcast_in_dim.40), calls=%async_computation.1 | async-start | bytes 65536 | tf_op jit(solution)/shard_map/all_to_all | solution.py:151
  48.3 7.9 %all-to-all-start.2 = ((f32[4,8,256]{2,1,0:T(8,128)}), f32[4,8,256]{2,1,0:T(8,128)S(1)}, u32[]{:S(2)}, u32[]{:S(2)}) async-start(f32[4,8,256]{2,1,0:T(8,128)} %broadcast_in_dim.41), calls=%async_computation.2 | async-start | bytes 65536 | tf_op jit(solution)/shard_map/all_to_all | solution.py:151
  57.1 19.6 %all-to-all-start.3 = ((f32[32,16,256]{2,1,0:T(8,128)}), f32[32,16,256]{2,1,0:T(8,128)S(1)}, u32[]{:S(2)}, u32[]{:S(2)}) async-start(f32[32,16,256]{2,1,0:T(8,128)} %broadcast_in_dim.42), calls=%async_computation.3 | async-start | bytes 1048576 | tf_op jit(solution)/shard_map/all_to_all | solution.py:156
  91.6 14.5 %collective-permute-start = (f32[16,128,256]{2,1,0:T(8,128)S(1)}, f32[16,128,256]{2,1,0:T(8,128)S(1)}, u32[]{:S(2)}, u32[]{:S(2)}) collective-permute-start(f32[16,128,256]{2,1,0:T(8,128)S(1)} %get-tuple-element.11), channel_id=1, source_target_pairs={{0,4},{4,0},{1,5},{5,1},{2,6},{6,2},{3,7},{7,3},{8,12},{12,8},{9,1... | collective-permute-start | bytes 6291464 | tf_op jit(solution)/shard_map/ppermute | solution.py:210
Sparse Core Ops, SparseCore 0:
  9.4 76.6 all-gather.1
